TPU v7x, 32 devices: a whole 2x2x4 slice. The times are simulated.
32 devices in a mesh: domain: 8 (over y, x, core), band: 4 (over z).
Axes of the slice: x: 2, y: 2, z: 4, core: 2. Of those that a mesh axis runs over, the one named last changes fastest.
Arguments:
- psi: float32 [4, 48, 32, 128], P('band', 'domain'), may hold values from -6 to 6
- potential: float32 [48, 32, 128], P('domain', 'band'), may hold values from -2 to 2
- projectors: float32 [8, 8, 2, 8, 1024], P('domain'), may hold values from -0.1875 to 0.1875
- offsets: int32 [8, 8, 2], P('domain'), may hold values from 0 to 184
- intersection: int32 [8, 8, 2], P('domain'), may hold values from -1 to 31, as said below
- dmat: float32 [256, 8, 8], P('domain'), may hold values from -9 to 9
Outputs:
- filtered: float32 [4, 48, 32, 128], P('band', 'domain')
Inputs may be any that keep to these rules, and one draw needn't show every extreme that they name: intersection[s, d, k] is -1 for an empty slot, else the index among the 32 atoms owned by domain device d of an atom whose projector reaches into domain device s's block; in every draw some owner d receives all 2 slots live from every source s. `offsets`: footprints are whole runs of 8 tiles inside the source block and may intersection one another.
All inputs are finite; a program needn't handle non-finite values.
Results may differ from a plain program's by a relative error of at most 0.00022.
Values sent between devices are 32-bit elements; how exact they have to be, the bound alone decides.
No kernel may reach another device: no remote copies, remote signals or barrier semaphores. Data moves between devices by JAX's collectives and lax.ppermute only.
A program may use at most 64 MiB of HBM per device.

v0:
```python
import jax
import jax.numpy as jnp
from jax import lax
from jax.sharding import PartitionSpec as P

DEGREE = 4


stencil_weights = (
    -5369.0 / 1800.0,
    12.0 / 7.0,
    -15.0 / 56.0,
    10.0 / 189.0,
    -1.0 / 112.0,
    2.0 / 1925.0,
    -1.0 / 16632.0,
)
filter_center = 6.0
filter_half_width = 4.0
highest = lax.Precision.HIGHEST


def extended(value, sides, width):
    for axis, dim in sides:
        size, length = (lax.axis_size(axis), value.shape[dim])
        up = [(i, (i + 1) % size) for i in range(size - 1)]
        down = [(j, i) for i, j in up]
        last = lax.slice_in_dim(value, length - width, length, axis=dim)
        initial = lax.slice_in_dim(value, 0, width, axis=dim)
        before = lax.ppermute(last, axis, up)
        after = lax.ppermute(initial, axis, down)
        value = jnp.concatenate([before, value, after], axis=dim)
    return value


def kinetic(grid_field, padded, reach_cells):
    planes = grid_field.shape[0]
    summed = 3.0 * stencil_weights[0] * grid_field
    for distance in range(1, reach_cells + 1):
        beside_all = (
            padded[reach_cells + distance : reach_cells + distance + planes]
            + padded[reach_cells - distance : reach_cells - distance + planes]
        )
        beside_all = (
            beside_all + jnp.roll(grid_field, distance, 1) + jnp.roll(grid_field, -distance, 1)
        )
        beside_all = (
            beside_all + jnp.roll(grid_field, distance, 2) + jnp.roll(grid_field, -distance, 2)
        )
        summed = summed + stencil_weights[distance] * beside_all
    return -0.5 * summed


def shards(psi, potential, projectors, offsets, intersection, dmat):
    reach_cells = len(stencil_weights) - 1
    pot_full = lax.all_gather(potential, "band", axis=1, tiled=True)
    projector_block = projectors[0]
    domains = projector_block.shape[0]
    cap_slots = projector_block.shape[1]
    proj_count = projector_block.shape[2]
    foot_tiles = projector_block.shape[3] // 128
    tile_index = (offsets[0][..., None] + jnp.arange(foot_tiles, dtype=jnp.int32)).reshape(-1)
    slot_atoms = intersection[0]
    live_slots = (slot_atoms >= 0).astype(jnp.float32)
    atom_count = dmat.shape[0]
    incoming = lax.all_to_all(slot_atoms, "domain", split_axis=0, concat_axis=0, tiled=True)
    in_hot = (incoming.reshape(-1)[:, None] == jnp.arange(atom_count, dtype=jnp.int32)).astype(
        jnp.float32
    )

    def owner_side(partial_value):
        received = lax.all_to_all(partial_value, "domain", split_axis=0, concat_axis=0, tiled=True)
        coefficient = jnp.dot(in_hot.T, received.reshape(-1, proj_count), precision=highest)
        applied = jnp.einsum("aij,aj->ai", dmat, coefficient, precision=highest)
        returned = jnp.dot(in_hot, applied, precision=highest).reshape(
            domains, cap_slots, proj_count
        )
        return lax.all_to_all(returned, "domain", split_axis=0, concat_axis=0, tiled=True)

    def hamiltonian(grid_field):
        padded = extended(grid_field, (("domain", 0),), reach_cells)
        tiles = grid_field.reshape(-1, 128)
        footprint = tiles[tile_index].reshape(domains, cap_slots, -1)
        partial_value = (
            jnp.einsum("dkil,dkl->dki", projector_block, footprint, precision=highest)
            * live_slots[..., None]
        )
        returned = owner_side(partial_value)
        contrib = jnp.einsum("dkil,dki->dkl", projector_block, returned, precision=highest).reshape(
            -1, 128
        )
        nonlocal_term = jnp.zeros_like(tiles).at[tile_index].add(contrib).reshape(grid_field.shape)
        return kinetic(grid_field, padded, reach_cells) + pot_full * grid_field + nonlocal_term

    state = psi[0]
    previous = state
    current = (hamiltonian(state) - filter_center * state) / filter_half_width
    for degree in range(1, DEGREE):
        following = (
            2.0 * (hamiltonian(current) - filter_center * current) / filter_half_width - previous
        )
        previous, current = (current, following)
    return current[None]


def solution(mesh):
    return jax.shard_map(
        shards,
        mesh=mesh,
        in_specs=(
            P("band", "domain", None, None),
            P("domain", "band", None),
            P("domain", None, None, None, None),
            P("domain", None, None),
            P("domain", None, None),
            P("domain", None, None),
        ),
        out_specs=P("band", "domain", None, None),
        check_vma=False,
    )
```

profile of v0, /device:TPU:0, one launch (start us, length us, event | category | flops | bytes accessed | tf_op | source)
XLA Modules:
  0.0 173.2 jit_solution(14876016404611144924)
XLA Ops:
  0.0 3.1 %collective-permute-start.1 = (f32[6,32,128]{2,1,0:T(8,128)}, f32[6,32,128]{2,1,0:T(8,128)}, u32[]{:S(2)}, u32[]{:S(2)}) collective-permute-start(f32[6,32,128]{2,1,0:T(8,128)} %bitcast.104), channel_id=1, source_target_pairs={{0,4},{4,8},{8,12},{12,16},{16,20},{20,24},{24,28},{1,5},{5,9},{9,... | collective-permute-start | bytes 294920 | tf_op jit(solution)/shard_map/ppermute | solution.py:30
  5.8 6.5 %all-to-all-start = ((s32[8,1,2]{2,1,0:T(1,128)}), s32[8,1,2]{2,1,0:T(1,128)S(1)}, u32[]{:S(2)}, u32[]{:S(2)}) async-start(s32[8,1,2]{2,1,0:T(1,128)} %copy.22), calls=%async_computation | async-start | bytes 8192 | tf_op jit(solution)/shard_map/all_to_all | solution.py:66
  26.8 4.2 %all-to-all-start.1 = ((f32[8,2,8]{2,1,0:T(2,128)}), f32[8,2,8]{2,1,0:T(2,128)S(1)}, u32[]{:S(2)}, u32[]{:S(2)}) async-start(f32[8,2,8]{2,1,0:T(2,128)} %broadcast_multiply_fusion.4), calls=%async_computation.1 | async-start | bytes 16384 | tf_op jit(solution)/shard_map/all_to_all | solution.py:72
  32.8 2.9 %all-to-all-done.1 = f32[8,2,8]{2,1,0:T(2,128)S(1)} async-done(((f32[8,2,8]{2,1,0:T(2,128)}), f32[8,2,8]{2,1,0:T(2,128)S(1)}, u32[]{:S(2)}, u32[]{:S(2)}) %all-to-all-start.1) | async-done | bytes 544 | tf_op jit(solution)/shard_map/all_to_all | solution.py:72
  37.3 3.3 %all-to-all-start.2 = ((f32[8,2,8]{2,1,0:T(2,128)}), f32[8,2,8]{2,1,0:T(2,128)S(1)}, u32[]{:S(2)}, u32[]{:S(2)}) async-start(f32[8,2,8]{2,1,0:T(2,128)} %bitcast.15), calls=%async_computation.2 | async-start | bytes 16384 | tf_op jit(solution)/shard_map/all_to_all | solution.py:78
  40.6 13.5 %all_gather.3 = f32[6,32,128]{2,1,0:T(8,128)S(1)} all-gather(f32[6,8,128]{2,1,0:T(8,128)S(1)} %copy-done.18), channel_id=1, replica_groups=mesh['domain'=8,'band'=4] {'band'}, dimensions={1}, use_global_device_ids=true | all-gather | bytes 122880 | tf_op jit(solution)/shard_map/all_gather | solution.py:56
  56.7 2.1 %broadcast_multiply_fusion = (f32[6,32,128]{2,1,0:T(8,128)S(1)}, f32[6,32,128]{2,1,0:T(8,128)S(1)}) fusion(f32[6,32,128]{2,1,0:T(8,128)S(1)} %bitcast.131, f32[6,32,128]{2,1,0:T(8,128)S(1)} %bitcast.135, f32[6,32,128]{2,1,0:T(8,128)S(1)} %all_gather.3, f32[6,32,6]{2,1,0:T(8,128)} %get-tuple-element.196, f32[6,32,122]{2,1,0:T(8,128)} %get-tuple-element.198, ...), kind=kLoop, calls=%fused_computation.315 | loop fusion | flops 2064384 | bytes 3047424 | tf_op jit(solution)/shard_map/div | solution.py:97
  72.1 6.5 %all-to-all-start.3 = ((f32[8,2,8]{2,1,0:T(2,128)}), f32[8,2,8]{2,1,0:T(2,128)S(1)}, u32[]{:S(2)}, u32[]{:S(2)}) async-start(f32[8,2,8]{2,1,0:T(2,128)} %broadcast_multiply_fusion.3), calls=%async_computation.3 | async-start | bytes 16384 | tf_op jit(solution)/shard_map/all_to_all | solution.py:72
  79.2 4.1 %all-to-all-done.3 = f32[8,2,8]{2,1,0:T(2,128)S(1)} async-done(((f32[8,2,8]{2,1,0:T(2,128)}), f32[8,2,8]{2,1,0:T(2,128)S(1)}, u32[]{:S(2)}, u32[]{:S(2)}) %all-to-all-start.3) | async-done | bytes 544 | tf_op jit(solution)/shard_map/all_to_all | solution.py:72
  84.4 3.3 %all-to-all-start.4 = ((f32[8,2,8]{2,1,0:T(2,128)}), f32[8,2,8]{2,1,0:T(2,128)S(1)}, u32[]{:S(2)}, u32[]{:S(2)}) async-start(f32[8,2,8]{2,1,0:T(2,128)} %bitcast.25), calls=%async_computation.4 | async-start | bytes 16384 | tf_op jit(solution)/shard_map/all_to_all | solution.py:78
  88.3 4.0 %all-to-all-done.4 = f32[8,2,8]{2,1,0:T(2,128)S(1)} async-done(((f32[8,2,8]{2,1,0:T(2,128)}), f32[8,2,8]{2,1,0:T(2,128)S(1)}, u32[]{:S(2)}, u32[]{:S(2)}) %all-to-all-start.4) | async-done | bytes 544 | tf_op jit(solution)/shard_map/all_to_all | solution.py:78
  95.0 2.1 %multiply_subtract_fusion.1 = f32[6,32,128]{2,1,0:T(8,128)S(1)} fusion(f32[6,32,128]{2,1,0:T(8,128)S(1)} %get-tuple-element.6, f32[6,32,128]{2,1,0:T(8,128)S(1)} %bitcast.136, f32[6,32,128]{2,1,0:T(8,128)S(1)} %all_gather.3, f32[6,32,128]{2,1,0:T(8,128)S(1)} %get-tuple-element.5, f32[6,32,6]{2,1,0:T(8,128)S(1)} %get-tuple-element.148, ...), kind=kLoop, calls=%fused_computation.310 | loop fusion | flops 2088960 | bytes 3145728 | tf_op jit(solution)/shard_map/sub | solution.py:100
  99.5 2.3 %collective-permute-start.5 = (f32[6,32,128]{2,1,0:T(8,128)S(1)}, f32[6,32,128]{2,1,0:T(8,128)}, u32[]{:S(2)}, u32[]{:S(2)}) collective-permute-start(f32[6,32,128]{2,1,0:T(8,128)S(1)} %multiply_subtract_fusion.1), channel_id=1, source_target_pairs={{0,4},{4,8},{8,12},{12,16},{16,20},{20,24},{24,28},{1,5},{5,9},{9,... | collective-permute-start | bytes 294920 | tf_op jit(solution)/shard_map/ppermute | solution.py:30
  110.8 4.7 %all-to-all-start.5 = ((f32[8,2,8]{2,1,0:T(2,128)}), f32[8,2,8]{2,1,0:T(2,128)S(1)}, u32[]{:S(2)}, u32[]{:S(2)}) async-start(f32[8,2,8]{2,1,0:T(2,128)} %broadcast_multiply_fusion.2), calls=%async_computation.5 | async-start | bytes 16384 | tf_op jit(solution)/shard_map/all_to_all | solution.py:72
  116.1 4.1 %all-to-all-done.5 = f32[8,2,8]{2,1,0:T(2,128)S(1)} async-done(((f32[8,2,8]{2,1,0:T(2,128)}), f32[8,2,8]{2,1,0:T(2,128)S(1)}, u32[]{:S(2)}, u32[]{:S(2)}) %all-to-all-start.5) | async-done | bytes 544 | tf_op jit(solution)/shard_map/all_to_all | solution.py:72
  121.2 3.3 %all-to-all-start.6 = ((f32[8,2,8]{2,1,0:T(2,128)}), f32[8,2,8]{2,1,0:T(2,128)S(1)}, u32[]{:S(2)}, u32[]{:S(2)}) async-start(f32[8,2,8]{2,1,0:T(2,128)} %bitcast.35), calls=%async_computation.6 | async-start | bytes 16384 | tf_op jit(solution)/shard_map/all_to_all | solution.py:78
  125.2 4.0 %all-to-all-done.6 = f32[8,2,8]{2,1,0:T(2,128)S(1)} async-done(((f32[8,2,8]{2,1,0:T(2,128)}), f32[8,2,8]{2,1,0:T(2,128)S(1)}, u32[]{:S(2)}, u32[]{:S(2)}) %all-to-all-start.6) | async-done | bytes 544 | tf_op jit(solution)/shard_map/all_to_all | solution.py:78
  132.0 2.1 %multiply_subtract_fusion = f32[6,32,128]{2,1,0:T(8,128)S(1)} fusion(f32[6,32,128]{2,1,0:T(8,128)S(1)} %multiply_subtract_fusion.1, f32[6,32,128]{2,1,0:T(8,128)S(1)} %bitcast.137, f32[6,32,128]{2,1,0:T(8,128)S(1)} %all_gather.3, f32[6,32,6]{2,1,0:T(8,128)S(1)} %get-tuple-element.100, f32[6,32,122]{2,1,0:T(8,128)S(1)} %get-tuple-element.102, ...), kind=kLoop, calls=%fused_computation.309 | loop fusion | flops 2113536 | bytes 3047424 | tf_op jit(solution)/shard_map/sub | solution.py:100
  136.6 2.3 %collective-permute-start.7 = (f32[6,32,128]{2,1,0:T(8,128)S(1)}, f32[6,32,128]{2,1,0:T(8,128)}, u32[]{:S(2)}, u32[]{:S(2)}) collective-permute-start(f32[6,32,128]{2,1,0:T(8,128)S(1)} %multiply_subtract_fusion), channel_id=1, source_target_pairs={{0,4},{4,8},{8,12},{12,16},{16,20},{20,24},{24,28},{1,5},{5,9},{9,... | collective-permute-start | bytes 294920 | tf_op jit(solution)/shard_map/ppermute | solution.py:30
  147.2 4.7 %all-to-all-start.7 = ((f32[8,2,8]{2,1,0:T(2,128)}), f32[8,2,8]{2,1,0:T(2,128)S(1)}, u32[]{:S(2)}, u32[]{:S(2)}) async-start(f32[8,2,8]{2,1,0:T(2,128)} %broadcast_multiply_fusion.1), calls=%async_computation.7 | async-start | bytes 16384 | tf_op jit(solution)/shard_map/all_to_all | solution.py:72
  152.4 4.1 %all-to-all-done.7 = f32[8,2,8]{2,1,0:T(2,128)S(1)} async-done(((f32[8,2,8]{2,1,0:T(2,128)}), f32[8,2,8]{2,1,0:T(2,128)S(1)}, u32[]{:S(2)}, u32[]{:S(2)}) %all-to-all-start.7) | async-done | bytes 544 | tf_op jit(solution)/shard_map/all_to_all | solution.py:72
  157.6 3.3 %all-to-all-start.8 = ((f32[8,2,8]{2,1,0:T(2,128)}), f32[8,2,8]{2,1,0:T(2,128)S(1)}, u32[]{:S(2)}, u32[]{:S(2)}) async-start(f32[8,2,8]{2,1,0:T(2,128)} %bitcast.45), calls=%async_computation.8 | async-start | bytes 16384 | tf_op jit(solution)/shard_map/all_to_all | solution.py:78
  160.9 4.6 %all-to-all-done.8 = f32[8,2,8]{2,1,0:T(2,128)S(1)} async-done(((f32[8,2,8]{2,1,0:T(2,128)}), f32[8,2,8]{2,1,0:T(2,128)S(1)}, u32[]{:S(2)}, u32[]{:S(2)}) %all-to-all-start.8) | async-done | bytes 544 | tf_op jit(solution)/shard_map/all_to_all | solution.py:78
  170.4 2.7 %subtract_bitcast_fusion = f32[1,6,32,128]{3,2,1,0:T(8,128)} fusion(f32[6,32,128]{2,1,0:T(8,128)S(1)} %multiply_subtract_fusion.1, f32[6,32,128]{2,1,0:T(8,128)S(1)} %multiply_subtract_fusion, f32[6,32,128]{2,1,0:T(8,128)S(1)} %bitcast.134, f32[6,32,128]{2,1,0:T(8,128)S(1)} %all_gather.3, f32[6,32,6]{2,1,0:T(8,128)} %get-tuple-element.52, ...), kind=kLoop, calls=%fused_computation.308 | loop fusion | flops 2088960 | bytes 3047424 | tf_op jit(solution)/shard_map/broadcast_in_dim | solution.py:103
  (220 shorter events, 74.1 us)
Async XLA Ops:
  0.0 25.1 %copy-start = (f32[1,8,2,8,1024]{4,3,2,1,0:T(8,128)S(1)}, f32[1,8,2,8,1024]{4,3,2,1,0:T(8,128)}, u32[]{:S(2)}) copy-start(f32[1,8,2,8,1024]{4,3,2,1,0:T(8,128)} %param.8) | copy-start | bytes 1572868
  0.0 17.0 %copy-start.1 = (f32[1,6,32,128]{3,2,1,0:T(8,128)S(1)}, f32[1,6,32,128]{3,2,1,0:T(8,128)}, u32[]{:S(2)}) copy-start(f32[1,6,32,128]{3,2,1,0:T(8,128)} %param.6) | copy-start | bytes 294916
  0.0 55.9 %collective-permute-start.1 = (f32[6,32,128]{2,1,0:T(8,128)}, f32[6,32,128]{2,1,0:T(8,128)}, u32[]{:S(2)}, u32[]{:S(2)}) collective-permute-start(f32[6,32,128]{2,1,0:T(8,128)} %bitcast.104), channel_id=1, source_target_pairs={{0,4},{4,8},{8,12},{12,16},{16,20},{20,24},{24,28},{1,5},{5,9},{9,... | collective-permute-start | bytes 294920 | tf_op jit(solution)/shard_map/ppermute | solution.py:30
  3.1 52.8 %collective-permute-start = (f32[6,32,128]{2,1,0:T(8,128)}, f32[6,32,128]{2,1,0:T(8,128)}, u32[]{:S(2)}, u32[]{:S(2)}) collective-permute-start(f32[6,32,128]{2,1,0:T(8,128)} %bitcast.105), channel_id=1, source_target_pairs={{4,0},{8,4},{12,8},{16,12},{20,16},{24,20},{28,24},{5,1},{9,5},{13... | collective-permute-start | bytes 294920 | tf_op jit(solution)/shard_map/ppermute | solution.py:31
  5.8 21.1 %all-to-all-start = ((s32[8,1,2]{2,1,0:T(1,128)}), s32[8,1,2]{2,1,0:T(1,128)S(1)}, u32[]{:S(2)}, u32[]{:S(2)}) async-start(s32[8,1,2]{2,1,0:T(1,128)} %copy.22), calls=%async_computation | async-start | bytes 8192 | tf_op jit(solution)/shard_map/all_to_all | solution.py:66
  24.4 30.5 %copy-start.24 = (s32[128]{0:T(128)}, s32[128]{0:T(128)S(1)}, u32[]{:S(2)}) copy-start(s32[128]{0:T(128)S(1)} %fusion.249) | copy-start | bytes 1540
  26.8 8.9 %all-to-all-start.1 = ((f32[8,2,8]{2,1,0:T(2,128)}), f32[8,2,8]{2,1,0:T(2,128)S(1)}, u32[]{:S(2)}, u32[]{:S(2)}) async-start(f32[8,2,8]{2,1,0:T(2,128)} %broadcast_multiply_fusion.4), calls=%async_computation.1 | async-start | bytes 16384 | tf_op jit(solution)/shard_map/all_to_all | solution.py:72
  36.5 4.1 %copy-start.18 = (f32[6,8,128]{2,1,0:T(8,128)S(1)}, f32[6,8,128]{2,1,0:T(8,128)}, u32[]{:S(2)}) copy-start(f32[6,8,128]{2,1,0:T(8,128)} %param.7) | copy-start | bytes 73732
  37.3 16.8 %all-to-all-start.2 = ((f32[8,2,8]{2,1,0:T(2,128)}), f32[8,2,8]{2,1,0:T(2,128)S(1)}, u32[]{:S(2)}, u32[]{:S(2)}) async-start(f32[8,2,8]{2,1,0:T(2,128)} %bitcast.15), calls=%async_computation.2 | async-start | bytes 16384 | tf_op jit(solution)/shard_map/all_to_all | solution.py:78
  61.3 32.9 %collective-permute-start.3 = (f32[6,32,128]{2,1,0:T(8,128)S(1)}, f32[6,32,128]{2,1,0:T(8,128)}, u32[]{:S(2)}, u32[]{:S(2)}) collective-permute-start(f32[6,32,128]{2,1,0:T(8,128)S(1)} %get-tuple-element.5), channel_id=1, source_target_pairs={{0,4},{4,8},{8,12},{12,16},{16,20},{20,24},{24,28},{1,5},{5,9},{9,... | collective-permute-start | bytes 294920 | tf_op jit(solution)/shard_map/ppermute | solution.py:30
  63.2 31.0 %collective-permute-start.2 = (f32[6,32,128]{2,1,0:T(8,128)S(1)}, f32[6,32,128]{2,1,0:T(8,128)}, u32[]{:S(2)}, u32[]{:S(2)}) collective-permute-start(f32[6,32,128]{2,1,0:T(8,128)S(1)} %get-tuple-element.5), channel_id=1, source_target_pairs={{4,0},{8,4},{12,8},{16,12},{20,16},{24,20},{28,24},{5,1},{9,5},{13... | collective-permute-start | bytes 294920 | tf_op jit(solution)/shard_map/ppermute | solution.py:31
  72.1 11.2 %all-to-all-start.3 = ((f32[8,2,8]{2,1,0:T(2,128)}), f32[8,2,8]{2,1,0:T(2,128)S(1)}, u32[]{:S(2)}, u32[]{:S(2)}) async-start(f32[8,2,8]{2,1,0:T(2,128)} %broadcast_multiply_fusion.3), calls=%async_computation.3 | async-start | bytes 16384 | tf_op jit(solution)/shard_map/all_to_all | solution.py:72
  79.2 4.1 %copy-start.26 = (s32[16]{0:T(128)S(1)}, s32[16]{0:T(128)}, u32[]{:S(2)}) copy-start(s32[16]{0:T(128)} %copy-done.25) | copy-start | bytes 196
  84.4 8.0 %all-to-all-start.4 = ((f32[8,2,8]{2,1,0:T(2,128)}), f32[8,2,8]{2,1,0:T(2,128)S(1)}, u32[]{:S(2)}, u32[]{:S(2)}) async-start(f32[8,2,8]{2,1,0:T(2,128)} %bitcast.25), calls=%async_computation.4 | async-start | bytes 16384 | tf_op jit(solution)/shard_map/all_to_all | solution.py:78
  99.5 31.7 %collective-permute-start.5 = (f32[6,32,128]{2,1,0:T(8,128)S(1)}, f32[6,32,128]{2,1,0:T(8,128)}, u32[]{:S(2)}, u32[]{:S(2)}) collective-permute-start(f32[6,32,128]{2,1,0:T(8,128)S(1)} %multiply_subtract_fusion.1), channel_id=1, source_target_pairs={{0,4},{4,8},{8,12},{12,16},{16,20},{20,24},{24,28},{1,5},{5,9},{9,... | collective-permute-start | bytes 294920 | tf_op jit(solution)/shard_map/ppermute | solution.py:30
  101.9 29.3 %collective-permute-start.4 = (f32[6,32,128]{2,1,0:T(8,128)S(1)}, f32[6,32,128]{2,1,0:T(8,128)}, u32[]{:S(2)}, u32[]{:S(2)}) collective-permute-start(f32[6,32,128]{2,1,0:T(8,128)S(1)} %multiply_subtract_fusion.1), channel_id=1, source_target_pairs={{4,0},{8,4},{12,8},{16,12},{20,16},{24,20},{28,24},{5,1},{9,5},{13... | collective-permute-start | bytes 294920 | tf_op jit(solution)/shard_map/ppermute | solution.py:31
  110.8 9.4 %all-to-all-start.5 = ((f32[8,2,8]{2,1,0:T(2,128)}), f32[8,2,8]{2,1,0:T(2,128)S(1)}, u32[]{:S(2)}, u32[]{:S(2)}) async-start(f32[8,2,8]{2,1,0:T(2,128)} %broadcast_multiply_fusion.2), calls=%async_computation.5 | async-start | bytes 16384 | tf_op jit(solution)/shard_map/all_to_all | solution.py:72
  116.1 4.1 %copy-start.27 = (s32[16]{0:T(128)S(1)}, s32[16]{0:T(128)}, u32[]{:S(2)}) copy-start(s32[16]{0:T(128)} %copy-done.25) | copy-start | bytes 196
  121.2 8.0 %all-to-all-start.6 = ((f32[8,2,8]{2,1,0:T(2,128)}), f32[8,2,8]{2,1,0:T(2,128)S(1)}, u32[]{:S(2)}, u32[]{:S(2)}) async-start(f32[8,2,8]{2,1,0:T(2,128)} %bitcast.35), calls=%async_computation.6 | async-start | bytes 16384 | tf_op jit(solution)/shard_map/all_to_all | solution.py:78
  136.6 33.1 %collective-permute-start.7 = (f32[6,32,128]{2,1,0:T(8,128)S(1)}, f32[6,32,128]{2,1,0:T(8,128)}, u32[]{:S(2)}, u32[]{:S(2)}) collective-permute-start(f32[6,32,128]{2,1,0:T(8,128)S(1)} %multiply_subtract_fusion), channel_id=1, source_target_pairs={{0,4},{4,8},{8,12},{12,16},{16,20},{20,24},{24,28},{1,5},{5,9},{9,... | collective-permute-start | bytes 294920 | tf_op jit(solution)/shard_map/ppermute | solution.py:30
  138.9 30.8 %collective-permute-start.6 = (f32[6,32,128]{2,1,0:T(8,128)S(1)}, f32[6,32,128]{2,1,0:T(8,128)}, u32[]{:S(2)}, u32[]{:S(2)}) collective-permute-start(f32[6,32,128]{2,1,0:T(8,128)S(1)} %multiply_subtract_fusion), channel_id=1, source_target_pairs={{4,0},{8,4},{12,8},{16,12},{20,16},{24,20},{28,24},{5,1},{9,5},{13... | collective-permute-start | bytes 294920 | tf_op jit(solution)/shard_map/ppermute | solution.py:31
  147.2 9.4 %all-to-all-start.7 = ((f32[8,2,8]{2,1,0:T(2,128)}), f32[8,2,8]{2,1,0:T(2,128)S(1)}, u32[]{:S(2)}, u32[]{:S(2)}) async-start(f32[8,2,8]{2,1,0:T(2,128)} %broadcast_multiply_fusion.1), calls=%async_computation.7 | async-start | bytes 16384 | tf_op jit(solution)/shard_map/all_to_all | solution.py:72
  152.4 4.1 %copy-start.28 = (s32[16]{0:T(128)S(1)}, s32[16]{0:T(128)}, u32[]{:S(2)}) copy-start(s32[16]{0:T(128)} %copy-done.25) | copy-start | bytes 196
  157.6 8.0 %all-to-all-start.8 = ((f32[8,2,8]{2,1,0:T(2,128)}), f32[8,2,8]{2,1,0:T(2,128)S(1)}, u32[]{:S(2)}, u32[]{:S(2)}) async-start(f32[8,2,8]{2,1,0:T(2,128)} %bitcast.45), calls=%async_computation.8 | async-start | bytes 16384 | tf_op jit(solution)/shard_map/all_to_all | solution.py:78
  (22 other events, 19.7 us)
where the time goes:
time: 175 us; the launch traced here: 173 us
  starting transfers between devices  54.7 us (31%)
  local copies, waits for them, and re-layouts  47.6 us (27%)
  waiting for transfers between devices  27.9 us (16%)
  other arithmetic  18.2 us (10%)
  blocking collectives  13.5 us (8%)
  matrix products  10.3 us (6%)
    slice x48, local copies, waits for them, and re-layouts, kinetic(): jnp.roll(grid_field, distance, 1)  21.3 us
    all_to_all x4, starting transfers between devices, owner_side(): lax.all_to_all(partial_value, 'domain', split_axis=0, concat_axis=0, tile...  20.1 us
    all_to_all x4, waiting for transfers between devices, owner_side(): lax.all_to_all(partial_value, 'domain', split_axis=0, concat_axis=0, tile...  15.2 us
    slice x48, local copies, waits for them, and re-layouts, kinetic(): jnp.roll(grid_field, distance, 2)  14.5 us
    all_gather x1, blocking collectives, shards(): pot_full = lax.all_gather(potential, 'band', axis=1, tiled=True)  13.5 us
    all_to_all x4, starting transfers between devices, owner_side(): lax.all_to_all(returned, 'domain', split_axis=0, concat_axis=0, tiled=True)  13.3 us
    all_to_all x4, waiting for transfers between devices, owner_side(): lax.all_to_all(returned, 'domain', split_axis=0, concat_axis=0, tiled=True)  12.7 us
    ppermute x4, starting transfers between devices, extended(): before = lax.ppermute(last, axis, up)  9.69 us
  transfers between devices with their start and end apart: 17, of which 7 were waited for; matrix products, arithmetic and copies ran while one was open for 32% of the time, Pallas kernels for 0%

commit v1 on v0

v1 whole, which is shorter than its diff:
```python
import functools

import jax
import jax.numpy as jnp
from jax import lax
from jax.experimental import pallas as pl
from jax.experimental.pallas import tpu as pltpu
from jax.sharding import PartitionSpec as P

DEGREE = 4

stencil_weights = (
    -5369.0 / 1800.0,
    12.0 / 7.0,
    -15.0 / 56.0,
    10.0 / 189.0,
    -1.0 / 112.0,
    2.0 / 1925.0,
    -1.0 / 16632.0,
)
reach = len(stencil_weights) - 1
filter_center = 6.0
filter_half_width = 4.0
highest = lax.Precision.HIGHEST
f32 = jnp.float32
VMEM = pl.BlockSpec(memory_space=pltpu.VMEM)
SMEM = pl.BlockSpec(memory_space=pltpu.SMEM)


def iota(shape, dim):
    return lax.broadcasted_iota(jnp.int32, shape, dim)


def partials(y_ref, p_ref, off_ref, r_ref, dims):
    n, cap, nproj, foot, chunk = dims
    for slot in range(n * cap):
        start = off_ref[slot % cap, slot // cap]
        rows = pl.ds(slot * nproj, nproj)
        total = None
        for tile in range(foot):
            cells = jnp.broadcast_to(y_ref[pl.ds(start + tile, 1), :], (nproj, 128))
            term = p_ref[rows, tile * 128 : (tile + 1) * 128] * cells
            total = term if total is None else total + term
        r_ref[rows, :] = total
    return lax.dot_general(
        jnp.ones((8, 128), f32),
        r_ref[...],
        (((1,), (1,)), ((), ())),
        precision=highest,
        preferred_element_type=f32,
    )


def by_owner(rows, n, chunk):
    lanes = n * chunk
    shape = (n, lanes)
    ahead = (iota(shape, 1) // chunk - iota(shape, 0) + n) % n
    out = rows
    for step in range(1, n):
        moved = pltpu.roll(rows, n - step, 0)
        moved = pltpu.roll(moved, step * chunk, 1)
        out = jnp.where(ahead == step, moved, out)
    return out


def start_kernel(dims, y_ref, p_ref, off_ref, atom_ref, dmat_ref, out_ref, r_ref):
    n, cap, nproj, foot, chunk = dims
    lanes = n * chunk
    out_ref[:, 0, :] = jnp.broadcast_to(
        partials(y_ref, p_ref, off_ref, r_ref, dims)[0:1], (n, lanes)
    )
    lane = iota((1, lanes), 1) // nproj
    atoms = jnp.zeros((1, lanes), f32)
    for slot in range(n * cap):
        value = atom_ref[slot % cap, slot // cap].astype(f32)
        atoms = jnp.where(lane == slot, value, atoms)
    out_ref[:, 1, :] = jnp.broadcast_to(atoms, (n, lanes))
    count = dmat_ref.shape[1]
    for group in range(128 // count):
        block = dmat_ref[group * 2 * nproj : (group + 1) * 2 * nproj, :]
        for peer in range(n):
            out_ref[peer, 8:, group * count : (group + 1) * count] = block


def step_kernel(dims, nband, first, last, *refs):
    n, cap, nproj, foot, chunk = dims
    refs = list(refs)
    take = lambda: refs.pop(0)
    info_ref, off_ref = take(), take()
    y_ref, a_ref, b_ref, got_ref, p_ref = take(), take(), take(), take(), take()
    if first:
        atom_ref = take()
        v_pieces = [take() for _ in range(nband)]
        prev_ref = None
    else:
        prev_ref, v_ref, w_ref = take(), take(), take()
    out_ref = take()
    if not last:
        c_ref = take()
    if first:
        v_ref, w_ref = take(), take()
    pad_ref, lo_ref, hi_ref, r_ref = take(), take(), take(), take()
    cells = y_ref.shape[0]
    ny = 32
    planes = cells // ny
    lanes = n * chunk
    weights = stencil_weights

    if first:
        if nband > 1:
            piece_rows = ny // nband
            for back, piece in enumerate(v_pieces):
                at = lax.rem(info_ref[1] - back + nband, nband) * piece_rows
                for plane in range(planes):
                    spot = pl.multiple_of(plane * ny + at, 8)
                    v_ref[pl.ds(spot, piece_rows), :] = piece[
                        plane * piece_rows : (plane + 1) * piece_rows, :
                    ]
        else:
            v_ref[...] = v_pieces[0][...]
        atoms = by_owner(got_ref[:, 1, :], n, chunk)
        row = iota((chunk, 128), 0)
        column = iota((chunk, 128), 1)
        count = 128 // (nproj // 2)
        parity = (iota((chunk, 2 * nproj), 1) // nproj) == (iota((chunk, 2 * nproj), 0) % 2)
        spread = (iota((2 * nproj, lanes), 1) % nproj == iota((2 * nproj, lanes), 0) % nproj)
        spread = spread.astype(f32)
        for owner in range(n):
            mine = jnp.zeros((chunk, 128), jnp.int32)
            for k in range(cap):
                mine = jnp.where(row // nproj == k, atom_ref[k, owner], mine)
            pick = (column == (row % nproj) // 2 * count + mine) & (mine >= 0)
            entries = lax.dot_general(
                pick.astype(f32),
                got_ref[owner, 8:, 0:128],
                (((1,), (1,)), ((), ())),
                precision=highest,
                preferred_element_type=f32,
            )
            entries = jnp.where(parity, entries, 0.0)
            block = jnp.dot(entries, spread, precision=highest, preferred_element_type=f32)
            mine_row = jnp.zeros((chunk, lanes), f32)
            row_wide = iota((chunk, lanes), 0) // nproj
            for k in range(cap):
                mine_row = jnp.where(row_wide == k, atom_ref[k, owner].astype(f32), mine_row)
            same = (atoms[owner : owner + 1, :] == mine_row) & (mine_row >= 0.0)
            w_ref[pl.ds(owner * chunk, chunk), :] = jnp.where(same, block, 0.0)
        coefficients = by_owner(got_ref[:, 0, :], n, chunk)
    else:
        coefficients = by_owner(got_ref[...], n, chunk)

    odd = jnp.full((cells, 128), info_ref[0], jnp.int32) == 1
    from_a, from_b = a_ref[...], b_ref[...]
    lo_ref[...] = jnp.where(odd, from_a, from_b)
    hi_ref[...] = jnp.where(odd, from_b, from_a)
    tall = ny + 16
    for plane in range(planes):
        own = y_ref[plane * ny : (plane + 1) * ny, :]
        base = plane * tall
        pad_ref[base + 8 : base + 8 + ny, :] = own
        pad_ref[base : base + 8, :] = own[ny - 8 :, :]
        pad_ref[base + 8 + ny : base + tall, :] = own[0:8, :]

    apart = iota((128, 128), 0) - iota((128, 128), 1)
    apart = jnp.abs(apart)
    apart = jnp.minimum(apart, 128 - apart)
    circulant = jnp.full((128, 128), 3.0 * weights[0], f32)
    circulant = jnp.where(apart > reach, 0.0, circulant)
    for distance in range(1, reach + 1):
        circulant = jnp.where(apart == distance, weights[distance], circulant)
    along_z = jnp.dot(y_ref[...], circulant, precision=highest, preferred_element_type=f32)

    scale = (1.0 if first else 2.0) / filter_half_width

    def plane_of(index):
        if index < 0:
            ref, index = lo_ref, index + planes
        elif index >= planes:
            ref, index = hi_ref, index - planes
        else:
            ref = y_ref
        return ref[index * ny : (index + 1) * ny, :]

    for plane in range(planes):
        rows = slice(plane * ny, (plane + 1) * ny)
        base = plane * tall + 8
        own = y_ref[rows, :]
        lap = along_z[rows, :]
        for distance in range(1, reach + 1):
            beside = plane_of(plane + distance) + plane_of(plane - distance)
            beside = beside + pad_ref[base + distance : base + distance + ny, :]
            beside = beside + pad_ref[base - distance : base - distance + ny, :]
            lap = lap + weights[distance] * beside
        value = scale * ((v_ref[rows, :] - filter_center) * own - 0.5 * lap)
        if prev_ref is not None:
            value = value - prev_ref[rows, :]
        out_ref[rows, :] = value

    sublane = iota((foot, 128), 0)
    for slot in range(n * cap):
        owner = slot // cap
        rows = slice(slot * nproj, (slot + 1) * nproj)
        returned = jnp.sum(
            w_ref[rows, :] * coefficients[owner : owner + 1, :], axis=1, keepdims=True
        )
        returned = jnp.broadcast_to(returned * scale, (nproj, 128))
        contrib = jnp.zeros((foot, 128), f32)
        for tile in range(foot):
            term = jnp.sum(
                p_ref[rows, tile * 128 : (tile + 1) * 128] * returned, axis=0, keepdims=True
            )
            contrib = jnp.where(sublane == tile, term, contrib)
        start = off_ref[slot % cap, slot // cap]
        out_ref[pl.ds(start, foot), :] = out_ref[pl.ds(start, foot), :] + contrib

    if not last:
        c_ref[...] = jnp.broadcast_to(
            partials(out_ref, p_ref, off_ref, r_ref, dims)[0:1], (n, lanes)
        )


def beside_slabs(y, n):
    pairs = [(i, i ^ 1) for i in range(n) if i ^ 1 < n]
    cross = [(i, i + 1) for i in range(1, n - 1, 2)] + [(i + 1, i) for i in range(1, n - 1, 2)]
    return lax.ppermute(y, "domain", pairs), lax.ppermute(y, "domain", cross)


def shards(psi, potential, projectors, offsets, intersection, dmat):
    n = lax.axis_size("domain")
    nband = lax.axis_size("band")
    cap, nproj = projectors.shape[2], projectors.shape[3]
    foot = projectors.shape[4] // 128
    chunk = cap * nproj
    lanes = n * chunk
    dims = (n, cap, nproj, foot, chunk)
    cells = psi.shape[1] * psi.shape[2]
    y = psi.reshape(cells, 128)
    p = projectors.reshape(lanes, foot * 128)
    off = offsets[0].T
    atom = intersection[0].T
    couplings = dmat.transpose(1, 2, 0).reshape(nproj * nproj, dmat.shape[0])
    info = jnp.stack([lax.axis_index("domain") % 2, lax.axis_index("band")]).astype(jnp.int32)
    params = pltpu.CompilerParams(vmem_limit_bytes=40 * 1024 * 1024)

    start = pl.pallas_call(
        functools.partial(start_kernel, dims),
        out_shape=jax.ShapeDtypeStruct((n, 24, lanes), f32),
        in_specs=[VMEM, VMEM, SMEM, SMEM, VMEM],
        out_specs=VMEM,
        scratch_shapes=[pltpu.VMEM((lanes, 128), f32)],
        compiler_params=params,
        name="first_partials",
    )
    got = lax.all_to_all(
        start(y, p, off, atom, couplings), "domain", split_axis=0, concat_axis=0, tiled=True
    )
    if potential.shape[1] % 8 == 0 and nband <= 8:
        pieces = [potential.reshape(-1, 128)]
        for back in range(1, nband):
            ring = [(i, (i + back) % nband) for i in range(nband)]
            pieces.append(lax.ppermute(pieces[0], "band", ring))
    else:
        pieces = [lax.all_gather(potential, "band", axis=1, tiled=True).reshape(cells, 128)]

    y_shape = jax.ShapeDtypeStruct((cells, 128), f32)
    c_shape = jax.ShapeDtypeStruct((n, lanes), f32)
    scratch = [
        pltpu.VMEM((cells // 32 * 48, 128), f32),
        pltpu.VMEM((cells, 128), f32),
        pltpu.VMEM((cells, 128), f32),
        pltpu.VMEM((lanes, 128), f32),
    ]
    from_a, from_b = beside_slabs(y, n)
    previous = y
    y, c, v, w = pl.pallas_call(
        functools.partial(step_kernel, dims, len(pieces), True, False),
        out_shape=(y_shape, c_shape, y_shape, jax.ShapeDtypeStruct((lanes, lanes), f32)),
        in_specs=[SMEM, SMEM] + [VMEM] * 5 + [SMEM] + [VMEM] * len(pieces),
        out_specs=(VMEM,) * 4,
        scratch_shapes=scratch,
        compiler_params=params,
        name="first_step",
    )(info, off, y, from_a, from_b, got, p, atom, *pieces)
    for degree in range(1, DEGREE):
        last = degree == DEGREE - 1
        got = lax.all_to_all(c, "domain", split_axis=0, concat_axis=0, tiled=True)
        from_a, from_b = beside_slabs(y, n)
        out = pl.pallas_call(
            functools.partial(step_kernel, dims, len(pieces), False, last),
            out_shape=(y_shape,) if last else (y_shape, c_shape),
            in_specs=[SMEM, SMEM] + [VMEM] * 8,
            out_specs=(VMEM,) if last else (VMEM, VMEM),
            scratch_shapes=scratch,
            compiler_params=params,
            name="last_step" if last else "next_step",
        )(info, off, y, from_a, from_b, got, p, previous, v, w)
        previous, y = y, out[0]
        if not last:
            c = out[1]
    return y.reshape(psi.shape)


def solution(mesh):
    return jax.shard_map(
        shards,
        mesh=mesh,
        in_specs=(
            P("band", "domain", None, None),
            P("domain", "band", None),
            P("domain", None, None, None, None),
            P("domain", None, None),
            P("domain", None, None),
            P("domain", None, None),
        ),
        out_specs=P("band", "domain", None, None),
        check_vma=False,
    )
```

time: 175 us -> 60.5 us (0.35)
  local copies, waits for them, and re-layouts: 47.6 us -> 3.4 us
  starting transfers between devices: 54.7 us -> 21.1 us
  waiting for transfers between devices: 27.9 us -> 5.04 us
  other arithmetic: 18.2 us -> 0.08 us
  matrix products: 10.3 us -> 0 us
  Pallas kernels: 0 us -> 8.68 us
  blocking collectives: 13.5 us -> 21.5 us
    all_to_all x9 -> x1, starting transfers between devices: 39.8 us -> 3.49 us  [shards(): lax.all_to_all(start(y, p, off, atom, couplings), 'domain', split_axis=0,...]
    slice x96 -> x0, local copies, waits for them, and re-layouts: 35.7 us -> none  [the longest x48 21.3 us: kinetic(): jnp.roll(grid_field, distance, 1)]
    all_to_all x9 -> x1, waiting for transfers between devices: 27.9 us -> 5.01 us  [shards(): lax.all_to_all(start(y, p, off, atom, couplings), 'domain', split_axis=0,...]
    all_to_all x0 -> x3, blocking collectives: none -> 21.5 us  [shards(): got = lax.all_to_all(c, 'domain', split_axis=0, concat_axis=0, tiled=True)]
    all_gather x1 -> x0, blocking collectives: 13.5 us -> none  [shards(): pot_full = lax.all_gather(potential, 'band', axis=1, tiled=True)]
    dot_general x16 -> x0, matrix products: 10.3 us -> none  [the longest x4 4.21 us: hamiltonian(): jnp.einsum('dkil,dkl->dki', projector_block, footprint, precision=highest)]
    pallas_call x0 -> x5, Pallas kernels: none -> 8.68 us  [the longest x3 4.56 us: shards(): pl.pallas_call(functools.partial(step_kernel, dims, len(pieces), False, l...]
    scatter-add x4 -> x0, other arithmetic: 4.87 us -> none  [hamiltonian(): jnp.zeros_like(tiles).at[tile_index].add(contrib).reshape(grid_field.shape)]
  transfers between devices with their start and end apart: 17 -> 12, of which waited for: 7 -> 1; matrix products, arithmetic and copies ran while one was open for 32% -> 0% of each run, Pallas kernels for 0% -> 2%
where the time goes in v1:
time: 60.5 us; the launch traced here: 59.9 us
  blocking collectives  21.5 us (36%)
  starting transfers between devices  21.1 us (35%)
  Pallas kernels  8.68 us (14%)
  waiting for transfers between devices  5.04 us (8%)
  local copies, waits for them, and re-layouts  3.4 us (6%)
    all_to_all x3, blocking collectives, shards(): got = lax.all_to_all(c, 'domain', split_axis=0, concat_axis=0, tiled=True)  21.5 us
    ppermute x8, starting transfers between devices, beside_slabs(): return (lax.ppermute(y, 'domain', pairs), lax.ppermute(y, 'domain', cross))  11.6 us
    ppermute x3, starting transfers between devices, shards(): pieces.append(lax.ppermute(pieces[0], 'band', ring))  6.06 us
    all_to_all x1, waiting for transfers between devices, shards(): lax.all_to_all(start(y, p, off, atom, couplings), 'domain', split_axis=0,...  5.01 us
    pallas_call x3, Pallas kernels, shards(): pl.pallas_call(functools.partial(step_kernel, dims, len(pieces), False, l...  4.56 us
    all_to_all x1, starting transfers between devices, shards(): lax.all_to_all(start(y, p, off, atom, couplings), 'domain', split_axis=0,...  3.49 us
    unnamed x16, local copies, waits for them, and re-layouts  3.4 us
    pallas_call x1, Pallas kernels, shards(): pl.pallas_call(functools.partial(step_kernel, dims, len(pieces), True, Fa...  2.67 us
  transfers between devices with their start and end apart: 12, of which 1 were waited for; matrix products, arithmetic and copies ran while one was open for 0% of the time, Pallas kernels for 2%

profile of v1, /device:TPU:0, one launch (start us, length us, event | category | flops | bytes accessed | tf_op | source)
XLA Modules:
  0.0 59.9 jit_solution(6365599587710857058)
XLA Ops:
  0.0 5.0 %collective-permute-start.4 = (f32[48,128]{1,0:T(8,128)}, f32[48,128]{1,0:T(8,128)S(1)}, u32[]{:S(2)}, u32[]{:S(2)}) collective-permute-start(f32[48,128]{1,0:T(8,128)} %bitcast.43), channel_id=1, source_target_pairs={{0,3},{1,0},{2,1},{3,2},{4,7},{5,4},{6,5},{7,6},{8,11},{9,8},{10,9... | collective-permute-start | bytes 73736 | tf_op jit(solution)/shard_map/ppermute | solution.py:261
  5.1 1.0 %collective-permute-start.2 = (f32[48,128]{1,0:T(8,128)}, f32[48,128]{1,0:T(8,128)S(1)}, u32[]{:S(2)}, u32[]{:S(2)}) collective-permute-start(f32[48,128]{1,0:T(8,128)} %bitcast.45), channel_id=1, source_target_pairs={{0,1},{1,2},{2,3},{3,0},{4,5},{5,6},{6,7},{7,4},{8,9},{9,10},{10,1... | collective-permute-start | bytes 73736 | tf_op jit(solution)/shard_map/ppermute | solution.py:261
  6.1 0.7 %collective-permute-start.1 = (f32[192,128]{1,0:T(8,128)}, f32[192,128]{1,0:T(8,128)S(1)}, u32[]{:S(2)}, u32[]{:S(2)}) collective-permute-start(f32[192,128]{1,0:T(8,128)} %bitcast.32), channel_id=1, source_target_pairs={{4,8},{12,16},{20,24},{8,4},{16,12},{24,20},{5,9},{13,17},{21,25},... | collective-permute-start | bytes 294920 | tf_op jit(solution)/shard_map/ppermute | solution.py:225
  6.7 2.9 %collective-permute-start = (f32[192,128]{1,0:T(8,128)}, f32[192,128]{1,0:T(8,128)S(1)}, u32[]{:S(2)}, u32[]{:S(2)}) collective-permute-start(f32[192,128]{1,0:T(8,128)} %bitcast.33), channel_id=1, source_target_pairs={{0,4},{4,0},{8,12},{12,8},{16,20},{20,16},{24,28},{28,24},{1,5},{5... | collective-permute-start | bytes 294920 | tf_op jit(solution)/shard_map/ppermute | solution.py:225
  9.6 0.7 %copy-done.7 = s32[1,8,2]{1,2,0:T(2,128)S(1)} copy-done((s32[1,8,2]{1,2,0:T(2,128)S(1)}, s32[1,8,2]{1,2,0:T(2,128)}, u32[]{:S(2)}) %copy-start.7) | copy-done | bytes 88
  10.3 1.0 %copy-done = f32[1,8,2,8,1024]{4,3,2,1,0:T(8,128)S(1)} copy-done((f32[1,8,2,8,1024]{4,3,2,1,0:T(8,128)S(1)}, f32[1,8,2,8,1024]{4,3,2,1,0:T(8,128)}, u32[]{:S(2)}) %copy-start) | copy-done | bytes 524312
  11.4 0.9 %copy-done.2 = f32[1,6,32,128]{3,2,1,0:T(8,128)S(1)} copy-done((f32[1,6,32,128]{3,2,1,0:T(8,128)S(1)}, f32[1,6,32,128]{3,2,1,0:T(8,128)}, u32[]{:S(2)}) %copy-start.2) | copy-done | bytes 98328
  12.3 0.8 %copy-done.4 = f32[32,8,8]{0,2,1:T(8,128)S(1)} copy-done((f32[32,8,8]{0,2,1:T(8,128)S(1)}, f32[32,8,8]{0,2,1:T(8,128)}, u32[]{:S(2)}) %copy-start.4) | copy-done | bytes 8216
  13.0 1.5 %first_partials.1 = f32[8,24,128]{2,1,0:T(8,128)} custom-call(f32[192,128]{1,0:T(8,128)S(1)} %bitcast.34, f32[128,1024]{1,0:T(8,128)S(1)} %bitcast.27, s32[2,8]{1,0:T(2,128)S(1)} %bitcast.38, s32[2,8]{1,0:T(2,128)S(1)} %bitcast.50, f32[64,32]{1,0:T(8,128)S(1)} %bitcast.37), custom_call_target="tpu_custom_call" | custom-call | tf_op jit(solution)/shard_map/first_partials/pallas_call | solution.py:255
  14.5 3.5 %all-to-all-start = ((f32[8,24,128]{2,1,0:T(8,128)}), f32[8,24,128]{2,1,0:T(8,128)S(1)}, u32[]{:S(2)}, u32[]{:S(2)}) async-start(f32[8,24,128]{2,1,0:T(8,128)} %first_partials.1), calls=%async_computation | async-start | bytes 196608 | tf_op jit(solution)/shard_map/all_to_all | solution.py:254
  18.1 5.0 %all-to-all-done.refs_5_ = f32[8,24,128]{2,1,0:T(8,128)S(1)} async-done(((f32[8,24,128]{2,1,0:T(8,128)}), f32[8,24,128]{2,1,0:T(8,128)S(1)}, u32[]{:S(2)}, u32[]{:S(2)}) %all-to-all-start) | async-done | bytes 98336 | tf_op jit(solution)/shard_map/all_to_all | solution.py:254
  23.1 2.7 %first_step.1 = (f32[192,128]{1,0:T(8,128)S(1)}, f32[8,128]{1,0:T(8,128)S(1)}, f32[192,128]{1,0:T(8,128)S(1)}, f32[128,128]{1,0:T(8,128)S(1)}) custom-call(s32[2]{0:T(128)S(1)} %pad_add_fusion.refs_0_, s32[2,8]{1,0:T(2,128)S(1)} %bitcast.39, f32[192,128]{1,0:T(8,128)S(1)} %bitcast.35, f32[192,128]{1,0:T(8,128)S(1)} %collective-permute-done.refs_3_, ...), custom_call_target="tpu_custom_call" | custom-call | tf_op jit(solution)/shard_map/first_step/pallas_call | solution.py:275
  25.8 0.7 %collective-permute-start.6 = (f32[192,128]{1,0:T(8,128)S(1)}, f32[192,128]{1,0:T(8,128)S(1)}, u32[]{:S(2)}, u32[]{:S(2)}) collective-permute-start(f32[192,128]{1,0:T(8,128)S(1)} %get-tuple-element.13.refs_2_.refs_7_), channel_id=1, source_target_pairs={{4,8},{12,16},{20,24},{8,4},{16,12},{24,20},{5,9},{13,17},{21,25},... | collective-permute-start | bytes 294920 | tf_op jit(solution)/shard_map/ppermute | solution.py:225
  26.5 2.0 %collective-permute-start.5 = (f32[192,128]{1,0:T(8,128)S(1)}, f32[192,128]{1,0:T(8,128)S(1)}, u32[]{:S(2)}, u32[]{:S(2)}) collective-permute-start(f32[192,128]{1,0:T(8,128)S(1)} %get-tuple-element.13.refs_2_.refs_7_), channel_id=1, source_target_pairs={{0,4},{4,0},{8,12},{12,8},{16,20},{20,16},{24,28},{28,24},{1,5},{5... | collective-permute-start | bytes 294920 | tf_op jit(solution)/shard_map/ppermute | solution.py:225
  28.5 7.2 %all_to_all.38 = f32[8,1,128]{2,1,0:T(1,128)S(1)} all-to-all(f32[8,1,128]{2,1,0:T(1,128)S(1)} %bitcast.52), channel_id=1, replica_groups=mesh['domain'=8,'band'=4] {'domain'}, dimensions={0} | all-to-all | bytes 8192 | tf_op jit(solution)/shard_map/all_to_all | solution.py:286
  35.6 1.4 %next_step.2 = (f32[192,128]{1,0:T(8,128)S(1)}, f32[8,128]{1,0:T(8,128)S(1)}) custom-call(s32[2]{0:T(128)S(1)} %pad_add_fusion.refs_0_, s32[2,8]{1,0:T(2,128)S(1)} %bitcast.40, f32[192,128]{1,0:T(8,128)S(1)} %get-tuple-element.13.refs_2_.refs_7_, f32[192,128]{1,0:T(8,128)S(1)} %collective-permute-done.5.refs_3_, ...), custom_call_target="tpu_custom_call" | custom-call | tf_op jit(solution)/shard_map/next_step/pallas_call | solution.py:288
  37.1 0.7 %collective-permute-start.8 = (f32[192,128]{1,0:T(8,128)S(1)}, f32[192,128]{1,0:T(8,128)S(1)}, u32[]{:S(2)}, u32[]{:S(2)}) collective-permute-start(f32[192,128]{1,0:T(8,128)S(1)} %get-tuple-element.17.refs_2_.refs_7_), channel_id=1, source_target_pairs={{4,8},{12,16},{20,24},{8,4},{16,12},{24,20},{5,9},{13,17},{21,25},... | collective-permute-start | bytes 294920 | tf_op jit(solution)/shard_map/ppermute | solution.py:225
  37.8 2.0 %collective-permute-start.7 = (f32[192,128]{1,0:T(8,128)S(1)}, f32[192,128]{1,0:T(8,128)S(1)}, u32[]{:S(2)}, u32[]{:S(2)}) collective-permute-start(f32[192,128]{1,0:T(8,128)S(1)} %get-tuple-element.17.refs_2_.refs_7_), channel_id=1, source_target_pairs={{0,4},{4,0},{8,12},{12,8},{16,20},{20,16},{24,28},{28,24},{1,5},{5... | collective-permute-start | bytes 294920 | tf_op jit(solution)/shard_map/ppermute | solution.py:225
  39.7 7.2 %all_to_all.39 = f32[8,1,128]{2,1,0:T(1,128)S(1)} all-to-all(f32[8,1,128]{2,1,0:T(1,128)S(1)} %bitcast.54), channel_id=1, replica_groups=mesh['domain'=8,'band'=4] {'domain'}, dimensions={0} | all-to-all | bytes 8192 | tf_op jit(solution)/shard_map/all_to_all | solution.py:286
  46.9 1.4 %next_step.3 = (f32[192,128]{1,0:T(8,128)S(1)}, f32[8,128]{1,0:T(8,128)S(1)}) custom-call(s32[2]{0:T(128)S(1)} %pad_add_fusion.refs_0_, s32[2,8]{1,0:T(2,128)S(1)} %bitcast.41, f32[192,128]{1,0:T(8,128)S(1)} %get-tuple-element.17.refs_2_.refs_7_, f32[192,128]{1,0:T(8,128)S(1)} %collective-permute-done.7.refs_3_, ...), custom_call_target="tpu_custom_call" | custom-call | tf_op jit(solution)/shard_map/next_step/pallas_call | solution.py:288
  48.3 0.7 %collective-permute-start.10 = (f32[192,128]{1,0:T(8,128)S(1)}, f32[192,128]{1,0:T(8,128)S(1)}, u32[]{:S(2)}, u32[]{:S(2)}) collective-permute-start(f32[192,128]{1,0:T(8,128)S(1)} %get-tuple-element.19.refs_2_), channel_id=1, source_target_pairs={{4,8},{12,16},{20,24},{8,4},{16,12},{24,20},{5,9},{13,17},{21,25},... | collective-permute-start | bytes 294920 | tf_op jit(solution)/shard_map/ppermute | solution.py:225
  49.0 2.0 %collective-permute-start.9 = (f32[192,128]{1,0:T(8,128)S(1)}, f32[192,128]{1,0:T(8,128)S(1)}, u32[]{:S(2)}, u32[]{:S(2)}) collective-permute-start(f32[192,128]{1,0:T(8,128)S(1)} %get-tuple-element.19.refs_2_), channel_id=1, source_target_pairs={{0,4},{4,0},{8,12},{12,8},{16,20},{20,16},{24,28},{28,24},{1,5},{5... | collective-permute-start | bytes 294920 | tf_op jit(solution)/shard_map/ppermute | solution.py:225
  51.0 7.2 %all_to_all.40 = f32[8,1,128]{2,1,0:T(1,128)S(1)} all-to-all(f32[8,1,128]{2,1,0:T(1,128)S(1)} %bitcast.53), channel_id=1, replica_groups=mesh['domain'=8,'band'=4] {'domain'}, dimensions={0} | all-to-all | bytes 8192 | tf_op jit(solution)/shard_map/all_to_all | solution.py:286
  58.2 1.7 %last_step.1 = f32[192,128]{1,0:T(8,128)} custom-call(s32[2]{0:T(128)S(1)} %pad_add_fusion.refs_0_, s32[2,8]{1,0:T(2,128)S(1)} %bitcast.42, f32[192,128]{1,0:T(8,128)S(1)} %get-tuple-element.19.refs_2_, f32[192,128]{1,0:T(8,128)S(1)} %collective-permute-done.9.refs_3_, f32[192,128]{1,0:T(8,128)S(1)} %collective-permute-done.10.refs_4_, ...), custom_call_target="tpu_custom_call" | custom-call | tf_op jit(solution)/shard_map/last_step/pallas_call | solution.py:288
  (25 shorter events, 0.1 us)
Async XLA Ops:
  0.0 18.1 %collective-permute-start.4 = (f32[48,128]{1,0:T(8,128)}, f32[48,128]{1,0:T(8,128)S(1)}, u32[]{:S(2)}, u32[]{:S(2)}) collective-permute-start(f32[48,128]{1,0:T(8,128)} %bitcast.43), channel_id=1, source_target_pairs={{0,3},{1,0},{2,1},{3,2},{4,7},{5,4},{6,5},{7,6},{8,11},{9,8},{10,9... | collective-permute-start | bytes 73736 | tf_op jit(solution)/shard_map/ppermute | solution.py:261
  5.0 13.0 %collective-permute-start.3 = (f32[48,128]{1,0:T(8,128)}, f32[48,128]{1,0:T(8,128)S(1)}, u32[]{:S(2)}, u32[]{:S(2)}) collective-permute-start(f32[48,128]{1,0:T(8,128)} %bitcast.44), channel_id=1, source_target_pairs={{0,2},{1,3},{2,0},{3,1},{4,6},{5,7},{6,4},{7,5},{8,10},{9,11},{10,... | collective-permute-start | bytes 73736 | tf_op jit(solution)/shard_map/ppermute | solution.py:261
  5.1 13.0 %collective-permute-start.2 = (f32[48,128]{1,0:T(8,128)}, f32[48,128]{1,0:T(8,128)S(1)}, u32[]{:S(2)}, u32[]{:S(2)}) collective-permute-start(f32[48,128]{1,0:T(8,128)} %bitcast.45), channel_id=1, source_target_pairs={{0,1},{1,2},{2,3},{3,0},{4,5},{5,6},{6,7},{7,4},{8,9},{9,10},{10,1... | collective-permute-start | bytes 73736 | tf_op jit(solution)/shard_map/ppermute | solution.py:261
  6.1 17.1 %collective-permute-start.1 = (f32[192,128]{1,0:T(8,128)}, f32[192,128]{1,0:T(8,128)S(1)}, u32[]{:S(2)}, u32[]{:S(2)}) collective-permute-start(f32[192,128]{1,0:T(8,128)} %bitcast.32), channel_id=1, source_target_pairs={{4,8},{12,16},{20,24},{8,4},{16,12},{24,20},{5,9},{13,17},{21,25},... | collective-permute-start | bytes 294920 | tf_op jit(solution)/shard_map/ppermute | solution.py:225
  6.7 16.4 %collective-permute-start = (f32[192,128]{1,0:T(8,128)}, f32[192,128]{1,0:T(8,128)S(1)}, u32[]{:S(2)}, u32[]{:S(2)}) collective-permute-start(f32[192,128]{1,0:T(8,128)} %bitcast.33), channel_id=1, source_target_pairs={{0,4},{4,0},{8,12},{12,8},{16,20},{20,16},{24,28},{28,24},{1,5},{5... | collective-permute-start | bytes 294920 | tf_op jit(solution)/shard_map/ppermute | solution.py:225
  9.6 0.7 %copy-start.7 = (s32[1,8,2]{1,2,0:T(2,128)S(1)}, s32[1,8,2]{1,2,0:T(2,128)}, u32[]{:S(2)}) copy-start(s32[1,8,2]{1,2,0:T(2,128)} %param.10) | copy-start | bytes 196
  9.6 0.7 %copy-start.5 = (s32[1,8,2]{1,2,0:T(2,128)S(1)}, s32[1,8,2]{1,2,0:T(2,128)}, u32[]{:S(2)}) copy-start(s32[1,8,2]{1,2,0:T(2,128)} %param.9) | copy-start | bytes 196
  10.3 1.0 %copy-start = (f32[1,8,2,8,1024]{4,3,2,1,0:T(8,128)S(1)}, f32[1,8,2,8,1024]{4,3,2,1,0:T(8,128)}, u32[]{:S(2)}) copy-start(f32[1,8,2,8,1024]{4,3,2,1,0:T(8,128)} %param.8) | copy-start | bytes 1572868
  11.4 0.9 %copy-start.2 = (f32[1,6,32,128]{3,2,1,0:T(8,128)S(1)}, f32[1,6,32,128]{3,2,1,0:T(8,128)}, u32[]{:S(2)}) copy-start(f32[1,6,32,128]{3,2,1,0:T(8,128)} %param.6) | copy-start | bytes 294916
  12.3 0.8 %copy-start.4 = (f32[32,8,8]{0,2,1:T(8,128)S(1)}, f32[32,8,8]{0,2,1:T(8,128)}, u32[]{:S(2)}) copy-start(f32[32,8,8]{0,2,1:T(8,128)} %param.11) | copy-start | bytes 24580
  13.0 10.1 %copy-start.1 = (f32[1,8,2,8,1024]{4,3,2,1,0:T(8,128)S(1)}, f32[1,8,2,8,1024]{4,3,2,1,0:T(8,128)}, u32[]{:S(2)}) copy-start(f32[1,8,2,8,1024]{4,3,2,1,0:T(8,128)} %param.8) | copy-start | bytes 1572868
  14.5 8.6 %copy-start.3 = (f32[1,6,32,128]{3,2,1,0:T(8,128)S(1)}, f32[1,6,32,128]{3,2,1,0:T(8,128)}, u32[]{:S(2)}) copy-start(f32[1,6,32,128]{3,2,1,0:T(8,128)} %param.6) | copy-start | bytes 294916
  14.5 8.6 %all-to-all-start = ((f32[8,24,128]{2,1,0:T(8,128)}), f32[8,24,128]{2,1,0:T(8,128)S(1)}, u32[]{:S(2)}, u32[]{:S(2)}) async-start(f32[8,24,128]{2,1,0:T(8,128)} %first_partials.1), calls=%async_computation | async-start | bytes 196608 | tf_op jit(solution)/shard_map/all_to_all | solution.py:254
  18.0 5.1 %copy-start.6 = (f32[6,8,128]{2,1,0:T(8,128)S(1)}, f32[6,8,128]{2,1,0:T(8,128)}, u32[]{:S(2)}) copy-start(f32[6,8,128]{2,1,0:T(8,128)} %param.7) | copy-start | bytes 73732
  25.8 9.8 %collective-permute-start.6 = (f32[192,128]{1,0:T(8,128)S(1)}, f32[192,128]{1,0:T(8,128)S(1)}, u32[]{:S(2)}, u32[]{:S(2)}) collective-permute-start(f32[192,128]{1,0:T(8,128)S(1)} %get-tuple-element.13.refs_2_.refs_7_), channel_id=1, source_target_pairs={{4,8},{12,16},{20,24},{8,4},{16,12},{24,20},{5,9},{13,17},{21,25},... | collective-permute-start | bytes 294920 | tf_op jit(solution)/shard_map/ppermute | solution.py:225
  26.5 9.1 %collective-permute-start.5 = (f32[192,128]{1,0:T(8,128)S(1)}, f32[192,128]{1,0:T(8,128)S(1)}, u32[]{:S(2)}, u32[]{:S(2)}) collective-permute-start(f32[192,128]{1,0:T(8,128)S(1)} %get-tuple-element.13.refs_2_.refs_7_), channel_id=1, source_target_pairs={{0,4},{4,0},{8,12},{12,8},{16,20},{20,16},{24,28},{28,24},{1,5},{5... | collective-permute-start | bytes 294920 | tf_op jit(solution)/shard_map/ppermute | solution.py:225
  37.1 9.9 %collective-permute-start.8 = (f32[192,128]{1,0:T(8,128)S(1)}, f32[192,128]{1,0:T(8,128)S(1)}, u32[]{:S(2)}, u32[]{:S(2)}) collective-permute-start(f32[192,128]{1,0:T(8,128)S(1)} %get-tuple-element.17.refs_2_.refs_7_), channel_id=1, source_target_pairs={{4,8},{12,16},{20,24},{8,4},{16,12},{24,20},{5,9},{13,17},{21,25},... | collective-permute-start | bytes 294920 | tf_op jit(solution)/shard_map/ppermute | solution.py:225
  37.8 9.2 %collective-permute-start.7 = (f32[192,128]{1,0:T(8,128)S(1)}, f32[192,128]{1,0:T(8,128)S(1)}, u32[]{:S(2)}, u32[]{:S(2)}) collective-permute-start(f32[192,128]{1,0:T(8,128)S(1)} %get-tuple-element.17.refs_2_.refs_7_), channel_id=1, source_target_pairs={{0,4},{4,0},{8,12},{12,8},{16,20},{20,16},{24,28},{28,24},{1,5},{5... | collective-permute-start | bytes 294920 | tf_op jit(solution)/shard_map/ppermute | solution.py:225
  48.3 9.9 %collective-permute-start.10 = (f32[192,128]{1,0:T(8,128)S(1)}, f32[192,128]{1,0:T(8,128)S(1)}, u32[]{:S(2)}, u32[]{:S(2)}) collective-permute-start(f32[192,128]{1,0:T(8,128)S(1)} %get-tuple-element.19.refs_2_), channel_id=1, source_target_pairs={{4,8},{12,16},{20,24},{8,4},{16,12},{24,20},{5,9},{13,17},{21,25},... | collective-permute-start | bytes 294920 | tf_op jit(solution)/shard_map/ppermute | solution.py:225
  49.0 9.2 %collective-permute-start.9 = (f32[192,128]{1,0:T(8,128)S(1)}, f32[192,128]{1,0:T(8,128)S(1)}, u32[]{:S(2)}, u32[]{:S(2)}) collective-permute-start(f32[192,128]{1,0:T(8,128)S(1)} %get-tuple-element.19.refs_2_), channel_id=1, source_target_pairs={{0,4},{4,0},{8,12},{12,8},{16,20},{20,16},{24,28},{28,24},{1,5},{5... | collective-permute-start | bytes 294920 | tf_op jit(solution)/shard_map/ppermute | solution.py:225

commit v2 on v1

v2 whole, which is shorter than its diff:
```python
import functools

import jax
import jax.numpy as jnp
from jax import lax
from jax.experimental import pallas as pl
from jax.experimental.pallas import tpu as pltpu
from jax.sharding import PartitionSpec as P

DEGREE = 4
BIG = 100000

stencil_weights = (
    -5369.0 / 1800.0,
    12.0 / 7.0,
    -15.0 / 56.0,
    10.0 / 189.0,
    -1.0 / 112.0,
    2.0 / 1925.0,
    -1.0 / 16632.0,
)
reach = len(stencil_weights) - 1
filter_center = 6.0
filter_half_width = 4.0
highest = lax.Precision.HIGHEST
f32 = jnp.float32
VMEM = pl.BlockSpec(memory_space=pltpu.VMEM)
SMEM = pl.BlockSpec(memory_space=pltpu.SMEM)


def iota(shape, dim):
    return lax.broadcasted_iota(jnp.int32, shape, dim)


def partials(y_ref, p_ref, off_ref, r_ref, dims):
    n, cap, nproj, foot, chunk = dims
    for slot in range(n * cap):
        start = off_ref[slot % cap, slot // cap]
        rows = pl.ds(slot * nproj, nproj)
        total = None
        for tile in range(foot):
            cells = jnp.broadcast_to(y_ref[pl.ds(start + tile, 1), :], (nproj, 128))
            term = p_ref[rows, tile * 128 : (tile + 1) * 128] * cells
            total = term if total is None else total + term
        r_ref[rows, :] = total
    return lax.dot_general(
        jnp.ones((8, 128), f32),
        r_ref[...],
        (((1,), (1,)), ((), ())),
        precision=highest,
        preferred_element_type=f32,
    )


def by_owner(rows, n, chunk):
    lanes = n * chunk
    shape = (n, lanes)
    ahead = (iota(shape, 1) // chunk - iota(shape, 0) + n) % n
    out = rows
    for step in range(1, n):
        moved = pltpu.roll(rows, n - step, 0)
        moved = pltpu.roll(moved, step * chunk, 1)
        out = jnp.where(ahead == step, moved, out)
    return out


def start_kernel(dims, *refs):
    n, cap, nproj, foot, chunk = dims
    sources, (out_ref, y_ref, p_ref, v_ref) = refs[:6], refs[6:10]
    off_ref, atom_ref, dmat_ref, r_ref, sems = refs[10:]
    lanes = n * chunk
    targets = (y_ref, p_ref, off_ref, atom_ref, dmat_ref, v_ref)
    copies = [
        pltpu.make_async_copy(source, target, sems.at[index])
        for index, (source, target) in enumerate(zip(sources, targets))
    ]
    for copy in copies:
        copy.start()
    copies[3].wait()
    copies[4].wait()
    lane = iota((1, lanes), 1) // nproj
    atoms = jnp.zeros((1, lanes), f32)
    for slot in range(n * cap):
        value = atom_ref[slot % cap, slot // cap].astype(f32)
        atoms = jnp.where(lane == slot, value, atoms)
    out_ref[:, 1, :] = jnp.broadcast_to(atoms, (n, lanes))
    count = dmat_ref.shape[1]
    for group in range(128 // count):
        block = dmat_ref[group * 2 * nproj : (group + 1) * 2 * nproj, :]
        for peer in range(n):
            out_ref[peer, 8:, group * count : (group + 1) * count] = block
    for copy in copies[:3] + copies[5:]:
        copy.wait()
    out_ref[:, 0, :] = jnp.broadcast_to(
        partials(y_ref, p_ref, off_ref, r_ref, dims)[0:1], (n, lanes)
    )


def local_kernel(first, *refs):
    if first:
        y_ref, part_ref, pad_ref = refs
    else:
        y_ref, v_ref, prev_ref, part_ref, pad_ref = refs
    weights = stencil_weights
    ny = 32
    planes = y_ref.shape[0] // ny
    tall = ny + 16
    for plane in range(planes):
        own = y_ref[plane * ny : (plane + 1) * ny, :]
        base = plane * tall
        pad_ref[base + 8 : base + 8 + ny, :] = own
        pad_ref[base : base + 8, :] = own[ny - 8 :, :]
        pad_ref[base + 8 + ny : base + tall, :] = own[0:8, :]
    apart = jnp.abs(iota((128, 128), 0) - iota((128, 128), 1))
    apart = jnp.minimum(apart, 128 - apart)
    circulant = jnp.full((128, 128), 3.0 * weights[0], f32)
    circulant = jnp.where(apart > reach, 0.0, circulant)
    for distance in range(1, reach + 1):
        circulant = jnp.where(apart == distance, weights[distance], circulant)
    along_z = jnp.dot(y_ref[...], circulant, precision=highest, preferred_element_type=f32)
    scale = (1.0 if first else 2.0) / filter_half_width
    for plane in range(planes):
        rows = slice(plane * ny, (plane + 1) * ny)
        base = plane * tall + 8
        own = y_ref[rows, :]
        lap = along_z[rows, :]
        for distance in range(1, reach + 1):
            beside = pad_ref[base + distance : base + distance + ny, :]
            beside = beside + pad_ref[base - distance : base - distance + ny, :]
            for index in (plane - distance, plane + distance):
                if 0 <= index < planes:
                    beside = beside + y_ref[index * ny : (index + 1) * ny, :]
            lap = lap + weights[distance] * beside
        if first:
            value = scale * (-filter_center * own - 0.5 * lap)
        else:
            value = scale * ((v_ref[rows, :] - filter_center) * own - 0.5 * lap)
            value = value - prev_ref[rows, :]
        part_ref[rows, :] = value


def couple_kernel(dims, first, *refs):
    n, cap, nproj, foot, chunk = dims
    if first:
        off_ref, atom_ref, got_ref, part_ref, p_ref, out_ref, w_ref = refs
    else:
        off_ref, got_ref, part_ref, p_ref, w_ref, out_ref = refs
    lanes = n * chunk
    if first:
        atoms = by_owner(got_ref[:, 1, :], n, chunk)
        row = iota((chunk, 128), 0)
        column = iota((chunk, 128), 1)
        count = 128 // (nproj // 2)
        parity = (iota((chunk, 2 * nproj), 1) // nproj) == (iota((chunk, 2 * nproj), 0) % 2)
        spread = iota((2 * nproj, lanes), 1) % nproj == iota((2 * nproj, lanes), 0) % nproj
        spread = spread.astype(f32)
        row_wide = iota((chunk, lanes), 0) // nproj
        for owner in range(n):
            mine = jnp.zeros((chunk, 128), jnp.int32)
            mine_wide = jnp.zeros((chunk, lanes), f32)
            for k in range(cap):
                atom = atom_ref[k, owner]
                mine = jnp.where(row // nproj == k, atom, mine)
                mine_wide = jnp.where(row_wide == k, atom.astype(f32), mine_wide)
            pick = (column == (row % nproj) // 2 * count + mine) & (mine >= 0)
            entries = lax.dot_general(
                pick.astype(f32),
                got_ref[owner, 8:, 0:128],
                (((1,), (1,)), ((), ())),
                precision=highest,
                preferred_element_type=f32,
            )
            entries = jnp.where(parity, entries, 0.0)
            block = jnp.dot(entries, spread, precision=highest, preferred_element_type=f32)
            same = (atoms[owner : owner + 1, :] == mine_wide) & (mine_wide >= 0.0)
            w_ref[pl.ds(owner * chunk, chunk), :] = jnp.where(same, block, 0.0)
        coefficients = by_owner(got_ref[:, 0, :], n, chunk)
    else:
        coefficients = by_owner(got_ref[...], n, chunk)
    scale = (1.0 if first else 2.0) / filter_half_width
    out_ref[...] = part_ref[...]
    sublane = iota((foot, 128), 0)
    for slot in range(n * cap):
        owner = slot // cap
        rows = slice(slot * nproj, (slot + 1) * nproj)
        returned = jnp.sum(
            w_ref[rows, :] * coefficients[owner : owner + 1, :], axis=1, keepdims=True
        )
        returned = jnp.broadcast_to(returned * scale, (nproj, 128))
        contrib = jnp.zeros((foot, 128), f32)
        for tile in range(foot):
            term = jnp.sum(
                p_ref[rows, tile * 128 : (tile + 1) * 128] * returned, axis=0, keepdims=True
            )
            contrib = jnp.where(sublane == tile, term, contrib)
        start = off_ref[slot % cap, slot // cap]
        out_ref[pl.ds(start, foot), :] = out_ref[pl.ds(start, foot), :] + contrib


def step_kernel(dims, nband, first, last, *refs):
    n, cap, nproj, foot, chunk = dims
    refs = list(refs)
    take = lambda: refs.pop(0)
    info_ref, part_ref, a_ref, b_ref = take(), take(), take(), take()
    if first:
        y_ref = take()
        v_pieces = [take() for _ in range(nband)]
    if not last:
        off_ref, p_ref = take(), take()
    out_ref = take()
    if not last:
        c_ref = take()
    if first:
        v_ref = take()
    lo_ref, hi_ref = take(), take()
    cells = part_ref.shape[0]
    ny = 32
    planes = cells // ny
    lanes = n * chunk
    weights = stencil_weights
    if first and nband > 1:
        piece_rows = ny // nband
        for back, piece in enumerate(v_pieces):
            at = lax.rem(info_ref[1] - back + nband, nband) * piece_rows
            for plane in range(planes):
                spot = pl.multiple_of(plane * ny + at, 8)
                v_ref[pl.ds(spot, piece_rows), :] = piece[
                    plane * piece_rows : (plane + 1) * piece_rows, :
                ]
    elif first:
        v_ref[...] = v_pieces[0][...]
    odd = jnp.full((cells, 128), info_ref[0], jnp.int32) == 1
    from_a, from_b = a_ref[...], b_ref[...]
    lo_ref[...] = jnp.where(odd, from_a, from_b)
    hi_ref[...] = jnp.where(odd, from_b, from_a)
    scale = (1.0 if first else 2.0) / filter_half_width
    for plane in range(planes):
        rows = slice(plane * ny, (plane + 1) * ny)
        value = part_ref[rows, :]
        for distance in range(1, reach + 1):
            for index in (plane - distance, plane + distance):
                if index < 0:
                    beside = lo_ref[(index + planes) * ny : (index + planes + 1) * ny, :]
                elif index >= planes:
                    beside = hi_ref[(index - planes) * ny : (index - planes + 1) * ny, :]
                else:
                    continue
                value = value + (-0.5 * scale * weights[distance]) * beside
        if first:
            value = value + (scale * v_ref[rows, :]) * y_ref[rows, :]
        out_ref[rows, :] = value
    if not last:
        r_ref = take()
        c_ref[...] = jnp.broadcast_to(
            partials(out_ref, p_ref, off_ref, r_ref, dims)[0:1], (n, lanes)
        )


def beside_slabs(y, n):
    pairs = [(i, i ^ 1) for i in range(n) if i ^ 1 < n]
    cross = [(i, i + 1) for i in range(1, n - 1, 2)] + [(i + 1, i) for i in range(1, n - 1, 2)]
    return lax.ppermute(y, "domain", pairs), lax.ppermute(y, "domain", cross)


def shards(psi, potential, projectors, offsets, intersection, dmat):
    n = lax.axis_size("domain")
    nband = lax.axis_size("band")
    cap, nproj = projectors.shape[2], projectors.shape[3]
    foot = projectors.shape[4] // 128
    chunk = cap * nproj
    lanes = n * chunk
    dims = (n, cap, nproj, foot, chunk)
    cells = psi.shape[1] * psi.shape[2]
    y = psi.reshape(cells, 128)
    p = projectors.reshape(lanes, foot * 128)
    off = offsets[0].T
    atom = intersection[0].T
    couplings = dmat.transpose(1, 2, 0).reshape(nproj * nproj, dmat.shape[0])
    info = jnp.stack([lax.axis_index("domain") % 2, lax.axis_index("band")]).astype(jnp.int32)
    v_piece = potential.reshape(-1, 128)
    params = pltpu.CompilerParams(vmem_limit_bytes=40 * 1024 * 1024)
    y_shape = jax.ShapeDtypeStruct((cells, 128), f32)
    c_shape = jax.ShapeDtypeStruct((n, lanes), f32)
    row_scratch = pltpu.VMEM((lanes, 128), f32)

    def call(kernel, name, outs, ins, scratch=(), flops=40, smem=()):
        return pl.pallas_call(
            kernel,
            out_shape=outs,
            in_specs=[SMEM if index in smem else VMEM for index in range(len(ins))],
            out_specs=(VMEM,) * len(outs),
            scratch_shapes=scratch,
            compiler_params=params,
            cost_estimate=pl.CostEstimate(
                flops=flops * cells * 128, bytes_accessed=16 * cells * 128, transcendentals=0
            ),
            name=name,
        )(*ins)

    sources = (y, p, off, atom, couplings, v_piece)
    sources = [pltpu.with_memory_space_constraint(x, pltpu.HBM) for x in sources]
    payload, y, p, v_piece = pl.pallas_call(
        functools.partial(start_kernel, dims),
        out_shape=(
            jax.ShapeDtypeStruct((n, 24, lanes), f32),
            y_shape,
            jax.ShapeDtypeStruct(p.shape, f32),
            jax.ShapeDtypeStruct(v_piece.shape, f32),
        ),
        in_specs=[pl.BlockSpec(memory_space=pltpu.HBM)] * 6,
        out_specs=(VMEM,) * 4,
        scratch_shapes=[
            pltpu.SMEM(off.shape, jnp.int32),
            pltpu.SMEM(off.shape, jnp.int32),
            pltpu.VMEM(couplings.shape, f32),
            row_scratch,
            pltpu.SemaphoreType.DMA((6,)),
        ],
        compiler_params=params,
        name="first_partials",
    )(*sources)
    got = lax.all_to_all(payload, "domain", split_axis=0, concat_axis=0, tiled=True)
    if potential.shape[1] % 8 == 0 and nband <= 8:
        pieces = [v_piece]
        for back in range(1, nband):
            ring = [(i, (i + back) % nband) for i in range(nband)]
            pieces.append(lax.ppermute(v_piece, "band", ring))
    else:
        whole = v_piece.reshape(potential.shape)
        pieces = [lax.all_gather(whole, "band", axis=1, tiled=True).reshape(cells, 128)]

    slabs = [pltpu.VMEM((cells, 128), f32)] * 2
    padded = [pltpu.VMEM((cells // 32 * 48, 128), f32)]
    v = w = previous = None
    for degree in range(DEGREE):
        first, last = degree == 0, degree == DEGREE - 1
        if not first:
            got = lax.all_to_all(c, "domain", split_axis=0, concat_axis=0, tiled=True)
        from_a, from_b = beside_slabs(y, n)
        ins = (y,) if first else (y, v, previous)
        (part,) = call(functools.partial(local_kernel, first), "local", (y_shape,), ins, padded)
        couple = functools.partial(couple_kernel, dims, first)
        if first:
            outs = (y_shape, jax.ShapeDtypeStruct((lanes, lanes), f32))
            ins = (off, atom, got, part, p)
            part, w = call(couple, "first_couple", outs, ins, flops=BIG, smem=(0, 1))
        else:
            (part,) = call(couple, "couple", (y_shape,), (off, got, part, p, w), flops=BIG, smem=(0,))
        ins = (info, part, from_a, from_b)
        outs = (y_shape,)
        smem = (0,)
        if first:
            ins += (y, *pieces)
        if not last:
            smem += (len(ins),)
            ins += (off, p)
            outs += (c_shape,)
        if first:
            outs += (y_shape,)
        step = functools.partial(step_kernel, dims, len(pieces), first, last)
        scratch = slabs if last else slabs + [row_scratch]
        out = call(step, "last_step" if last else "step", outs, ins, scratch, smem=smem)
        previous, y = y, out[0]
        if not last:
            c = out[1]
        if first:
            v = out[2]
    return y.reshape(psi.shape)


def solution(mesh):
    return jax.shard_map(
        shards,
        mesh=mesh,
        in_specs=(
            P("band", "domain", None, None),
            P("domain", "band", None),
            P("domain", None, None, None, None),
            P("domain", None, None),
            P("domain", None, None),
            P("domain", None, None),
        ),
        out_specs=P("band", "domain", None, None),
        check_vma=False,
    )
```

time: 60.5 us -> 61.3 us (1.013)
  the two profiles are of different devices: /device:TPU:0 before, /device:TPU:11 now
where the time goes in v2:
time: 61.3 us; the launch traced here: 60.9 us
  starting transfers between devices  35.1 us (57%)
  Pallas kernels  13.5 us (22%)
  waiting for transfers between devices  12 us (20%)
    ppermute x8, starting transfers between devices, beside_slabs(): return (lax.ppermute(y, 'domain', pairs), lax.ppermute(y, 'domain', cross))  14.8 us
    all_to_all x3, starting transfers between devices, shards(): got = lax.all_to_all(c, 'domain', split_axis=0, concat_axis=0, tiled=True)  11.6 us
    pallas_call x12, Pallas kernels, call(): pl.pallas_call(kernel, out_shape=outs, in_specs=[SMEM if index in smem el...  11.5 us
    ppermute x8, waiting for transfers between devices, beside_slabs(): return (lax.ppermute(y, 'domain', pairs), lax.ppermute(y, 'domain', cross))  8.9 us
    ppermute x3, starting transfers between devices, shards(): pieces.append(lax.ppermute(v_piece, 'band', ring))  4.73 us
    all_to_all x1, starting transfers between devices, shards(): lax.all_to_all(payload, 'domain', split_axis=0, concat_axis=0, tiled=True)  3.94 us
    all_to_all x1, waiting for transfers between devices, shards(): lax.all_to_all(payload, 'domain', split_axis=0, concat_axis=0, tiled=True)  3.04 us
    pallas_call x1, Pallas kernels, shards(): pl.pallas_call(functools.partial(start_kernel, dims), out_shape=(jax.Shap...  2.05 us
  transfers between devices with their start and end apart: 15, of which 4 were waited for; matrix products, arithmetic and copies ran while one was open for 0% of the time, Pallas kernels for 10%

profile of v2, /device:TPU:11, one launch (start us, length us, event | category | flops | bytes accessed | tf_op | source)
XLA Modules:
  0.0 60.9 jit_solution(13400758459749713043)
XLA Ops:
  0.0 2.1 %first_partials.1 = (f32[8,24,128]{2,1,0:T(8,128)}, f32[192,128]{1,0:T(8,128)S(1)}, f32[128,1024]{1,0:T(8,128)S(1)}, f32[48,128]{1,0:T(8,128)S(1)}) custom-call(f32[192,128]{1,0:T(8,128)} %bitcast.41, f32[128,1024]{1,0:T(8,128)} %bitcast.40, s32[2,8]{1,0:T(2,128)} %bitcast.27, s32[2,8]{1,0:T(2,128)} %bitcast.38, f32[64,32]{1,0:T(8,128)} %bitcast.42, ...), custom_call_target="tpu_custom_call" | custom-call | tf_op jit(solution)/shard_map/first_partials/pallas_call | solution.py:302
  2.3 2.3 %collective-permute-start.3 = (f32[48,128]{1,0:T(8,128)S(1)}, f32[48,128]{1,0:T(8,128)S(1)}, u32[]{:S(2)}, u32[]{:S(2)}) collective-permute-start(f32[48,128]{1,0:T(8,128)S(1)} %get-tuple-element.22.refs_5_), channel_id=1, source_target_pairs={{0,2},{1,3},{2,0},{3,1},{4,6},{5,7},{6,4},{7,5},{8,10},{9,11},{10,... | collective-permute-start | bytes 73736 | tf_op jit(solution)/shard_map/ppermute | solution.py:327
  4.6 2.2 %collective-permute-start.2 = (f32[48,128]{1,0:T(8,128)S(1)}, f32[48,128]{1,0:T(8,128)S(1)}, u32[]{:S(2)}, u32[]{:S(2)}) collective-permute-start(f32[48,128]{1,0:T(8,128)S(1)} %get-tuple-element.22.refs_5_), channel_id=1, source_target_pairs={{0,1},{1,2},{2,3},{3,0},{4,5},{5,6},{6,7},{7,4},{8,9},{9,10},{10,1... | collective-permute-start | bytes 73736 | tf_op jit(solution)/shard_map/ppermute | solution.py:327
  6.8 4.5 %collective-permute-start.1 = (f32[192,128]{1,0:T(8,128)S(1)}, f32[192,128]{1,0:T(8,128)S(1)}, u32[]{:S(2)}, u32[]{:S(2)}) collective-permute-start(f32[192,128]{1,0:T(8,128)S(1)} %get-tuple-element.19.refs_0_.refs_4_.refs_2_), channel_id=1, source_target_pairs={{4,8},{12,16},{20,24},{8,4},{16,12},{24,20},{5,9},{13,17},{21,25},... | collective-permute-start | bytes 294920 | tf_op jit(solution)/shard_map/ppermute | solution.py:262
  11.4 3.9 %all-to-all-start = ((f32[8,24,128]{2,1,0:T(8,128)}), f32[8,24,128]{2,1,0:T(8,128)S(1)}, u32[]{:S(2)}, u32[]{:S(2)}) async-start(f32[8,24,128]{2,1,0:T(8,128)} %get-tuple-element.18), calls=%async_computation | async-start | bytes 196608 | tf_op jit(solution)/shard_map/all_to_all | solution.py:322
  15.7 3.0 %all-to-all-done.refs_2_ = f32[8,24,128]{2,1,0:T(8,128)S(1)} async-done(((f32[8,24,128]{2,1,0:T(8,128)}), f32[8,24,128]{2,1,0:T(8,128)S(1)}, u32[]{:S(2)}, u32[]{:S(2)}) %all-to-all-start) | async-done | bytes 98336 | tf_op jit(solution)/shard_map/all_to_all | solution.py:322
  18.8 2.1 %first_couple.1 = (f32[192,128]{1,0:T(8,128)S(1)}, f32[128,128]{1,0:T(8,128)S(1)}) custom-call(s32[2,8]{1,0:T(2,128)S(1)} %bitcast.28, s32[2,8]{1,0:T(2,128)S(1)} %bitcast.39, f32[8,24,128]{2,1,0:T(8,128)S(1)} %all-to-all-done.refs_2_, f32[192,128]{1,0:T(8,128)S(1)} %local.4.refs_3_, f32[128,1024]{1,0:T(8,128)S(1)} %get-tuple-element.20.refs_4_.refs_10_.refs_3_.refs_5_), custom_call_target="tpu_custom_call" | custom-call | flops 2457600000 | bytes 393216 | tf_op jit(solution)/shard_map/first_couple/pallas_call | solution.py:287
  21.0 1.5 %step.3 = (f32[192,128]{1,0:T(8,128)S(1)}, f32[8,128]{1,0:T(8,128)}, f32[192,128]{1,0:T(8,128)S(1)}) custom-call(s32[2]{0:T(128)S(1)} %pad_add_fusion.refs_0_, f32[192,128]{1,0:T(8,128)S(1)} %get-tuple-element.21.refs_1_, f32[192,128]{1,0:T(8,128)S(1)} %collective-permute-done.refs_2_, f32[192,128]{1,0:T(8,128)S(1)} %collective-permute-done.1.refs_3_, ...), custom_call_target="tpu_custom_call" | custom-call | flops 983040 | bytes 393216 | tf_op jit(solution)/shard_map/step/pallas_call | solution.py:287
  22.5 5.0 %all-to-all-start.1 = ((f32[8,1,128]{2,1,0:T(1,128)}), f32[8,1,128]{2,1,0:T(1,128)S(1)}, u32[]{:S(2)}, u32[]{:S(2)}) async-start(f32[8,1,128]{2,1,0:T(1,128)} %bitcast.14), calls=%async_computation.1 | async-start | bytes 8192 | tf_op jit(solution)/shard_map/all_to_all | solution.py:338
  27.4 3.3 %collective-permute-start.6 = (f32[192,128]{1,0:T(8,128)S(1)}, f32[192,128]{1,0:T(8,128)S(1)}, u32[]{:S(2)}, u32[]{:S(2)}) collective-permute-start(f32[192,128]{1,0:T(8,128)S(1)} %get-tuple-element.24.refs_0_.refs_2_), channel_id=1, source_target_pairs={{4,8},{12,16},{20,24},{8,4},{16,12},{24,20},{5,9},{13,17},{21,25},... | collective-permute-start | bytes 294920 | tf_op jit(solution)/shard_map/ppermute | solution.py:262
  30.9 0.3 local.5.refs_2_
  31.2 0.9 %couple.3.refs_1_ = f32[192,128]{1,0:T(8,128)S(1)} custom-call(s32[2,8]{1,0:T(2,128)S(1)} %bitcast.30, f32[8,128]{1,0:T(8,128)S(1)} %bitcast.36, f32[192,128]{1,0:T(8,128)S(1)} %local.5.refs_2_, f32[128,1024]{1,0:T(8,128)S(1)} %get-tuple-element.20.refs_4_.refs_10_.refs_3_.refs_5_, f32[128,128]{1,0:T(8,128)S(1)} %get-tuple-element.26.refs_4_), custom_call_target="tpu_custom_call" | custom-call | flops 2457600000 | bytes 393216 | tf_op jit(solution)/shard_map/couple/pallas_call | solution.py:287
  32.1 3.0 %collective-permute-done.6.refs_3_ = f32[192,128]{1,0:T(8,128)S(1)} collective-permute-done((f32[192,128]{1,0:T(8,128)S(1)}, f32[192,128]{1,0:T(8,128)S(1)}, u32[]{:S(2)}, u32[]{:S(2)}) %collective-permute-start.6) | collective-permute-done | bytes 98336 | tf_op jit(solution)/shard_map/ppermute | solution.py:262
  35.0 1.4 %step.4 = (f32[192,128]{1,0:T(8,128)S(1)}, f32[8,128]{1,0:T(8,128)}) custom-call(s32[2]{0:T(128)S(1)} %pad_add_fusion.refs_0_, f32[192,128]{1,0:T(8,128)S(1)} %couple.3.refs_1_, f32[192,128]{1,0:T(8,128)S(1)} %collective-permute-done.5.refs_2_, f32[192,128]{1,0:T(8,128)S(1)} %collective-permute-done.6.refs_3_, s32[2,8]{1,0:T(2,128)S(1)} %bitcast.31, ...), custom_call_target="tpu_custom_call" | custom-call | flops 983040 | bytes 393216 | tf_op jit(solution)/shard_map/step/pallas_call | solution.py:287
  36.5 3.3 %all-to-all-start.2 = ((f32[8,1,128]{2,1,0:T(1,128)}), f32[8,1,128]{2,1,0:T(1,128)S(1)}, u32[]{:S(2)}, u32[]{:S(2)}) async-start(f32[8,1,128]{2,1,0:T(1,128)} %bitcast.17), calls=%async_computation.2 | async-start | bytes 8192 | tf_op jit(solution)/shard_map/all_to_all | solution.py:338
  39.8 3.3 %collective-permute-start.8 = (f32[192,128]{1,0:T(8,128)S(1)}, f32[192,128]{1,0:T(8,128)S(1)}, u32[]{:S(2)}, u32[]{:S(2)}) collective-permute-start(f32[192,128]{1,0:T(8,128)S(1)} %get-tuple-element.28.refs_0_.refs_2_), channel_id=1, source_target_pairs={{4,8},{12,16},{20,24},{8,4},{16,12},{24,20},{5,9},{13,17},{21,25},... | collective-permute-start | bytes 294920 | tf_op jit(solution)/shard_map/ppermute | solution.py:262
  43.5 0.9 %couple.4.refs_1_ = f32[192,128]{1,0:T(8,128)S(1)} custom-call(s32[2,8]{1,0:T(2,128)S(1)} %bitcast.32, f32[8,128]{1,0:T(8,128)S(1)} %bitcast.37, f32[192,128]{1,0:T(8,128)S(1)} %local.6.refs_2_, f32[128,1024]{1,0:T(8,128)S(1)} %get-tuple-element.20.refs_4_.refs_10_.refs_3_.refs_5_, f32[128,128]{1,0:T(8,128)S(1)} %get-tuple-element.26.refs_4_), custom_call_target="tpu_custom_call" | custom-call | flops 2457600000 | bytes 393216 | tf_op jit(solution)/shard_map/couple/pallas_call | solution.py:287
  44.4 3.0 %collective-permute-done.8.refs_3_ = f32[192,128]{1,0:T(8,128)S(1)} collective-permute-done((f32[192,128]{1,0:T(8,128)S(1)}, f32[192,128]{1,0:T(8,128)S(1)}, u32[]{:S(2)}, u32[]{:S(2)}) %collective-permute-start.8) | collective-permute-done | bytes 98336 | tf_op jit(solution)/shard_map/ppermute | solution.py:262
  47.3 1.4 %step.5 = (f32[192,128]{1,0:T(8,128)S(1)}, f32[8,128]{1,0:T(8,128)}) custom-call(s32[2]{0:T(128)S(1)} %pad_add_fusion.refs_0_, f32[192,128]{1,0:T(8,128)S(1)} %couple.4.refs_1_, f32[192,128]{1,0:T(8,128)S(1)} %collective-permute-done.7.refs_2_, f32[192,128]{1,0:T(8,128)S(1)} %collective-permute-done.8.refs_3_, s32[2,8]{1,0:T(2,128)S(1)} %bitcast.33, ...), custom_call_target="tpu_custom_call" | custom-call | flops 983040 | bytes 393216 | tf_op jit(solution)/shard_map/step/pallas_call | solution.py:287
  48.8 3.3 %all-to-all-start.3 = ((f32[8,1,128]{2,1,0:T(1,128)}), f32[8,1,128]{2,1,0:T(1,128)S(1)}, u32[]{:S(2)}, u32[]{:S(2)}) async-start(f32[8,1,128]{2,1,0:T(1,128)} %bitcast.20), calls=%async_computation.3 | async-start | bytes 8192 | tf_op jit(solution)/shard_map/all_to_all | solution.py:338
  52.1 3.3 %collective-permute-start.10 = (f32[192,128]{1,0:T(8,128)S(1)}, f32[192,128]{1,0:T(8,128)S(1)}, u32[]{:S(2)}, u32[]{:S(2)}) collective-permute-start(f32[192,128]{1,0:T(8,128)S(1)} %get-tuple-element.30.refs_0_), channel_id=1, source_target_pairs={{4,8},{12,16},{20,24},{8,4},{16,12},{24,20},{5,9},{13,17},{21,25},... | collective-permute-start | bytes 294920 | tf_op jit(solution)/shard_map/ppermute | solution.py:262
  55.8 0.9 %couple.5.refs_1_ = f32[192,128]{1,0:T(8,128)S(1)} custom-call(s32[2,8]{1,0:T(2,128)S(1)} %bitcast.34, f32[8,128]{1,0:T(8,128)S(1)} %bitcast.35, f32[192,128]{1,0:T(8,128)S(1)} %local.7.refs_2_, f32[128,1024]{1,0:T(8,128)S(1)} %get-tuple-element.20.refs_4_.refs_10_.refs_3_.refs_5_, f32[128,128]{1,0:T(8,128)S(1)} %get-tuple-element.26.refs_4_), custom_call_target="tpu_custom_call" | custom-call | flops 2457600000 | bytes 393216 | tf_op jit(solution)/shard_map/couple/pallas_call | solution.py:287
  56.7 3.0 %collective-permute-done.10.refs_3_ = f32[192,128]{1,0:T(8,128)S(1)} collective-permute-done((f32[192,128]{1,0:T(8,128)S(1)}, f32[192,128]{1,0:T(8,128)S(1)}, u32[]{:S(2)}, u32[]{:S(2)}) %collective-permute-start.10) | collective-permute-done | bytes 98336 | tf_op jit(solution)/shard_map/ppermute | solution.py:262
  59.6 1.2 %last_step.1 = f32[192,128]{1,0:T(8,128)} custom-call(s32[2]{0:T(128)S(1)} %pad_add_fusion.refs_0_, f32[192,128]{1,0:T(8,128)S(1)} %couple.5.refs_1_, f32[192,128]{1,0:T(8,128)S(1)} %collective-permute-done.9.refs_2_, f32[192,128]{1,0:T(8,128)S(1)} %collective-permute-done.10.refs_3_), custom_call_target="tpu_custom_call" | custom-call | flops 983040 | bytes 393216 | tf_op jit(solution)/shard_map/last_step/pallas_call | solution.py:287
  (24 shorter events, 1.5 us)
Async XLA Ops:
  2.1 18.9 %collective-permute-start.4 = (f32[48,128]{1,0:T(8,128)S(1)}, f32[48,128]{1,0:T(8,128)S(1)}, u32[]{:S(2)}, u32[]{:S(2)}) collective-permute-start(f32[48,128]{1,0:T(8,128)S(1)} %get-tuple-element.22.refs_5_), channel_id=1, source_target_pairs={{0,3},{1,0},{2,1},{3,2},{4,7},{5,4},{6,5},{7,6},{8,11},{9,8},{10,9... | collective-permute-start | bytes 73736 | tf_op jit(solution)/shard_map/ppermute | solution.py:327
  2.3 18.7 %collective-permute-start.3 = (f32[48,128]{1,0:T(8,128)S(1)}, f32[48,128]{1,0:T(8,128)S(1)}, u32[]{:S(2)}, u32[]{:S(2)}) collective-permute-start(f32[48,128]{1,0:T(8,128)S(1)} %get-tuple-element.22.refs_5_), channel_id=1, source_target_pairs={{0,2},{1,3},{2,0},{3,1},{4,6},{5,7},{6,4},{7,5},{8,10},{9,11},{10,... | collective-permute-start | bytes 73736 | tf_op jit(solution)/shard_map/ppermute | solution.py:327
  4.6 16.4 %collective-permute-start.2 = (f32[48,128]{1,0:T(8,128)S(1)}, f32[48,128]{1,0:T(8,128)S(1)}, u32[]{:S(2)}, u32[]{:S(2)}) collective-permute-start(f32[48,128]{1,0:T(8,128)S(1)} %get-tuple-element.22.refs_5_), channel_id=1, source_target_pairs={{0,1},{1,2},{2,3},{3,0},{4,5},{5,6},{6,7},{7,4},{8,9},{9,10},{10,1... | collective-permute-start | bytes 73736 | tf_op jit(solution)/shard_map/ppermute | solution.py:327
  6.8 14.2 %collective-permute-start.1 = (f32[192,128]{1,0:T(8,128)S(1)}, f32[192,128]{1,0:T(8,128)S(1)}, u32[]{:S(2)}, u32[]{:S(2)}) collective-permute-start(f32[192,128]{1,0:T(8,128)S(1)} %get-tuple-element.19.refs_0_.refs_4_.refs_2_), channel_id=1, source_target_pairs={{4,8},{12,16},{20,24},{8,4},{16,12},{24,20},{5,9},{13,17},{21,25},... | collective-permute-start | bytes 294920 | tf_op jit(solution)/shard_map/ppermute | solution.py:262
  11.3 9.7 %collective-permute-start = (f32[192,128]{1,0:T(8,128)S(1)}, f32[192,128]{1,0:T(8,128)S(1)}, u32[]{:S(2)}, u32[]{:S(2)}) collective-permute-start(f32[192,128]{1,0:T(8,128)S(1)} %get-tuple-element.19.refs_0_.refs_4_.refs_2_), channel_id=1, source_target_pairs={{0,4},{4,0},{8,12},{12,8},{16,20},{20,16},{24,28},{28,24},{1,5},{5... | collective-permute-start | bytes 294920 | tf_op jit(solution)/shard_map/ppermute | solution.py:262
  11.4 7.4 %all-to-all-start = ((f32[8,24,128]{2,1,0:T(8,128)}), f32[8,24,128]{2,1,0:T(8,128)S(1)}, u32[]{:S(2)}, u32[]{:S(2)}) async-start(f32[8,24,128]{2,1,0:T(8,128)} %get-tuple-element.18), calls=%async_computation | async-start | bytes 196608 | tf_op jit(solution)/shard_map/all_to_all | solution.py:322
  15.6 3.1 %copy-start.1 = (s32[1,8,2]{1,2,0:T(2,128)S(1)}, s32[1,8,2]{1,2,0:T(2,128)}, u32[]{:S(2)}) copy-start(s32[1,8,2]{1,2,0:T(2,128)} %param.10) | copy-start | bytes 196
  15.7 3.1 %copy-start = (s32[1,8,2]{1,2,0:T(2,128)S(1)}, s32[1,8,2]{1,2,0:T(2,128)}, u32[]{:S(2)}) copy-start(s32[1,8,2]{1,2,0:T(2,128)} %param.9) | copy-start | bytes 196
  22.5 8.7 %all-to-all-start.1 = ((f32[8,1,128]{2,1,0:T(1,128)}), f32[8,1,128]{2,1,0:T(1,128)S(1)}, u32[]{:S(2)}, u32[]{:S(2)}) async-start(f32[8,1,128]{2,1,0:T(1,128)} %bitcast.14), calls=%async_computation.1 | async-start | bytes 8192 | tf_op jit(solution)/shard_map/all_to_all | solution.py:338
  27.4 7.6 %collective-permute-start.6 = (f32[192,128]{1,0:T(8,128)S(1)}, f32[192,128]{1,0:T(8,128)S(1)}, u32[]{:S(2)}, u32[]{:S(2)}) collective-permute-start(f32[192,128]{1,0:T(8,128)S(1)} %get-tuple-element.24.refs_0_.refs_2_), channel_id=1, source_target_pairs={{4,8},{12,16},{20,24},{8,4},{16,12},{24,20},{5,9},{13,17},{21,25},... | collective-permute-start | bytes 294920 | tf_op jit(solution)/shard_map/ppermute | solution.py:262
  30.8 4.2 %collective-permute-start.5 = (f32[192,128]{1,0:T(8,128)S(1)}, f32[192,128]{1,0:T(8,128)S(1)}, u32[]{:S(2)}, u32[]{:S(2)}) collective-permute-start(f32[192,128]{1,0:T(8,128)S(1)} %get-tuple-element.24.refs_0_.refs_2_), channel_id=1, source_target_pairs={{0,4},{4,0},{8,12},{12,8},{16,20},{20,16},{24,28},{28,24},{1,5},{5... | collective-permute-start | bytes 294920 | tf_op jit(solution)/shard_map/ppermute | solution.py:262
  36.5 7.0 %all-to-all-start.2 = ((f32[8,1,128]{2,1,0:T(1,128)}), f32[8,1,128]{2,1,0:T(1,128)S(1)}, u32[]{:S(2)}, u32[]{:S(2)}) async-start(f32[8,1,128]{2,1,0:T(1,128)} %bitcast.17), calls=%async_computation.2 | async-start | bytes 8192 | tf_op jit(solution)/shard_map/all_to_all | solution.py:338
  39.8 7.5 %collective-permute-start.8 = (f32[192,128]{1,0:T(8,128)S(1)}, f32[192,128]{1,0:T(8,128)S(1)}, u32[]{:S(2)}, u32[]{:S(2)}) collective-permute-start(f32[192,128]{1,0:T(8,128)S(1)} %get-tuple-element.28.refs_0_.refs_2_), channel_id=1, source_target_pairs={{4,8},{12,16},{20,24},{8,4},{16,12},{24,20},{5,9},{13,17},{21,25},... | collective-permute-start | bytes 294920 | tf_op jit(solution)/shard_map/ppermute | solution.py:262
  43.1 4.2 %collective-permute-start.7 = (f32[192,128]{1,0:T(8,128)S(1)}, f32[192,128]{1,0:T(8,128)S(1)}, u32[]{:S(2)}, u32[]{:S(2)}) collective-permute-start(f32[192,128]{1,0:T(8,128)S(1)} %get-tuple-element.28.refs_0_.refs_2_), channel_id=1, source_target_pairs={{0,4},{4,0},{8,12},{12,8},{16,20},{20,16},{24,28},{28,24},{1,5},{5... | collective-permute-start | bytes 294920 | tf_op jit(solution)/shard_map/ppermute | solution.py:262
  48.8 7.0 %all-to-all-start.3 = ((f32[8,1,128]{2,1,0:T(1,128)}), f32[8,1,128]{2,1,0:T(1,128)S(1)}, u32[]{:S(2)}, u32[]{:S(2)}) async-start(f32[8,1,128]{2,1,0:T(1,128)} %bitcast.20), calls=%async_computation.3 | async-start | bytes 8192 | tf_op jit(solution)/shard_map/all_to_all | solution.py:338
  52.1 7.5 %collective-permute-start.10 = (f32[192,128]{1,0:T(8,128)S(1)}, f32[192,128]{1,0:T(8,128)S(1)}, u32[]{:S(2)}, u32[]{:S(2)}) collective-permute-start(f32[192,128]{1,0:T(8,128)S(1)} %get-tuple-element.30.refs_0_), channel_id=1, source_target_pairs={{4,8},{12,16},{20,24},{8,4},{16,12},{24,20},{5,9},{13,17},{21,25},... | collective-permute-start | bytes 294920 | tf_op jit(solution)/shard_map/ppermute | solution.py:262
  55.4 4.2 %collective-permute-start.9 = (f32[192,128]{1,0:T(8,128)S(1)}, f32[192,128]{1,0:T(8,128)S(1)}, u32[]{:S(2)}, u32[]{:S(2)}) collective-permute-start(f32[192,128]{1,0:T(8,128)S(1)} %get-tuple-element.30.refs_0_), channel_id=1, source_target_pairs={{0,4},{4,0},{8,12},{12,8},{16,20},{20,16},{24,28},{28,24},{1,5},{5... | collective-permute-start | bytes 294920 | tf_op jit(solution)/shard_map/ppermute | solution.py:262

commit v3 on v1

--- a/solution.py
+++ b/solution.py
@@ -2,6 +2,7 @@
 
 import jax
 import jax.numpy as jnp
+import numpy as np
 from jax import lax
 from jax.experimental import pallas as pl
 from jax.experimental.pallas import tpu as pltpu
@@ -225,7 +226,7 @@
     return lax.ppermute(y, "domain", pairs), lax.ppermute(y, "domain", cross)
 
 
-def shards(psi, potential, projectors, offsets, intersection, dmat):
+def slab_form(psi, potential, projectors, offsets, intersection, dmat):
     n = lax.axis_size("domain")
     nband = lax.axis_size("band")
     cap, nproj = projectors.shape[2], projectors.shape[3]
@@ -300,6 +301,424 @@
     return y.reshape(psi.shape)
 
 
+NY = 32
+SLAB = 6 * NY
+PACK = 2 * SLAB + 24
+
+
+def circulant_z():
+    apart = jnp.abs(iota((128, 128), 0) - iota((128, 128), 1))
+    apart = jnp.minimum(apart, 128 - apart)
+    out = jnp.full((128, 128), 3.0 * stencil_weights[0], f32)
+    out = jnp.where(apart > reach, 0.0, out)
+    for distance in range(1, reach + 1):
+        out = jnp.where(apart == distance, stencil_weights[distance], out)
+    return out
+
+
+def stencil(y_ref, other_ref, v_ref, prev_ref, out_ref, pad_ref, slabs, scale, bases):
+    tall = NY + 16
+    for plane in range(6 * slabs):
+        own = y_ref[plane * NY : (plane + 1) * NY, :]
+        base = plane * tall
+        pad_ref[base + 8 : base + 8 + NY, :] = own
+        pad_ref[base : base + 8, :] = own[NY - 8 :, :]
+        pad_ref[base + 8 + NY : base + tall, :] = own[0:8, :]
+    along_z = jnp.dot(
+        y_ref[0 : slabs * SLAB, :],
+        circulant_z(),
+        precision=highest,
+        preferred_element_type=f32,
+    )
+    below, above = bases()
+    for slab in range(slabs):
+        for plane in range(6):
+            at = (slab * 6 + plane) * NY
+            rows = slice(at, at + NY)
+            base = (slab * 6 + plane) * tall + 8
+            own = y_ref[rows, :]
+            lap = along_z[rows, :]
+            for distance in range(1, reach + 1):
+                beside = pad_ref[base + distance : base + distance + NY, :]
+                beside = beside + pad_ref[base - distance : base - distance + NY, :]
+                for index in (plane - distance, plane + distance):
+                    if index < 0:
+                        spot = pl.multiple_of(below[slab] + (index + 6) * NY, 8)
+                        beside = beside + other_ref[pl.ds(spot, NY), :]
+                    elif index >= 6:
+                        spot = pl.multiple_of(above[slab] + (index - 6) * NY, 8)
+                        beside = beside + other_ref[pl.ds(spot, NY), :]
+                    else:
+                        spot = (slab * 6 + index) * NY
+                        beside = beside + y_ref[spot : spot + NY, :]
+                lap = lap + stencil_weights[distance] * beside
+            value = scale * ((v_ref[rows, :] - filter_center) * own - 0.5 * lap)
+            if prev_ref is not None:
+                value = value - prev_ref[rows, :]
+            out_ref[rows, :] = value
+
+
+def pack_kernel(dims, *refs):
+    n, cap, nproj, foot, chunk = dims
+    lanes = n * chunk
+    sources, pack_ref, scratch = refs[:5], refs[5], refs[6:]
+    p_ref, off_ref, atom_ref, dmat_ref, r_ref, sems = scratch
+    y_ref = pack_ref.at[0:SLAB, :]
+    targets = (y_ref, p_ref, off_ref, atom_ref, dmat_ref)
+    copies = [
+        pltpu.make_async_copy(source, target, sems.at[index])
+        for index, (source, target) in enumerate(zip(sources, targets))
+    ]
+    for copy in copies:
+        copy.start()
+    for copy in copies[2:]:
+        copy.wait()
+    lane = iota((1, lanes), 1) // nproj
+    atoms = jnp.zeros((1, lanes), f32)
+    starts = jnp.zeros((1, lanes), f32)
+    for slot in range(n * cap):
+        here = lane == slot
+        atoms = jnp.where(here, atom_ref[slot % cap, slot // cap].astype(f32), atoms)
+        starts = jnp.where(here, off_ref[slot % cap, slot // cap].astype(f32), starts)
+    small = 2 * SLAB
+    pack_ref[small + 1 : small + 2, :] = atoms
+    pack_ref[small + 2 : small + 3, :] = starts
+    count = dmat_ref.shape[1]
+    for group in range(128 // count):
+        block = dmat_ref[group * 2 * nproj : (group + 1) * 2 * nproj, :]
+        pack_ref[small + 8 :, group * count : (group + 1) * count] = block
+    copies[0].wait()
+    copies[1].wait()
+    pack_ref[small : small + 1, :] = partials(pack_ref, p_ref, off_ref, r_ref, dims)[0:1]
+
+
+def fill_kernel(pack_ref, *refs):
+    pieces, out_ref = refs[:-1], refs[-1]
+    out_ref[0:SLAB, :] = pack_ref[0:SLAB, :]
+    out_ref[2 * SLAB :, :] = pack_ref[2 * SLAB :, :]
+    rows = pieces[0].shape[0]
+    for back, piece in enumerate(pieces):
+        out_ref[SLAB + back * rows : SLAB + (back + 1) * rows, :] = piece[...]
+
+
+def begin_kernel(dims, nband, info_ref, got_ref, part_ref, y_ref, v_ref, w_ref, c_ref, int_ref, other_ref, pad_ref):
+    n, cap, nproj, foot, chunk = dims
+    half = n // 2
+    lanes = n * chunk
+    small = 2 * SLAB
+    piece = NY // nband
+    c_rows, atom_rows, start_rows = [], [], []
+    for local in range(half):
+        mine, theirs = info_ref[local], info_ref[half + local]
+        rows = slice(local * SLAB, (local + 1) * SLAB)
+        y_ref[rows, :] = got_ref[mine, 0:SLAB, :]
+        other_ref[rows, :] = got_ref[theirs, 0:SLAB, :]
+        for back in range(nband):
+            at = lax.rem(info_ref[4 * half] - back + nband, nband) * piece
+            for plane in range(6):
+                spot = pl.multiple_of(local * SLAB + plane * NY + at, 8)
+                source = SLAB + back * 6 * piece + plane * piece
+                v_ref[pl.ds(spot, piece), :] = got_ref[mine, source : source + piece, :]
+    other_ref[half * SLAB :, :] = jnp.zeros((SLAB, 128), f32)
+    for group in (0, half):
+        for local in range(half):
+            slab = info_ref[group + local]
+            c_rows.append(got_ref[slab, small : small + 1, :])
+            atom_rows.append(got_ref[slab, small + 1 : small + 2, :])
+            if group == 0:
+                start_rows.append(got_ref[slab, small + 2 : small + 3, :])
+    c_ref[...] = by_owner(jnp.concatenate(c_rows, 0), n, chunk)
+    atoms = by_owner(jnp.concatenate(atom_rows, 0), n, chunk)
+    lane = iota((1, 128), 1)
+    table = jnp.zeros((1, 128), jnp.int32)
+    for local in range(half):
+        int_ref[local : local + 1, :] = start_rows[local].astype(jnp.int32)
+        for side in range(2):
+            value = info_ref[(2 + side) * half + local]
+            table = jnp.where(lane == side * half + local, value, table)
+    int_ref[half : half + 1, :] = table
+    int_ref[half + 1 :, :] = jnp.zeros((8 - half - 1, 128), jnp.int32)
+
+    def bases():
+        return (
+            [info_ref[2 * half + local] for local in range(half)],
+            [info_ref[3 * half + local] for local in range(half)],
+        )
+
+    stencil(
+        y_ref, other_ref, v_ref, None, part_ref, pad_ref, half, 1.0 / filter_half_width, bases
+    )
+    square = (lanes, 128)
+    diagonal = iota(square, 0) == iota(square, 1)
+    ones = jnp.ones((128, 128), f32)
+    column = iota(square, 1).astype(f32)
+    count = 128 // (nproj // 2)
+    shift = (iota(square, 0) % nproj // 2 * count).astype(f32)
+    wide, picks = [], []
+    for local in range(half):
+        held = jnp.where(diagonal, atom_rows[local], 0.0)
+        mine = jnp.dot(held, ones, precision=highest, preferred_element_type=f32)
+        mine = jnp.round(mine)
+        wide.append(mine)
+        picks.append(jnp.where((column == shift + mine) & (mine >= 0.0), 1.0, 0.0))
+    tall = half * chunk
+    parity = iota((tall, 2 * nproj), 1) // nproj == iota((tall, 2 * nproj), 0) % 2
+    spread = iota((2 * nproj, 128), 1) % nproj == iota((2 * nproj, 128), 0) % nproj
+    spread = jnp.where(spread, 1.0, 0.0)
+    for owner in range(n):
+        rows = slice(owner * chunk, (owner + 1) * chunk)
+        pick = jnp.concatenate([p[rows, :] for p in picks], 0)
+        mine = jnp.concatenate([m[rows, :] for m in wide], 0)
+        entries = lax.dot_general(
+            pick,
+            got_ref[owner, small + 8 :, :],
+            (((1,), (1,)), ((), ())),
+            precision=highest,
+            preferred_element_type=f32,
+        )
+        entries = jnp.where(parity, entries, 0.0)
+        block = jnp.dot(entries, spread, precision=highest, preferred_element_type=f32)
+        same = (atoms[owner : owner + 1, :] == mine) & (mine >= 0.0)
+        w_ref[owner * tall : (owner + 1) * tall, :] = jnp.where(same, block, 0.0)
+
+
+def couple(dims, slabs, half, coefficients, w_ref, p_refs, start_of, out_ref, scale):
+    n, cap, nproj, foot, chunk = dims
+    sublane = iota((foot, 128), 0)
+    for slab in range(slabs):
+        for slot in range(n * cap):
+            owner, k = slot // cap, slot % cap
+            at = (owner * half + slab) * chunk + k * nproj
+            returned = jnp.sum(
+                w_ref[at : at + nproj, :] * coefficients[owner : owner + 1, :],
+                axis=1,
+                keepdims=True,
+            )
+            returned = jnp.broadcast_to(returned * scale, (nproj, 128))
+            contrib = jnp.zeros((foot, 128), f32)
+            rows = slice(slot * nproj, (slot + 1) * nproj)
+            for tile in range(foot):
+                term = jnp.sum(
+                    p_refs[slab][rows, tile * 128 : (tile + 1) * 128] * returned,
+                    axis=0,
+                    keepdims=True,
+                )
+                contrib = jnp.where(sublane == tile, term, contrib)
+            spot = pl.ds(start_of(slab, slot), foot)
+            out_ref[spot, :] = out_ref[spot, :] + contrib
+
+
+def next_partials(dims, half, send_ref, p_refs, start_of, r_ref):
+    n, cap, nproj, foot, chunk = dims
+    lanes = n * chunk
+    for slab in range(half):
+        for slot in range(n * cap):
+            start = start_of(slab, slot)
+            rows = slice(slot * nproj, (slot + 1) * nproj)
+            total = None
+            for tile in range(foot):
+                cells = jnp.broadcast_to(send_ref[pl.ds(start + tile, 1), :], (nproj, 128))
+                term = p_refs[slab][rows, tile * 128 : (tile + 1) * 128] * cells
+                total = term if total is None else total + term
+            r_ref[slab * lanes + slot * nproj : slab * lanes + (slot + 1) * nproj, :] = total
+    row = lax.dot_general(
+        jnp.ones((8, 128), f32),
+        r_ref[...],
+        (((1,), (1,)), ((), ())),
+        precision=highest,
+        preferred_element_type=f32,
+    )
+    for slab in range(half):
+        send_ref[half * SLAB + slab : half * SLAB + slab + 1, :] = row[
+            0:1, slab * lanes : (slab + 1) * lanes
+        ]
+    send_ref[half * SLAB + half :, :] = jnp.zeros((8 - half, 128), f32)
+
+
+def starts_from(int_s, nproj):
+    return lambda slab, slot: slab * SLAB + int_s[slab, slot * nproj]
+
+
+def first_kernel(dims, *refs):
+    n, cap, nproj, foot, chunk = dims
+    half = n // 2
+    int_ref, part_ref, w_ref, c_ref = refs[:4]
+    p_refs, (send_ref, r_ref, int_s, sem) = refs[4 : 4 + half], refs[4 + half :]
+    copy = pltpu.make_async_copy(int_ref, int_s, sem)
+    copy.start()
+    send_ref[0 : half * SLAB, :] = part_ref[...]
+    copy.wait()
+    start_of = starts_from(int_s, nproj)
+    scale = 1.0 / filter_half_width
+    couple(dims, half, half, c_ref[...], w_ref, p_refs, start_of, send_ref, scale)
+    next_partials(dims, half, send_ref, p_refs, start_of, r_ref)
+
+
+def chip_kernel(dims, last, *refs):
+    n, cap, nproj, foot, chunk = dims
+    half = n // 2
+    int_ref, y_ref, got_ref, prev_ref, v_ref, w_ref = refs[:6]
+    p_refs = refs[6 : 6 + half]
+    out_ref, other_ref, pad_ref, int_s, sem = refs[6 + half : 11 + half]
+    copy = pltpu.make_async_copy(int_ref, int_s, sem)
+    copy.start()
+    other_ref[0 : half * SLAB, :] = got_ref[0 : half * SLAB, :]
+    other_ref[half * SLAB :, :] = jnp.zeros((SLAB, 128), f32)
+    slabs = 1 if last else half
+    scale = 2.0 / filter_half_width
+
+    def bases():
+        copy.wait()
+        return (
+            [int_s[half, local] for local in range(half)],
+            [int_s[half, half + local] for local in range(half)],
+        )
+
+    stencil(y_ref, other_ref, v_ref, prev_ref, out_ref, pad_ref, slabs, scale, bases)
+    below = slice(half * SLAB, half * SLAB + half)
+    rows = jnp.concatenate([y_ref[below, :], got_ref[below, :]], 0)
+    coefficients = by_owner(rows, n, chunk)
+    start_of = starts_from(int_s, nproj)
+    couple(dims, slabs, half, coefficients, w_ref, p_refs, start_of, out_ref, scale)
+    if not last:
+        next_partials(dims, half, out_ref, p_refs, start_of, refs[11 + half])
+
+
+def chip_table(n):
+    half = n // 2
+    table = np.zeros((n, 4 * half), np.int32)
+    for device in range(n):
+        chip, core = device // 2, device % 2
+        for local in range(half):
+            there = chip ^ local
+            table[device, local] = 2 * there + core
+            table[device, half + local] = 2 * there + 1 - core
+            same = local * SLAB
+            far = there + (1 if core else -1)
+            cross = (far ^ chip) * SLAB if 0 <= far < half else half * SLAB
+            table[device, 2 * half + local] = same if core else cross
+            table[device, 3 * half + local] = cross if core else same
+    return table
+
+
+def chip_form(psi, potential, projectors, offsets, intersection, dmat):
+    n = lax.axis_size("domain")
+    nband = lax.axis_size("band")
+    cap, nproj = projectors.shape[2], projectors.shape[3]
+    foot = projectors.shape[4] // 128
+    chunk = cap * nproj
+    lanes = n * chunk
+    half = n // 2
+    dims = (n, cap, nproj, foot, chunk)
+    p = projectors.reshape(lanes, foot * 128)
+    v_piece = potential.reshape(-1, 128)
+    couplings = dmat.transpose(1, 2, 0).reshape(nproj * nproj, dmat.shape[0])
+    domain = lax.axis_index("domain")
+    info = jnp.concatenate(
+        [
+            lax.dynamic_slice_in_dim(jnp.asarray(chip_table(n)), domain, 1, 0)[0],
+            lax.axis_index("band").astype(jnp.int32)[None],
+        ]
+    )
+    params = pltpu.CompilerParams(vmem_limit_bytes=40 * 1024 * 1024)
+    HBM = pl.BlockSpec(memory_space=pltpu.HBM)
+    small = pl.CostEstimate(flops=1, bytes_accessed=1, transcendentals=0)
+
+    def shape(rows, dtype=f32):
+        return jax.ShapeDtypeStruct((rows, 128), dtype)
+
+    def swap(x, step):
+        return lax.ppermute(x, "domain", [(i, i ^ step) for i in range(n)])
+
+    all_p = [p] + [swap(p, 2 * local) for local in range(1, half)]
+    pieces = [v_piece]
+    for back in range(1, nband):
+        ring = [(i, (i + back) % nband) for i in range(nband)]
+        pieces.append(lax.ppermute(v_piece, "band", ring))
+    sources = (psi.reshape(SLAB, 128), p, offsets[0].T, intersection[0].T, couplings)
+    sources = [pltpu.with_memory_space_constraint(x, pltpu.HBM) for x in sources]
+    pack = pl.pallas_call(
+        functools.partial(pack_kernel, dims),
+        out_shape=shape(PACK),
+        in_specs=[HBM] * 5,
+        out_specs=VMEM,
+        scratch_shapes=[
+            pltpu.VMEM(p.shape, f32),
+            pltpu.SMEM((cap, n), jnp.int32),
+            pltpu.SMEM((cap, n), jnp.int32),
+            pltpu.VMEM(couplings.shape, f32),
+            pltpu.VMEM((lanes, 128), f32),
+            pltpu.SemaphoreType.DMA((5,)),
+        ],
+        compiler_params=params,
+        cost_estimate=small,
+        name="pack",
+    )(*sources)
+    pack = pl.pallas_call(
+        fill_kernel,
+        out_shape=shape(PACK),
+        in_specs=[VMEM] * (1 + nband),
+        out_specs=VMEM,
+        compiler_params=params,
+        cost_estimate=small,
+        name="fill",
+    )(pack, *pieces)
+    got = lax.all_gather(pack, "domain", axis=0)
+    other = pltpu.VMEM(((half + 1) * SLAB, 128), f32)
+    padded = pltpu.VMEM((half * 6 * (NY + 16), 128), f32)
+    row_scratch = pltpu.VMEM((half * lanes, 128), f32)
+    ints = [pltpu.SMEM((8, 128), jnp.int32), pltpu.SemaphoreType.DMA(())]
+    part, previous, v, w, c, table = pl.pallas_call(
+        functools.partial(begin_kernel, dims, nband),
+        out_shape=(
+            shape(half * SLAB),
+            shape(half * SLAB),
+            shape(half * SLAB),
+            shape(half * lanes),
+            shape(n),
+            shape(8, jnp.int32),
+        ),
+        in_specs=[SMEM, VMEM],
+        out_specs=(VMEM,) * 6,
+        scratch_shapes=[other, padded],
+        compiler_params=params,
+        cost_estimate=small,
+        name="begin",
+    )(info, got)
+    sent = shape(half * SLAB + 8)
+    y = pl.pallas_call(
+        functools.partial(first_kernel, dims),
+        out_shape=sent,
+        in_specs=[VMEM] * (4 + half),
+        out_specs=VMEM,
+        scratch_shapes=[row_scratch] + ints,
+        compiler_params=params,
+        name="first",
+    )(table, part, w, c, *all_p)
+    for degree in range(1, DEGREE):
+        last = degree == DEGREE - 1
+        following = pl.pallas_call(
+            functools.partial(chip_kernel, dims, last),
+            out_shape=shape(SLAB) if last else sent,
+            in_specs=[VMEM] * (6 + half),
+            out_specs=VMEM,
+            scratch_shapes=[other, padded] + ints + ([] if last else [row_scratch]),
+            compiler_params=params,
+            name="last" if last else "next",
+        )(table, y, swap(y, 1), previous, v, w, *all_p)
+        previous, y = y, following
+    return y.reshape(psi.shape)
+
+
+def shards(psi, potential, projectors, offsets, intersection, dmat):
+    n = lax.axis_size("domain")
+    nband = lax.axis_size("band")
+    pairs = n % 2 == 0 and (n // 2) & (n // 2 - 1) == 0
+    fits = 4 <= n <= 8 and potential.shape[1] % 8 == 0 and nband <= 8
+    form = chip_form if pairs and fits else slab_form
+    return form(psi, potential, projectors, offsets, intersection, dmat)
+
+
 def solution(mesh):
     return jax.shard_map(
         shards,

time: 60.5 us -> 77 us (1.27)
  waiting for transfers between devices: 5.04 us -> 36.4 us
  blocking collectives: 21.5 us -> 0 us
  between operations: 0.1 us -> 13.5 us
  starting transfers between devices: 21.1 us -> 10.7 us
  Pallas kernels: 8.68 us -> 13.3 us
    all_gather x0 -> x1, waiting for transfers between devices: none -> 28.6 us  [chip_form(): got = lax.all_gather(pack, 'domain', axis=0)]
    all_to_all x3 -> x0, blocking collectives: 21.5 us -> none  [shards(): got = lax.all_to_all(c, 'domain', split_axis=0, concat_axis=0, tiled=True)]
    ppermute x11 -> x9, waiting for transfers between devices: 0.03 us -> 7.76 us  [the longest x6 4.35 us: swap(): return lax.ppermute(x, 'domain', [(i, i ^ step) for i in range(n)])]
    ppermute x11 -> x9, starting transfers between devices: 17.6 us -> 10.7 us  [the longest x3 6.06 us: chip_form(): pieces.append(lax.ppermute(v_piece, 'band', ring))]
    all_to_all x1 -> x0, waiting for transfers between devices: 5.01 us -> none  [shards(): lax.all_to_all(start(y, p, off, atom, couplings), 'domain', split_axis=0,...]
    pallas_call x5 -> x7, Pallas kernels: 8.68 us -> 13.3 us  [the longest x3 6.85 us: chip_form(): pl.pallas_call(functools.partial(chip_kernel, dims, last), out_shape=shap...]
    all_to_all x1 -> x0, starting transfers between devices: 3.49 us -> none  [shards(): lax.all_to_all(start(y, p, off, atom, couplings), 'domain', split_axis=0,...]
    unnamed x16 -> x6, local copies, waits for them, and re-layouts: 3.4 us -> 2.18 us
  transfers between devices with their start and end apart: 12 -> 10, of which waited for: 1 -> 6; matrix products, arithmetic and copies ran while one was open for 0% -> 1% of each run, Pallas kernels for 2% -> 5%
where the time goes in v3:
time: 77 us; the launch traced here: 76.8 us
  waiting for transfers between devices  36.4 us (47%)
  between operations  13.5 us (18%)
  Pallas kernels  13.3 us (17%)
  starting transfers between devices  10.7 us (14%)
  local copies, waits for them, and re-layouts  2.87 us (4%)
    all_gather x1, waiting for transfers between devices, chip_form(): got = lax.all_gather(pack, 'domain', axis=0)  28.6 us
    pallas_call x3, Pallas kernels, chip_form(): pl.pallas_call(functools.partial(chip_kernel, dims, last), out_shape=shap...  6.85 us
    ppermute x3, starting transfers between devices, chip_form(): pieces.append(lax.ppermute(v_piece, 'band', ring))  6.06 us
    ppermute x6, starting transfers between devices, swap(): return lax.ppermute(x, 'domain', [(i, i ^ step) for i in range(n)])  4.6 us
    ppermute x6, waiting for transfers between devices, swap(): return lax.ppermute(x, 'domain', [(i, i ^ step) for i in range(n)])  4.35 us
    ppermute x3, waiting for transfers between devices, chip_form(): pieces.append(lax.ppermute(v_piece, 'band', ring))  3.41 us
    pallas_call x1, Pallas kernels, chip_form(): pl.pallas_call(functools.partial(begin_kernel, dims, nband), out_shape=(s...  2.54 us
    unnamed x6, local copies, waits for them, and re-layouts  2.18 us
  transfers between devices with their start and end apart: 10, of which 6 were waited for; matrix products, arithmetic and copies ran while one was open for 1% of the time, Pallas kernels for 5%

profile of v3, /device:TPU:0, one launch (start us, length us, event | category | flops | bytes accessed | tf_op | source)
XLA Modules:
  0.0 76.8 jit_solution(155473748014608719)
XLA Ops:
  6.5 5.0 %collective-permute-start.2 = (f32[48,128]{1,0:T(8,128)}, f32[48,128]{1,0:T(8,128)S(1)}, u32[]{:S(2)}, u32[]{:S(2)}) collective-permute-start(f32[48,128]{1,0:T(8,128)} %bitcast.26), channel_id=1, source_target_pairs={{0,3},{1,0},{2,1},{3,2},{4,7},{5,4},{6,5},{7,6},{8,11},{9,8},{10,9... | collective-permute-start | bytes 73736 | tf_op jit(solution)/shard_map/ppermute | solution.py:637
  11.6 1.0 %collective-permute-start = (f32[48,128]{1,0:T(8,128)}, f32[48,128]{1,0:T(8,128)S(1)}, u32[]{:S(2)}, u32[]{:S(2)}) collective-permute-start(f32[48,128]{1,0:T(8,128)} %bitcast.28), channel_id=1, source_target_pairs={{0,1},{1,2},{2,3},{3,0},{4,5},{5,6},{6,7},{7,4},{8,9},{9,10},{10,1... | collective-permute-start | bytes 73736 | tf_op jit(solution)/shard_map/ppermute | solution.py:637
  12.6 1.4 %pack.1.pack_ref = f32[408,128]{1,0:T(8,128)S(1)} custom-call(f32[192,128]{1,0:T(8,128)} %bitcast.30, f32[128,1024]{1,0:T(8,128)} %bitcast.17, s32[2,8]{1,0:T(2,128)} %bitcast.32, s32[2,8]{1,0:T(2,128)} %bitcast.33, f32[64,32]{1,0:T(8,128)} %bitcast.31), custom_call_target="tpu_custom_call" | custom-call | flops 1 | bytes 1 | tf_op jit(solution)/shard_map/pack/pallas_call | solution.py:640
  14.0 2.5 %collective-permute-done.1.refs_2_ = f32[48,128]{1,0:T(8,128)S(1)} collective-permute-done((f32[48,128]{1,0:T(8,128)}, f32[48,128]{1,0:T(8,128)S(1)}, u32[]{:S(2)}, u32[]{:S(2)}) %collective-permute-start.1) | collective-permute-done | bytes 24608 | tf_op jit(solution)/shard_map/ppermute | solution.py:637
  16.5 0.9 %collective-permute-done.refs_1_ = f32[48,128]{1,0:T(8,128)S(1)} collective-permute-done((f32[48,128]{1,0:T(8,128)}, f32[48,128]{1,0:T(8,128)S(1)}, u32[]{:S(2)}, u32[]{:S(2)}) %collective-permute-start) | collective-permute-done | bytes 24608 | tf_op jit(solution)/shard_map/ppermute | solution.py:637
  17.4 0.7 copy-done.2
  18.2 0.7 fill.1
  18.9 2.5 %collective-permute-start.5 = (f32[128,1024]{1,0:T(8,128)}, f32[128,1024]{1,0:T(8,128)S(1)}, u32[]{:S(2)}, u32[]{:S(2)}) collective-permute-start(f32[128,1024]{1,0:T(8,128)} %bitcast.18), channel_id=1, source_target_pairs={{0,24},{4,28},{8,16},{12,20},{16,8},{20,12},{24,0},{28,4},{1,25},{... | collective-permute-start | bytes 1572872 | tf_op jit(solution)/shard_map/ppermute | solution.py:631
  21.4 0.5 collective-permute-start.4
  21.9 0.5 collective-permute-start.3
  22.4 0.7 dynamic-slice_bitcast_fusion
  23.2 28.6 %all-gather.3.cloned.1.call-done = f32[3264,128]{1,0:T(8,128)} async-done(((f32[408,128]{1,0:T(8,128)}), f32[3264,128]{1,0:T(8,128)}) %all-gather.3.cloned.1.call-update) | async-done | bytes 1671184 | tf_op jit(solution)/shard_map/all_gather | solution.py:666
  51.8 1.4 %copy-done.1 = f32[3264,128]{1,0:T(8,128)S(1)} copy-done((f32[3264,128]{1,0:T(8,128)S(1)}, f32[3264,128]{1,0:T(8,128)}, u32[]{:S(2)}) %copy-start.1) | copy-done | bytes 1671192
  53.3 2.5 %begin.1 = (f32[768,128]{1,0:T(8,128)S(1)}, f32[768,128]{1,0:T(8,128)S(1)}, f32[768,128]{1,0:T(8,128)S(1)}, f32[512,128]{1,0:T(8,128)S(1)}, f32[8,128]{1,0:T(8,128)S(1)}, /*index=5*/s32[8,128]{1,0:T(8,128)S(1)}) custom-call(s32[17]{0:T(128)S(1)} %pad_add_fusion.info_ref, f32[8,408,128]{2,1,0:T(8,128)S(1)} %bitcast.25), custom_call_target="tpu_custom_call" | custom-call | flops 1 | bytes 1 | tf_op jit(solution)/shard_map/begin/pallas_call | solution.py:671
  55.9 1.8 %first.1.refs_1_.refs_3_ = f32[776,128]{1,0:T(8,128)S(1)} custom-call(s32[8,128]{1,0:T(8,128)S(1)} %get-tuple-element.11.refs_0_, f32[768,128]{1,0:T(8,128)S(1)} %get-tuple-element.12.refs_1_, f32[512,128]{1,0:T(8,128)S(1)} %get-tuple-element.13.refs_2_.refs_5_, f32[8,128]{1,0:T(8,128)S(1)} %get-tuple-element.14.refs_3_, f32[128,1024]{1,0:T(8,128)S(1)} %bitcast.21, ...), custom_call_target="tpu_custom_call" | custom-call | tf_op jit(solution)/shard_map/first/pallas_call | solution.py:689
  57.7 0.3 collective-permute-start.6
  58.0 1.5 %collective-permute-done.6.refs_2_ = f32[776,128]{1,0:T(8,128)S(1)} collective-permute-done((f32[776,128]{1,0:T(8,128)S(1)}, f32[776,128]{1,0:T(8,128)S(1)}, u32[]{:S(2)}, u32[]{:S(2)}) %collective-permute-start.6) | collective-permute-done | bytes 397344 | tf_op jit(solution)/shard_map/ppermute | solution.py:631
  59.5 2.6 %next.2.refs_1_.refs_3_ = f32[776,128]{1,0:T(8,128)S(1)} custom-call(s32[8,128]{1,0:T(8,128)S(1)} %get-tuple-element.11.refs_0_, f32[776,128]{1,0:T(8,128)S(1)} %first.1.refs_1_.refs_3_, f32[776,128]{1,0:T(8,128)S(1)} %collective-permute-done.6.refs_2_, f32[768,128]{1,0:T(8,128)S(1)} %get-tuple-element.15.refs_3_, f32[768,128]{1,0:T(8,128)S(1)} %get-tuple-element.16.refs_4_, ...), custom_call_target="tpu_custom_call" | custom-call | tf_op jit(solution)/shard_map/next/pallas_call | solution.py:700
  62.1 0.3 collective-permute-start.7
  62.4 1.4 %collective-permute-done.7.refs_2_ = f32[776,128]{1,0:T(8,128)S(1)} collective-permute-done((f32[776,128]{1,0:T(8,128)S(1)}, f32[776,128]{1,0:T(8,128)S(1)}, u32[]{:S(2)}, u32[]{:S(2)}) %collective-permute-start.7) | collective-permute-done | bytes 397344 | tf_op jit(solution)/shard_map/ppermute | solution.py:631
  63.9 2.6 %next.3.refs_1_ = f32[776,128]{1,0:T(8,128)S(1)} custom-call(s32[8,128]{1,0:T(8,128)S(1)} %get-tuple-element.11.refs_0_, f32[776,128]{1,0:T(8,128)S(1)} %next.2.refs_1_.refs_3_, f32[776,128]{1,0:T(8,128)S(1)} %collective-permute-done.7.refs_2_, f32[776,128]{1,0:T(8,128)S(1)} %first.1.refs_1_.refs_3_, f32[768,128]{1,0:T(8,128)S(1)} %get-tuple-element.16.refs_4_, ...), custom_call_target="tpu_custom_call" | custom-call | tf_op jit(solution)/shard_map/next/pallas_call | solution.py:700
  66.5 0.4 collective-permute-start.8
  66.8 1.4 %collective-permute-done.8.refs_2_ = f32[776,128]{1,0:T(8,128)S(1)} collective-permute-done((f32[776,128]{1,0:T(8,128)S(1)}, f32[776,128]{1,0:T(8,128)S(1)}, u32[]{:S(2)}, u32[]{:S(2)}) %collective-permute-start.8) | collective-permute-done | bytes 397344 | tf_op jit(solution)/shard_map/ppermute | solution.py:631
  68.3 1.6 %last.1 = f32[192,128]{1,0:T(8,128)} custom-call(s32[8,128]{1,0:T(8,128)S(1)} %get-tuple-element.11.refs_0_, f32[776,128]{1,0:T(8,128)S(1)} %next.3.refs_1_, f32[776,128]{1,0:T(8,128)S(1)} %collective-permute-done.8.refs_2_, f32[776,128]{1,0:T(8,128)S(1)} %next.2.refs_1_.refs_3_, f32[768,128]{1,0:T(8,128)S(1)} %get-tuple-element.16.refs_4_, ...), custom_call_target="tpu_custom_call" | custom-call | tf_op jit(solution)/shard_map/last/pallas_call | solution.py:700
  (12 shorter events, 0.1 us)
Async XLA Ops:
  6.5 49.3 %copy-start = (f32[1,8,2,8,1024]{4,3,2,1,0:T(8,128)S(1)}, f32[1,8,2,8,1024]{4,3,2,1,0:T(8,128)}, u32[]{:S(2)}) copy-start(f32[1,8,2,8,1024]{4,3,2,1,0:T(8,128)} %param.9) | copy-start | bytes 1572868
  6.5 45.3 %all-gather.3.cloned.1.call-start = ((), (), s32[]{:S(2)}) async-start(), calls=%async_computation | async-start | bytes 1880064 | tf_op jit(solution)/shard_map/all_gather | solution.py:666
  6.5 7.5 %collective-permute-start.2 = (f32[48,128]{1,0:T(8,128)}, f32[48,128]{1,0:T(8,128)S(1)}, u32[]{:S(2)}, u32[]{:S(2)}) collective-permute-start(f32[48,128]{1,0:T(8,128)} %bitcast.26), channel_id=1, source_target_pairs={{0,3},{1,0},{2,1},{3,2},{4,7},{5,4},{6,5},{7,6},{8,11},{9,8},{10,9... | collective-permute-start | bytes 73736 | tf_op jit(solution)/shard_map/ppermute | solution.py:637
  11.6 4.9 %collective-permute-start.1 = (f32[48,128]{1,0:T(8,128)}, f32[48,128]{1,0:T(8,128)S(1)}, u32[]{:S(2)}, u32[]{:S(2)}) collective-permute-start(f32[48,128]{1,0:T(8,128)} %bitcast.27), channel_id=1, source_target_pairs={{0,2},{1,3},{2,0},{3,1},{4,6},{5,7},{6,4},{7,5},{8,10},{9,11},{10,... | collective-permute-start | bytes 73736 | tf_op jit(solution)/shard_map/ppermute | solution.py:637
  11.6 5.8 %collective-permute-start = (f32[48,128]{1,0:T(8,128)}, f32[48,128]{1,0:T(8,128)S(1)}, u32[]{:S(2)}, u32[]{:S(2)}) collective-permute-start(f32[48,128]{1,0:T(8,128)} %bitcast.28), channel_id=1, source_target_pairs={{0,1},{1,2},{2,3},{3,0},{4,5},{5,6},{6,7},{7,4},{8,9},{9,10},{10,1... | collective-permute-start | bytes 73736 | tf_op jit(solution)/shard_map/ppermute | solution.py:637
  17.4 0.7 copy-start.2
  18.9 36.9 %collective-permute-start.5 = (f32[128,1024]{1,0:T(8,128)}, f32[128,1024]{1,0:T(8,128)S(1)}, u32[]{:S(2)}, u32[]{:S(2)}) collective-permute-start(f32[128,1024]{1,0:T(8,128)} %bitcast.18), channel_id=1, source_target_pairs={{0,24},{4,28},{8,16},{12,20},{16,8},{20,12},{24,0},{28,4},{1,25},{... | collective-permute-start | bytes 1572872 | tf_op jit(solution)/shard_map/ppermute | solution.py:631
  21.4 34.4 %collective-permute-start.4 = (f32[128,1024]{1,0:T(8,128)}, f32[128,1024]{1,0:T(8,128)S(1)}, u32[]{:S(2)}, u32[]{:S(2)}) collective-permute-start(f32[128,1024]{1,0:T(8,128)} %bitcast.19), channel_id=1, source_target_pairs={{0,16},{4,20},{8,24},{12,28},{16,0},{20,4},{24,8},{28,12},{1,17},{... | collective-permute-start | bytes 1572872 | tf_op jit(solution)/shard_map/ppermute | solution.py:631
  21.9 33.9 %collective-permute-start.3 = (f32[128,1024]{1,0:T(8,128)}, f32[128,1024]{1,0:T(8,128)S(1)}, u32[]{:S(2)}, u32[]{:S(2)}) collective-permute-start(f32[128,1024]{1,0:T(8,128)} %bitcast.20), channel_id=1, source_target_pairs={{0,8},{4,12},{8,0},{12,4},{16,24},{20,28},{24,16},{28,20},{1,9},{5... | collective-permute-start | bytes 1572872 | tf_op jit(solution)/shard_map/ppermute | solution.py:631
  51.8 1.4 %copy-start.1 = (f32[3264,128]{1,0:T(8,128)S(1)}, f32[3264,128]{1,0:T(8,128)}, u32[]{:S(2)}) copy-start(f32[3264,128]{1,0:T(8,128)} %all-gather.3.cloned.1.call-done) | copy-start | bytes 5013508
  57.7 1.8 %collective-permute-start.6 = (f32[776,128]{1,0:T(8,128)S(1)}, f32[776,128]{1,0:T(8,128)S(1)}, u32[]{:S(2)}, u32[]{:S(2)}) collective-permute-start(f32[776,128]{1,0:T(8,128)S(1)} %first.1.refs_1_.refs_3_), channel_id=1, source_target_pairs={{0,4},{4,0},{8,12},{12,8},{16,20},{20,16},{24,28},{28,24},{1,5},{5... | collective-permute-start | bytes 1191944 | tf_op jit(solution)/shard_map/ppermute | solution.py:631
  62.1 1.8 %collective-permute-start.7 = (f32[776,128]{1,0:T(8,128)S(1)}, f32[776,128]{1,0:T(8,128)S(1)}, u32[]{:S(2)}, u32[]{:S(2)}) collective-permute-start(f32[776,128]{1,0:T(8,128)S(1)} %next.2.refs_1_.refs_3_), channel_id=1, source_target_pairs={{0,4},{4,0},{8,12},{12,8},{16,20},{20,16},{24,28},{28,24},{1,5},{5... | collective-permute-start | bytes 1191944 | tf_op jit(solution)/shard_map/ppermute | solution.py:631
  66.5 1.8 %collective-permute-start.8 = (f32[776,128]{1,0:T(8,128)S(1)}, f32[776,128]{1,0:T(8,128)S(1)}, u32[]{:S(2)}, u32[]{:S(2)}) collective-permute-start(f32[776,128]{1,0:T(8,128)S(1)} %next.3.refs_1_), channel_id=1, source_target_pairs={{0,4},{4,0},{8,12},{12,8},{16,20},{20,16},{24,28},{28,24},{1,5},{5... | collective-permute-start | bytes 1191944 | tf_op jit(solution)/shard_map/ppermute | solution.py:631
Sparse Core Ops, SparseCore 0:
  19.0 32.7 all-gather.2

commit v4 on v3

--- a/solution.py
+++ b/solution.py
@@ -303,7 +303,7 @@
 
 NY = 32
 SLAB = 6 * NY
-PACK = 2 * SLAB + 24
+SMALL = 24
 
 
 def circulant_z():
@@ -361,10 +361,17 @@
 def pack_kernel(dims, *refs):
     n, cap, nproj, foot, chunk = dims
     lanes = n * chunk
-    sources, pack_ref, scratch = refs[:5], refs[5], refs[6:]
+    sources, pack_ref, scratch = refs[:6], refs[6], refs[7:]
     p_ref, off_ref, atom_ref, dmat_ref, r_ref, sems = scratch
-    y_ref = pack_ref.at[0:SLAB, :]
-    targets = (y_ref, p_ref, off_ref, atom_ref, dmat_ref)
+    small = pack_ref.shape[0] - SMALL
+    targets = (
+        pack_ref.at[0:SLAB, :],
+        p_ref,
+        off_ref,
+        atom_ref,
+        dmat_ref,
+        pack_ref.at[SLAB:small, :],
+    )
     copies = [
         pltpu.make_async_copy(source, target, sems.at[index])
         for index, (source, target) in enumerate(zip(sources, targets))
@@ -380,9 +387,9 @@
         here = lane == slot
         atoms = jnp.where(here, atom_ref[slot % cap, slot // cap].astype(f32), atoms)
         starts = jnp.where(here, off_ref[slot % cap, slot // cap].astype(f32), starts)
-    small = 2 * SLAB
     pack_ref[small + 1 : small + 2, :] = atoms
     pack_ref[small + 2 : small + 3, :] = starts
+    pack_ref[small + 3 : small + 8, :] = jnp.zeros((5, 128), f32)
     count = dmat_ref.shape[1]
     for group in range(128 // count):
         block = dmat_ref[group * 2 * nproj : (group + 1) * 2 * nproj, :]
@@ -392,41 +399,49 @@
     pack_ref[small : small + 1, :] = partials(pack_ref, p_ref, off_ref, r_ref, dims)[0:1]
 
 
-def fill_kernel(pack_ref, *refs):
-    pieces, out_ref = refs[:-1], refs[-1]
-    out_ref[0:SLAB, :] = pack_ref[0:SLAB, :]
-    out_ref[2 * SLAB :, :] = pack_ref[2 * SLAB :, :]
-    rows = pieces[0].shape[0]
-    for back, piece in enumerate(pieces):
-        out_ref[SLAB + back * rows : SLAB + (back + 1) * rows, :] = piece[...]
-
-
-def begin_kernel(dims, nband, info_ref, got_ref, part_ref, y_ref, v_ref, w_ref, c_ref, int_ref, other_ref, pad_ref):
+def sort_kernel(*refs):
+    packs, (pair_ref, v_ref) = refs[:-2], refs[-2:]
+    small = packs[0].shape[0] - SMALL
+    size = SLAB + SMALL
+    for local, pack in enumerate(packs):
+        pair_ref[local * size : local * size + SLAB, :] = pack[0:SLAB, :]
+        pair_ref[local * size + SLAB : (local + 1) * size, :] = pack[small:, :]
+        v_ref[local * (small - SLAB) : (local + 1) * (small - SLAB), :] = pack[SLAB:small, :]
+
+
+def relay_kernel(x_ref, y_ref, top_ref, bottom_ref):
+    rows = top_ref.shape[0]
+    top_ref[...] = x_ref[0:rows, :]
+    bottom_ref[...] = y_ref[rows:, :]
+
+
+def begin_kernel(dims, nband, info_ref, own_ref, got_ref, *refs):
     n, cap, nproj, foot, chunk = dims
     half = n // 2
+    v_pieces, refs = refs[:nband], refs[nband:]
+    part_ref, y_ref, v_ref, w_ref, c_ref, int_ref, other_ref, pad_ref, dmat_ref = refs
     lanes = n * chunk
-    small = 2 * SLAB
+    size = SLAB + SMALL
     piece = NY // nband
+    for back in range(nband):
+        at = lax.rem(info_ref[4 * half + n] - back + nband, nband) * piece
+        for plane in range(6 * half):
+            spot = pl.multiple_of(plane * NY + at, 8)
+            v_ref[pl.ds(spot, piece), :] = v_pieces[back][plane * piece : (plane + 1) * piece, :]
     c_rows, atom_rows, start_rows = [], [], []
-    for local in range(half):
-        mine, theirs = info_ref[local], info_ref[half + local]
-        rows = slice(local * SLAB, (local + 1) * SLAB)
-        y_ref[rows, :] = got_ref[mine, 0:SLAB, :]
-        other_ref[rows, :] = got_ref[theirs, 0:SLAB, :]
-        for back in range(nband):
-            at = lax.rem(info_ref[4 * half] - back + nband, nband) * piece
-            for plane in range(6):
-                spot = pl.multiple_of(local * SLAB + plane * NY + at, 8)
-                source = SLAB + back * 6 * piece + plane * piece
-                v_ref[pl.ds(spot, piece), :] = got_ref[mine, source : source + piece, :]
+    for group, source in enumerate((own_ref, got_ref)):
+        for local in range(half):
+            slab = local * size
+            rows = slice(local * SLAB, (local + 1) * SLAB)
+            target = other_ref if group else y_ref
+            target[rows, :] = source[slab : slab + SLAB, :]
+            small = slab + SLAB
+            c_rows.append(source[small : small + 1, :])
+            atom_rows.append(source[small + 1 : small + 2, :])
+            if group == 0:
+                start_rows.append(source[small + 2 : small + 3, :])
+            dmat_ref[group * half + local] = source[small + 8 : small + SMALL, :]
     other_ref[half * SLAB :, :] = jnp.zeros((SLAB, 128), f32)
-    for group in (0, half):
-        for local in range(half):
-            slab = info_ref[group + local]
-            c_rows.append(got_ref[slab, small : small + 1, :])
-            atom_rows.append(got_ref[slab, small + 1 : small + 2, :])
-            if group == 0:
-                start_rows.append(got_ref[slab, small + 2 : small + 3, :])
     c_ref[...] = by_owner(jnp.concatenate(c_rows, 0), n, chunk)
     atoms = by_owner(jnp.concatenate(atom_rows, 0), n, chunk)
     lane = iota((1, 128), 1)
@@ -471,7 +486,7 @@
         mine = jnp.concatenate([m[rows, :] for m in wide], 0)
         entries = lax.dot_general(
             pick,
-            got_ref[owner, small + 8 :, :],
+            dmat_ref[info_ref[4 * half + owner]],
             (((1,), (1,)), ((), ())),
             precision=highest,
             preferred_element_type=f32,
@@ -480,6 +495,13 @@
         block = jnp.dot(entries, spread, precision=highest, preferred_element_type=f32)
         same = (atoms[owner : owner + 1, :] == mine) & (mine >= 0.0)
         w_ref[owner * tall : (owner + 1) * tall, :] = jnp.where(same, block, 0.0)
+
+
+def p_rows(p_refs, slab, slot, nproj, tile):
+    ref, at = p_refs[slab], slot * nproj
+    if at >= ref.shape[0]:
+        ref, at = p_refs[slab + 1], at - ref.shape[0]
+    return ref[at : at + nproj, tile * 128 : (tile + 1) * 128]
 
 
 def couple(dims, slabs, half, coefficients, w_ref, p_refs, start_of, out_ref, scale):
@@ -496,10 +518,9 @@
             )
             returned = jnp.broadcast_to(returned * scale, (nproj, 128))
             contrib = jnp.zeros((foot, 128), f32)
-            rows = slice(slot * nproj, (slot + 1) * nproj)
             for tile in range(foot):
                 term = jnp.sum(
-                    p_refs[slab][rows, tile * 128 : (tile + 1) * 128] * returned,
+                    p_rows(p_refs, slab, slot, nproj, tile) * returned,
                     axis=0,
                     keepdims=True,
                 )
@@ -514,11 +535,10 @@
     for slab in range(half):
         for slot in range(n * cap):
             start = start_of(slab, slot)
-            rows = slice(slot * nproj, (slot + 1) * nproj)
             total = None
             for tile in range(foot):
                 cells = jnp.broadcast_to(send_ref[pl.ds(start + tile, 1), :], (nproj, 128))
-                term = p_refs[slab][rows, tile * 128 : (tile + 1) * 128] * cells
+                term = p_rows(p_refs, slab, slot, nproj, tile) * cells
                 total = term if total is None else total + term
             r_ref[slab * lanes + slot * nproj : slab * lanes + (slot + 1) * nproj, :] = total
     row = lax.dot_general(
@@ -543,7 +563,7 @@
     n, cap, nproj, foot, chunk = dims
     half = n // 2
     int_ref, part_ref, w_ref, c_ref = refs[:4]
-    p_refs, (send_ref, r_ref, int_s, sem) = refs[4 : 4 + half], refs[4 + half :]
+    p_refs, (send_ref, r_ref, int_s, sem) = refs[4 : 5 + half], refs[5 + half :]
     copy = pltpu.make_async_copy(int_ref, int_s, sem)
     copy.start()
     send_ref[0 : half * SLAB, :] = part_ref[...]
@@ -558,8 +578,8 @@
     n, cap, nproj, foot, chunk = dims
     half = n // 2
     int_ref, y_ref, got_ref, prev_ref, v_ref, w_ref = refs[:6]
-    p_refs = refs[6 : 6 + half]
-    out_ref, other_ref, pad_ref, int_s, sem = refs[6 + half : 11 + half]
+    p_refs = refs[6 : 7 + half]
+    out_ref, other_ref, pad_ref, int_s, sem = refs[7 + half : 12 + half]
     copy = pltpu.make_async_copy(int_ref, int_s, sem)
     copy.start()
     other_ref[0 : half * SLAB, :] = got_ref[0 : half * SLAB, :]
@@ -581,23 +601,24 @@
     start_of = starts_from(int_s, nproj)
     couple(dims, slabs, half, coefficients, w_ref, p_refs, start_of, out_ref, scale)
     if not last:
-        next_partials(dims, half, out_ref, p_refs, start_of, refs[11 + half])
+        next_partials(dims, half, out_ref, p_refs, start_of, refs[12 + half])
 
 
 def chip_table(n):
     half = n // 2
-    table = np.zeros((n, 4 * half), np.int32)
+    table = np.zeros((n, 4 * half + n), np.int32)
     for device in range(n):
         chip, core = device // 2, device % 2
         for local in range(half):
             there = chip ^ local
-            table[device, local] = 2 * there + core
-            table[device, half + local] = 2 * there + 1 - core
             same = local * SLAB
             far = there + (1 if core else -1)
             cross = (far ^ chip) * SLAB if 0 <= far < half else half * SLAB
             table[device, 2 * half + local] = same if core else cross
             table[device, 3 * half + local] = cross if core else same
+        for owner in range(n):
+            table[device, 4 * half + owner] = owner % 2 * half if core == 0 else (1 - owner % 2) * half
+            table[device, 4 * half + owner] += owner // 2 ^ chip
     return table
 
 
@@ -623,6 +644,7 @@
     params = pltpu.CompilerParams(vmem_limit_bytes=40 * 1024 * 1024)
     HBM = pl.BlockSpec(memory_space=pltpu.HBM)
     small = pl.CostEstimate(flops=1, bytes_accessed=1, transcendentals=0)
+    large = pl.CostEstimate(flops=10**10, bytes_accessed=1, transcendentals=0)
 
     def shape(rows, dtype=f32):
         return jax.ShapeDtypeStruct((rows, 128), dtype)
@@ -630,17 +652,12 @@
     def swap(x, step):
         return lax.ppermute(x, "domain", [(i, i ^ step) for i in range(n)])
 
-    all_p = [p] + [swap(p, 2 * local) for local in range(1, half)]
-    pieces = [v_piece]
-    for back in range(1, nband):
-        ring = [(i, (i + back) % nband) for i in range(nband)]
-        pieces.append(lax.ppermute(v_piece, "band", ring))
-    sources = (psi.reshape(SLAB, 128), p, offsets[0].T, intersection[0].T, couplings)
+    sources = (psi.reshape(SLAB, 128), p, offsets[0].T, intersection[0].T, couplings, v_piece)
     sources = [pltpu.with_memory_space_constraint(x, pltpu.HBM) for x in sources]
     pack = pl.pallas_call(
         functools.partial(pack_kernel, dims),
-        out_shape=shape(PACK),
-        in_specs=[HBM] * 5,
+        out_shape=shape(SLAB + v_piece.shape[0] + SMALL),
+        in_specs=[HBM] * 6,
         out_specs=VMEM,
         scratch_shapes=[
             pltpu.VMEM(p.shape, f32),
@@ -648,22 +665,39 @@
             pltpu.SMEM((cap, n), jnp.int32),
             pltpu.VMEM(couplings.shape, f32),
             pltpu.VMEM((lanes, 128), f32),
-            pltpu.SemaphoreType.DMA((5,)),
+            pltpu.SemaphoreType.DMA((6,)),
         ],
         compiler_params=params,
         cost_estimate=small,
         name="pack",
     )(*sources)
-    pack = pl.pallas_call(
-        fill_kernel,
-        out_shape=shape(PACK),
-        in_specs=[VMEM] * (1 + nband),
-        out_specs=VMEM,
+    packs = [pack] + [swap(pack, 2 * local) for local in range(1, half)]
+    own, v_piece = pl.pallas_call(
+        sort_kernel,
+        out_shape=(shape(half * (SLAB + SMALL)), shape(half * v_piece.shape[0])),
+        in_specs=[VMEM] * half,
+        out_specs=(VMEM, VMEM),
         compiler_params=params,
         cost_estimate=small,
-        name="fill",
-    )(pack, *pieces)
-    got = lax.all_gather(pack, "domain", axis=0)
+        name="sort",
+    )(*packs)
+    got = swap(own, 1)
+    pieces = [v_piece]
+    for back in range(1, nband):
+        ring = [(i, (i + back) % nband) for i in range(nband)]
+        pieces.append(lax.ppermute(v_piece, "band", ring))
+    p_x, p_y = swap(p, 2), swap(p, 4)
+    halves = (jax.ShapeDtypeStruct((lanes // 2, foot * 128), f32),) * 2
+    top, bottom = pl.pallas_call(
+        relay_kernel,
+        out_shape=halves,
+        in_specs=[VMEM] * 2,
+        out_specs=(VMEM, VMEM),
+        compiler_params=params,
+        cost_estimate=large,
+        name="relay",
+    )(p_x, p_y)
+    all_p = [p, p_x, p_y, swap(top, 4), swap(bottom, 2)]
     other = pltpu.VMEM(((half + 1) * SLAB, 128), f32)
     padded = pltpu.VMEM((half * 6 * (NY + 16), 128), f32)
     row_scratch = pltpu.VMEM((half * lanes, 128), f32)
@@ -678,18 +712,18 @@
             shape(n),
             shape(8, jnp.int32),
         ),
-        in_specs=[SMEM, VMEM],
+        in_specs=[SMEM] + [VMEM] * (2 + nband),
         out_specs=(VMEM,) * 6,
-        scratch_shapes=[other, padded],
+        scratch_shapes=[other, padded, pltpu.VMEM((n, 2 * nproj, 128), f32)],
         compiler_params=params,
         cost_estimate=small,
         name="begin",
-    )(info, got)
+    )(info, own, got, *pieces)
     sent = shape(half * SLAB + 8)
     y = pl.pallas_call(
         functools.partial(first_kernel, dims),
         out_shape=sent,
-        in_specs=[VMEM] * (4 + half),
+        in_specs=[VMEM] * (5 + half),
         out_specs=VMEM,
         scratch_shapes=[row_scratch] + ints,
         compiler_params=params,
@@ -700,7 +734,7 @@
         following = pl.pallas_call(
             functools.partial(chip_kernel, dims, last),
             out_shape=shape(SLAB) if last else sent,
-            in_specs=[VMEM] * (6 + half),
+            in_specs=[VMEM] * (7 + half),
             out_specs=VMEM,
             scratch_shapes=[other, padded] + ints + ([] if last else [row_scratch]),
             compiler_params=params,
@@ -713,9 +747,8 @@
 def shards(psi, potential, projectors, offsets, intersection, dmat):
     n = lax.axis_size("domain")
     nband = lax.axis_size("band")
-    pairs = n % 2 == 0 and (n // 2) & (n // 2 - 1) == 0
-    fits = 4 <= n <= 8 and potential.shape[1] % 8 == 0 and nband <= 8
-    form = chip_form if pairs and fits else slab_form
+    fits = n == 8 and potential.shape[1] % 8 == 0 and nband <= 8
+    form = chip_form if fits else slab_form
     return form(psi, potential, projectors, offsets, intersection, dmat)
 
 

time: 77 us -> 55.2 us (0.72)
  between operations: 13.5 us -> 0.12 us
  waiting for transfers between devices: 36.4 us -> 27.1 us
  starting transfers between devices: 10.7 us -> 14.2 us
  local copies, waits for them, and re-layouts: 2.87 us -> 0.69 us
    all_gather x1 -> x0, waiting for transfers between devices: 28.6 us -> none  [chip_form(): got = lax.all_gather(pack, 'domain', axis=0)]
    ppermute x6 -> x11, waiting for transfers between devices: 4.35 us -> 17.8 us  [swap(): return lax.ppermute(x, 'domain', [(i, i ^ step) for i in range(n)])]
    ppermute x6 -> x11, starting transfers between devices: 4.6 us -> 10.6 us  [swap(): return lax.ppermute(x, 'domain', [(i, i ^ step) for i in range(n)])]
    ppermute x3, waiting for transfers between devices: 3.41 us -> 9.34 us  [chip_form(): pieces.append(lax.ppermute(v_piece, 'band', ring))]
    ppermute x3, starting transfers between devices: 6.06 us -> 3.61 us  [chip_form(): pieces.append(lax.ppermute(v_piece, 'band', ring))]
    unnamed x6 -> x2, local copies, waits for them, and re-layouts: 2.18 us -> 0.01 us
    pallas_call x2 -> x3, Pallas kernels: 2.08 us -> 1.5 us  [the longest x1 1.43 us: chip_form(): pl.pallas_call(functools.partial(pack_kernel, dims), out_shape=shape(SLAB...]
  transfers between devices with their start and end apart: 10 -> 14, of which waited for: 6 -> 9; matrix products, arithmetic and copies ran while one was open for 1% -> 1% of each run, Pallas kernels for 5% -> 7%
where the time goes in v4:
time: 55.2 us; the launch traced here: 55 us
  waiting for transfers between devices  27.1 us (49%)
  starting transfers between devices  14.2 us (26%)
  Pallas kernels  12.7 us (23%)
  local copies, waits for them, and re-layouts  0.69 us (1%)
    ppermute x11, waiting for transfers between devices, swap(): return lax.ppermute(x, 'domain', [(i, i ^ step) for i in range(n)])  17.8 us
    ppermute x11, starting transfers between devices, swap(): return lax.ppermute(x, 'domain', [(i, i ^ step) for i in range(n)])  10.6 us
    ppermute x3, waiting for transfers between devices, chip_form(): pieces.append(lax.ppermute(v_piece, 'band', ring))  9.34 us
    pallas_call x3, Pallas kernels, chip_form(): pl.pallas_call(functools.partial(chip_kernel, dims, last), out_shape=shap...  6.87 us
    ppermute x3, starting transfers between devices, chip_form(): pieces.append(lax.ppermute(v_piece, 'band', ring))  3.61 us
    pallas_call x1, Pallas kernels, chip_form(): pl.pallas_call(functools.partial(begin_kernel, dims, nband), out_shape=(s...  2.52 us
    pallas_call x1, Pallas kernels, chip_form(): pl.pallas_call(functools.partial(first_kernel, dims), out_shape=sent, in_...  1.82 us
    pallas_call x1, Pallas kernels, chip_form(): pl.pallas_call(functools.partial(pack_kernel, dims), out_shape=shape(SLAB...  1.43 us
  transfers between devices with their start and end apart: 14, of which 9 were waited for; matrix products, arithmetic and copies ran while one was open for 1% of the time, Pallas kernels for 7%

profile of v4, /device:TPU:0, one launch (start us, length us, event | category | flops | bytes accessed | tf_op | source)
XLA Modules:
  0.0 55.0 jit_solution(345627393012193970)
XLA Ops:
  0.0 3.0 %collective-permute-start.8 = (f32[128,1024]{1,0:T(8,128)}, f32[128,1024]{1,0:T(8,128)S(1)}, u32[]{:S(2)}, u32[]{:S(2)}) collective-permute-start(f32[128,1024]{1,0:T(8,128)} %bitcast.16), channel_id=1, source_target_pairs={{0,16},{4,20},{8,24},{12,28},{16,0},{20,4},{24,8},{28,12},{1,17},{... | collective-permute-start | bytes 1572872 | tf_op jit(solution)/shard_map/ppermute | solution.py:653
  3.0 1.5 %collective-permute-start.7 = (f32[128,1024]{1,0:T(8,128)}, f32[128,1024]{1,0:T(8,128)S(1)}, u32[]{:S(2)}, u32[]{:S(2)}) collective-permute-start(f32[128,1024]{1,0:T(8,128)} %bitcast.17), channel_id=1, source_target_pairs={{0,8},{4,12},{8,0},{12,4},{16,24},{20,28},{24,16},{28,20},{1,9},{5... | collective-permute-start | bytes 1572872 | tf_op jit(solution)/shard_map/ppermute | solution.py:653
  4.5 1.4 %pack.1.refs_0_ = f32[264,128]{1,0:T(8,128)S(1)} custom-call(f32[192,128]{1,0:T(8,128)} %bitcast.23, f32[128,1024]{1,0:T(8,128)} %bitcast.18, s32[2,8]{1,0:T(2,128)} %bitcast.26, s32[2,8]{1,0:T(2,128)} %bitcast.27, f32[64,32]{1,0:T(8,128)} %bitcast.24, f32[48,128]{1,0:T(8,128)} %bitcast.25), custom_call_target="tpu_custom_call" | custom-call | flops 1 | bytes 1 | tf_op jit(solution)/shard_map/pack/pallas_call | solution.py:657
  6.0 2.0 %collective-permute-start.1 = (f32[264,128]{1,0:T(8,128)S(1)}, f32[264,128]{1,0:T(8,128)S(1)}, u32[]{:S(2)}, u32[]{:S(2)}) collective-permute-start(f32[264,128]{1,0:T(8,128)S(1)} %pack.1.refs_0_), channel_id=1, source_target_pairs={{0,16},{4,20},{8,24},{12,28},{16,0},{20,4},{24,8},{28,12},{1,17},{... | collective-permute-start | bytes 405512 | tf_op jit(solution)/shard_map/ppermute | solution.py:653
  8.0 1.5 %collective-permute-start = (f32[264,128]{1,0:T(8,128)S(1)}, f32[264,128]{1,0:T(8,128)S(1)}, u32[]{:S(2)}, u32[]{:S(2)}) collective-permute-start(f32[264,128]{1,0:T(8,128)S(1)} %pack.1.refs_0_), channel_id=1, source_target_pairs={{0,8},{4,12},{8,0},{12,4},{16,24},{20,28},{24,16},{28,20},{1,9},{5... | collective-permute-start | bytes 405512 | tf_op jit(solution)/shard_map/ppermute | solution.py:653
  9.5 10.9 %collective-permute-done.2.refs_3_ = f32[264,128]{1,0:T(8,128)S(1)} collective-permute-done((f32[264,128]{1,0:T(8,128)S(1)}, f32[264,128]{1,0:T(8,128)S(1)}, u32[]{:S(2)}, u32[]{:S(2)}) %collective-permute-start.2) | collective-permute-done | bytes 135200 | tf_op jit(solution)/shard_map/ppermute | solution.py:653
  20.3 0.6 %collective-permute-done.1.refs_2_ = f32[264,128]{1,0:T(8,128)S(1)} collective-permute-done((f32[264,128]{1,0:T(8,128)S(1)}, f32[264,128]{1,0:T(8,128)S(1)}, u32[]{:S(2)}, u32[]{:S(2)}) %collective-permute-start.1) | collective-permute-done | bytes 135200 | tf_op jit(solution)/shard_map/ppermute | solution.py:653
  20.9 1.5 %collective-permute-done.refs_1_ = f32[264,128]{1,0:T(8,128)S(1)} collective-permute-done((f32[264,128]{1,0:T(8,128)S(1)}, f32[264,128]{1,0:T(8,128)S(1)}, u32[]{:S(2)}, u32[]{:S(2)}) %collective-permute-start) | collective-permute-done | bytes 135200 | tf_op jit(solution)/shard_map/ppermute | solution.py:653
  22.5 0.4 collective-permute-start.9
  22.9 1.7 %collective-permute-start.10 = (f32[64,1024]{1,0:T(8,128)S(1)}, f32[64,1024]{1,0:T(8,128)S(1)}, u32[]{:S(2)}, u32[]{:S(2)}) collective-permute-start(f32[64,1024]{1,0:T(8,128)S(1)} %get-tuple-element.22), channel_id=1, source_target_pairs={{0,8},{4,12},{8,0},{12,4},{16,24},{20,28},{24,16},{28,20},{1,9},{5... | collective-permute-start | bytes 786440 | tf_op jit(solution)/shard_map/ppermute | solution.py:653
  24.6 3.6 %collective-permute-start.6 = (f32[192,128]{1,0:T(8,128)S(1)}, f32[192,128]{1,0:T(8,128)S(1)}, u32[]{:S(2)}, u32[]{:S(2)}) collective-permute-start(f32[192,128]{1,0:T(8,128)S(1)} %get-tuple-element.16.refs_0_), channel_id=1, source_target_pairs={{0,3},{1,0},{2,1},{3,2},{4,7},{5,4},{6,5},{7,6},{8,11},{9,8},{10,9... | collective-permute-start | bytes 294920 | tf_op jit(solution)/shard_map/ppermute | solution.py:688
  28.2 0.7 %dynamic-slice_bitcast_fusion = s32[24]{0:T(128)S(1)} fusion(s32[8,24]{1,0:T(8,128)} %constant.15.clone, s32[]{:T(128)S(6)} %select_n.3), kind=kLoop, calls=%fused_computation.1 | loop fusion | bytes 196 | tf_op jit(solution)/shard_map/squeeze | solution.py:640
  28.9 2.5 %collective-permute-done.6.refs_3_ = f32[192,128]{1,0:T(8,128)S(1)} collective-permute-done((f32[192,128]{1,0:T(8,128)S(1)}, f32[192,128]{1,0:T(8,128)S(1)}, u32[]{:S(2)}, u32[]{:S(2)}) %collective-permute-start.6) | collective-permute-done | bytes 98336 | tf_op jit(solution)/shard_map/ppermute | solution.py:688
  31.5 4.9 %collective-permute-done.5.refs_2_ = f32[192,128]{1,0:T(8,128)S(1)} collective-permute-done((f32[192,128]{1,0:T(8,128)S(1)}, f32[192,128]{1,0:T(8,128)S(1)}, u32[]{:S(2)}, u32[]{:S(2)}) %collective-permute-start.5) | collective-permute-done | bytes 98336 | tf_op jit(solution)/shard_map/ppermute | solution.py:688
  36.4 1.9 %collective-permute-done.4.refs_1_ = f32[192,128]{1,0:T(8,128)S(1)} collective-permute-done((f32[192,128]{1,0:T(8,128)S(1)}, f32[192,128]{1,0:T(8,128)S(1)}, u32[]{:S(2)}, u32[]{:S(2)}) %collective-permute-start.4) | collective-permute-done | bytes 98336 | tf_op jit(solution)/shard_map/ppermute | solution.py:688
  38.3 2.5 %begin.1 = (f32[768,128]{1,0:T(8,128)S(1)}, f32[768,128]{1,0:T(8,128)S(1)}, f32[768,128]{1,0:T(8,128)S(1)}, f32[512,128]{1,0:T(8,128)S(1)}, f32[8,128]{1,0:T(8,128)S(1)}, /*index=5*/s32[8,128]{1,0:T(8,128)S(1)}) custom-call(s32[25]{0:T(128)S(1)} %pad_add_fusion.info_ref, f32[864,128]{1,0:T(8,128)S(1)} %get-tuple-element.15.own_ref, ...), custom_call_target="tpu_custom_call" | custom-call | flops 1 | bytes 1 | tf_op jit(solution)/shard_map/begin/pallas_call | solution.py:705
  40.9 1.8 %first.1.refs_1_.refs_3_ = f32[776,128]{1,0:T(8,128)S(1)} custom-call(s32[8,128]{1,0:T(8,128)S(1)} %get-tuple-element.17.refs_0_, f32[768,128]{1,0:T(8,128)S(1)} %get-tuple-element.18.refs_1_, f32[512,128]{1,0:T(8,128)S(1)} %get-tuple-element.19.refs_2_.refs_5_, f32[8,128]{1,0:T(8,128)S(1)} %get-tuple-element.20.refs_3_, f32[128,1024]{1,0:T(8,128)S(1)} %bitcast.19, ...), custom_call_target="tpu_custom_call" | custom-call | tf_op jit(solution)/shard_map/first/pallas_call | solution.py:723
  42.8 1.7 %collective-permute-done.11.refs_2_ = f32[776,128]{1,0:T(8,128)S(1)} collective-permute-done((f32[776,128]{1,0:T(8,128)S(1)}, f32[776,128]{1,0:T(8,128)S(1)}, u32[]{:S(2)}, u32[]{:S(2)}) %collective-permute-start.11) | collective-permute-done | bytes 397344 | tf_op jit(solution)/shard_map/ppermute | solution.py:653
  44.5 2.6 %next.2.refs_1_.refs_3_ = f32[776,128]{1,0:T(8,128)S(1)} custom-call(s32[8,128]{1,0:T(8,128)S(1)} %get-tuple-element.17.refs_0_, f32[776,128]{1,0:T(8,128)S(1)} %first.1.refs_1_.refs_3_, f32[776,128]{1,0:T(8,128)S(1)} %collective-permute-done.11.refs_2_, f32[768,128]{1,0:T(8,128)S(1)} %get-tuple-element.23.refs_3_, ...), custom_call_target="tpu_custom_call" | custom-call | tf_op jit(solution)/shard_map/next/pallas_call | solution.py:734
  47.4 1.6 %collective-permute-done.12.refs_2_ = f32[776,128]{1,0:T(8,128)S(1)} collective-permute-done((f32[776,128]{1,0:T(8,128)S(1)}, f32[776,128]{1,0:T(8,128)S(1)}, u32[]{:S(2)}, u32[]{:S(2)}) %collective-permute-start.12) | collective-permute-done | bytes 397344 | tf_op jit(solution)/shard_map/ppermute | solution.py:653
  48.9 2.6 %next.3.refs_1_ = f32[776,128]{1,0:T(8,128)S(1)} custom-call(s32[8,128]{1,0:T(8,128)S(1)} %get-tuple-element.17.refs_0_, f32[776,128]{1,0:T(8,128)S(1)} %next.2.refs_1_.refs_3_, f32[776,128]{1,0:T(8,128)S(1)} %collective-permute-done.12.refs_2_, f32[776,128]{1,0:T(8,128)S(1)} %first.1.refs_1_.refs_3_, f32[768,128]{1,0:T(8,128)S(1)} %get-tuple-element.24.refs_4_, ...), custom_call_target="tpu_custom_call" | custom-call | tf_op jit(solution)/shard_map/next/pallas_call | solution.py:734
  51.5 0.2 collective-permute-start.13
  51.8 1.6 %collective-permute-done.13.refs_2_ = f32[776,128]{1,0:T(8,128)S(1)} collective-permute-done((f32[776,128]{1,0:T(8,128)S(1)}, f32[776,128]{1,0:T(8,128)S(1)}, u32[]{:S(2)}, u32[]{:S(2)}) %collective-permute-start.13) | collective-permute-done | bytes 397344 | tf_op jit(solution)/shard_map/ppermute | solution.py:653
  53.3 1.6 %last.1 = f32[192,128]{1,0:T(8,128)} custom-call(s32[8,128]{1,0:T(8,128)S(1)} %get-tuple-element.17.refs_0_, f32[776,128]{1,0:T(8,128)S(1)} %next.3.refs_1_, f32[776,128]{1,0:T(8,128)S(1)} %collective-permute-done.13.refs_2_, f32[776,128]{1,0:T(8,128)S(1)} %next.2.refs_1_.refs_3_, f32[768,128]{1,0:T(8,128)S(1)} %get-tuple-element.24.refs_4_, ...), custom_call_target="tpu_custom_call" | custom-call | tf_op jit(solution)/shard_map/last/pallas_call | solution.py:734
  (16 shorter events, 0.6 us)
Async XLA Ops:
  0.0 22.5 %collective-permute-start.8 = (f32[128,1024]{1,0:T(8,128)}, f32[128,1024]{1,0:T(8,128)S(1)}, u32[]{:S(2)}, u32[]{:S(2)}) collective-permute-start(f32[128,1024]{1,0:T(8,128)} %bitcast.16), channel_id=1, source_target_pairs={{0,16},{4,20},{8,24},{12,28},{16,0},{20,4},{24,8},{28,12},{1,17},{... | collective-permute-start | bytes 1572872 | tf_op jit(solution)/shard_map/ppermute | solution.py:653
  3.0 19.5 %collective-permute-start.7 = (f32[128,1024]{1,0:T(8,128)}, f32[128,1024]{1,0:T(8,128)S(1)}, u32[]{:S(2)}, u32[]{:S(2)}) collective-permute-start(f32[128,1024]{1,0:T(8,128)} %bitcast.17), channel_id=1, source_target_pairs={{0,8},{4,12},{8,0},{12,4},{16,24},{20,28},{24,16},{28,20},{1,9},{5... | collective-permute-start | bytes 1572872 | tf_op jit(solution)/shard_map/ppermute | solution.py:653
  5.9 14.4 %collective-permute-start.2 = (f32[264,128]{1,0:T(8,128)S(1)}, f32[264,128]{1,0:T(8,128)S(1)}, u32[]{:S(2)}, u32[]{:S(2)}) collective-permute-start(f32[264,128]{1,0:T(8,128)S(1)} %pack.1.refs_0_), channel_id=1, source_target_pairs={{0,24},{4,28},{8,16},{12,20},{16,8},{20,12},{24,0},{28,4},{1,25},{... | collective-permute-start | bytes 405512 | tf_op jit(solution)/shard_map/ppermute | solution.py:653
  6.0 14.9 %collective-permute-start.1 = (f32[264,128]{1,0:T(8,128)S(1)}, f32[264,128]{1,0:T(8,128)S(1)}, u32[]{:S(2)}, u32[]{:S(2)}) collective-permute-start(f32[264,128]{1,0:T(8,128)S(1)} %pack.1.refs_0_), channel_id=1, source_target_pairs={{0,16},{4,20},{8,24},{12,28},{16,0},{20,4},{24,8},{28,12},{1,17},{... | collective-permute-start | bytes 405512 | tf_op jit(solution)/shard_map/ppermute | solution.py:653
  8.0 14.4 %collective-permute-start = (f32[264,128]{1,0:T(8,128)S(1)}, f32[264,128]{1,0:T(8,128)S(1)}, u32[]{:S(2)}, u32[]{:S(2)}) collective-permute-start(f32[264,128]{1,0:T(8,128)S(1)} %pack.1.refs_0_), channel_id=1, source_target_pairs={{0,8},{4,12},{8,0},{12,4},{16,24},{20,28},{24,16},{28,20},{1,9},{5... | collective-permute-start | bytes 405512 | tf_op jit(solution)/shard_map/ppermute | solution.py:653
  22.4 15.9 %collective-permute-start.3 = (f32[864,128]{1,0:T(8,128)S(1)}, f32[864,128]{1,0:T(8,128)S(1)}, u32[]{:S(2)}, u32[]{:S(2)}) collective-permute-start(f32[864,128]{1,0:T(8,128)S(1)} %get-tuple-element.15.own_ref), channel_id=1, source_target_pairs={{0,4},{4,0},{8,12},{12,8},{16,20},{20,16},{24,28},{28,24},{1,5},{5... | collective-permute-start | bytes 1327112 | tf_op jit(solution)/shard_map/ppermute | solution.py:653
  22.5 18.3 %collective-permute-start.9 = (f32[64,1024]{1,0:T(8,128)S(1)}, f32[64,1024]{1,0:T(8,128)S(1)}, u32[]{:S(2)}, u32[]{:S(2)}) collective-permute-start(f32[64,1024]{1,0:T(8,128)S(1)} %get-tuple-element.21), channel_id=1, source_target_pairs={{0,16},{4,20},{8,24},{12,28},{16,0},{20,4},{24,8},{28,12},{1,17},{... | collective-permute-start | bytes 786440 | tf_op jit(solution)/shard_map/ppermute | solution.py:653
  22.9 18.0 %collective-permute-start.10 = (f32[64,1024]{1,0:T(8,128)S(1)}, f32[64,1024]{1,0:T(8,128)S(1)}, u32[]{:S(2)}, u32[]{:S(2)}) collective-permute-start(f32[64,1024]{1,0:T(8,128)S(1)} %get-tuple-element.22), channel_id=1, source_target_pairs={{0,8},{4,12},{8,0},{12,4},{16,24},{20,28},{24,16},{28,20},{1,9},{5... | collective-permute-start | bytes 786440 | tf_op jit(solution)/shard_map/ppermute | solution.py:653
  24.6 6.8 %collective-permute-start.6 = (f32[192,128]{1,0:T(8,128)S(1)}, f32[192,128]{1,0:T(8,128)S(1)}, u32[]{:S(2)}, u32[]{:S(2)}) collective-permute-start(f32[192,128]{1,0:T(8,128)S(1)} %get-tuple-element.16.refs_0_), channel_id=1, source_target_pairs={{0,3},{1,0},{2,1},{3,2},{4,7},{5,4},{6,5},{7,6},{8,11},{9,8},{10,9... | collective-permute-start | bytes 294920 | tf_op jit(solution)/shard_map/ppermute | solution.py:688
  28.9 7.5 %collective-permute-start.5 = (f32[192,128]{1,0:T(8,128)S(1)}, f32[192,128]{1,0:T(8,128)S(1)}, u32[]{:S(2)}, u32[]{:S(2)}) collective-permute-start(f32[192,128]{1,0:T(8,128)S(1)} %get-tuple-element.16.refs_0_), channel_id=1, source_target_pairs={{0,2},{1,3},{2,0},{3,1},{4,6},{5,7},{6,4},{7,5},{8,10},{9,11},{10,... | collective-permute-start | bytes 294920 | tf_op jit(solution)/shard_map/ppermute | solution.py:688
  31.4 6.9 %collective-permute-start.4 = (f32[192,128]{1,0:T(8,128)S(1)}, f32[192,128]{1,0:T(8,128)S(1)}, u32[]{:S(2)}, u32[]{:S(2)}) collective-permute-start(f32[192,128]{1,0:T(8,128)S(1)} %get-tuple-element.16.refs_0_), channel_id=1, source_target_pairs={{0,1},{1,2},{2,3},{3,0},{4,5},{5,6},{6,7},{7,4},{8,9},{9,10},{10,1... | collective-permute-start | bytes 294920 | tf_op jit(solution)/shard_map/ppermute | solution.py:688
  31.5 9.4 %copy-start = (f32[1,8,2,8,1024]{4,3,2,1,0:T(8,128)S(1)}, f32[1,8,2,8,1024]{4,3,2,1,0:T(8,128)}, u32[]{:S(2)}) copy-start(f32[1,8,2,8,1024]{4,3,2,1,0:T(8,128)} %param.9) | copy-start | bytes 1572868
  42.7 1.8 %collective-permute-start.11 = (f32[776,128]{1,0:T(8,128)S(1)}, f32[776,128]{1,0:T(8,128)S(1)}, u32[]{:S(2)}, u32[]{:S(2)}) collective-permute-start(f32[776,128]{1,0:T(8,128)S(1)} %first.1.refs_1_.refs_3_), channel_id=1, source_target_pairs={{0,4},{4,0},{8,12},{12,8},{16,20},{20,16},{24,28},{28,24},{1,5},{5... | collective-permute-start | bytes 1191944 | tf_op jit(solution)/shard_map/ppermute | solution.py:653
  47.1 1.8 %collective-permute-start.12 = (f32[776,128]{1,0:T(8,128)S(1)}, f32[776,128]{1,0:T(8,128)S(1)}, u32[]{:S(2)}, u32[]{:S(2)}) collective-permute-start(f32[776,128]{1,0:T(8,128)S(1)} %next.2.refs_1_.refs_3_), channel_id=1, source_target_pairs={{0,4},{4,0},{8,12},{12,8},{16,20},{20,16},{24,28},{28,24},{1,5},{5... | collective-permute-start | bytes 1191944 | tf_op jit(solution)/shard_map/ppermute | solution.py:653
  51.5 1.8 %collective-permute-start.13 = (f32[776,128]{1,0:T(8,128)S(1)}, f32[776,128]{1,0:T(8,128)S(1)}, u32[]{:S(2)}, u32[]{:S(2)}) collective-permute-start(f32[776,128]{1,0:T(8,128)S(1)} %next.3.refs_1_), channel_id=1, source_target_pairs={{0,4},{4,0},{8,12},{12,8},{16,20},{20,16},{24,28},{28,24},{1,5},{5... | collective-permute-start | bytes 1191944 | tf_op jit(solution)/shard_map/ppermute | solution.py:653

commit v5 on v4

--- a/solution.py
+++ b/solution.py
@@ -352,7 +352,10 @@
                         spot = (slab * 6 + index) * NY
                         beside = beside + y_ref[spot : spot + NY, :]
                 lap = lap + stencil_weights[distance] * beside
-            value = scale * ((v_ref[rows, :] - filter_center) * own - 0.5 * lap)
+            if v_ref is None:
+                value = scale * (-filter_center * own - 0.5 * lap)
+            else:
+                value = scale * ((v_ref[rows, :] - filter_center) * own - 0.5 * lap)
             if prev_ref is not None:
                 value = value - prev_ref[rows, :]
             out_ref[rows, :] = value
@@ -361,8 +364,8 @@
 def pack_kernel(dims, *refs):
     n, cap, nproj, foot, chunk = dims
     lanes = n * chunk
-    sources, pack_ref, scratch = refs[:6], refs[6], refs[7:]
-    p_ref, off_ref, atom_ref, dmat_ref, r_ref, sems = scratch
+    sources, (pack_ref, p_ref), scratch = refs[:6], refs[6:8], refs[8:]
+    off_ref, atom_ref, dmat_ref, r_ref, sems = scratch
     small = pack_ref.shape[0] - SMALL
     targets = (
         pack_ref.at[0:SLAB, :],
@@ -400,7 +403,7 @@
 
 
 def sort_kernel(*refs):
-    packs, (pair_ref, v_ref) = refs[:-2], refs[-2:]
+    packs, (pair_ref, v_ref) = refs[:-4], refs[-3:-1]
     small = packs[0].shape[0] - SMALL
     size = SLAB + SMALL
     for local, pack in enumerate(packs):
@@ -415,19 +418,12 @@
     bottom_ref[...] = y_ref[rows:, :]
 
 
-def begin_kernel(dims, nband, info_ref, own_ref, got_ref, *refs):
+def begin_kernel(dims, info_ref, own_ref, got_ref, *refs):
     n, cap, nproj, foot, chunk = dims
     half = n // 2
-    v_pieces, refs = refs[:nband], refs[nband:]
-    part_ref, y_ref, v_ref, w_ref, c_ref, int_ref, other_ref, pad_ref, dmat_ref = refs
+    part_ref, y_ref, w_ref, c_ref, int_ref, other_ref, pad_ref, dmat_ref = refs
     lanes = n * chunk
     size = SLAB + SMALL
-    piece = NY // nband
-    for back in range(nband):
-        at = lax.rem(info_ref[4 * half + n] - back + nband, nband) * piece
-        for plane in range(6 * half):
-            spot = pl.multiple_of(plane * NY + at, 8)
-            v_ref[pl.ds(spot, piece), :] = v_pieces[back][plane * piece : (plane + 1) * piece, :]
     c_rows, atom_rows, start_rows = [], [], []
     for group, source in enumerate((own_ref, got_ref)):
         for local in range(half):
@@ -451,6 +447,7 @@
         for side in range(2):
             value = info_ref[(2 + side) * half + local]
             table = jnp.where(lane == side * half + local, value, table)
+    table = jnp.where(lane == 2 * half, info_ref[4 * half + n], table)
     int_ref[half : half + 1, :] = table
     int_ref[half + 1 :, :] = jnp.zeros((8 - half - 1, 128), jnp.int32)
 
@@ -461,7 +458,7 @@
         )
 
     stencil(
-        y_ref, other_ref, v_ref, None, part_ref, pad_ref, half, 1.0 / filter_half_width, bases
+        y_ref, other_ref, None, None, part_ref, pad_ref, half, 1.0 / filter_half_width, bases
     )
     square = (lanes, 128)
     diagonal = iota(square, 0) == iota(square, 1)
@@ -559,6 +556,22 @@
     return lambda slab, slot: slab * SLAB + int_s[slab, slot * nproj]
 
 
+def potential_kernel(nband, table_ref, part_ref, y_ref, *refs):
+    pieces, (out_ref, v_ref, int_s, sem) = refs[:nband], refs[nband:]
+    copy = pltpu.make_async_copy(table_ref, int_s, sem)
+    copy.start()
+    copy.wait()
+    scale = 1.0 / filter_half_width
+    piece = NY // nband
+    for back in range(nband):
+        at = lax.rem(int_s[4, 8] - back + nband, nband) * piece
+        for plane in range(part_ref.shape[0] // NY):
+            spot = pl.ds(pl.multiple_of(plane * NY + at, 8), piece)
+            value = pieces[back][plane * piece : (plane + 1) * piece, :]
+            v_ref[spot, :] = value
+            out_ref[spot, :] = part_ref[spot, :] + scale * (value * y_ref[spot, :])
+
+
 def first_kernel(dims, *refs):
     n, cap, nproj, foot, chunk = dims
     half = n // 2
@@ -645,6 +658,7 @@
     HBM = pl.BlockSpec(memory_space=pltpu.HBM)
     small = pl.CostEstimate(flops=1, bytes_accessed=1, transcendentals=0)
     large = pl.CostEstimate(flops=10**10, bytes_accessed=1, transcendentals=0)
+    larger = pl.CostEstimate(flops=10**10, bytes_accessed=1, transcendentals=0)
 
     def shape(rows, dtype=f32):
         return jax.ShapeDtypeStruct((rows, 128), dtype)
@@ -654,13 +668,15 @@
 
     sources = (psi.reshape(SLAB, 128), p, offsets[0].T, intersection[0].T, couplings, v_piece)
     sources = [pltpu.with_memory_space_constraint(x, pltpu.HBM) for x in sources]
-    pack = pl.pallas_call(
+    pack, p = pl.pallas_call(
         functools.partial(pack_kernel, dims),
-        out_shape=shape(SLAB + v_piece.shape[0] + SMALL),
+        out_shape=(
+            shape(SLAB + v_piece.shape[0] + SMALL),
+            jax.ShapeDtypeStruct(p.shape, f32),
+        ),
         in_specs=[HBM] * 6,
-        out_specs=VMEM,
+        out_specs=(VMEM, VMEM),
         scratch_shapes=[
-            pltpu.VMEM(p.shape, f32),
             pltpu.SMEM((cap, n), jnp.int32),
             pltpu.SMEM((cap, n), jnp.int32),
             pltpu.VMEM(couplings.shape, f32),
@@ -672,15 +688,20 @@
         name="pack",
     )(*sources)
     packs = [pack] + [swap(pack, 2 * local) for local in range(1, half)]
-    own, v_piece = pl.pallas_call(
+    own, v_piece, p = pl.pallas_call(
         sort_kernel,
-        out_shape=(shape(half * (SLAB + SMALL)), shape(half * v_piece.shape[0])),
-        in_specs=[VMEM] * half,
-        out_specs=(VMEM, VMEM),
+        out_shape=(
+            shape(half * (SLAB + SMALL)),
+            shape(half * v_piece.shape[0]),
+            jax.ShapeDtypeStruct(p.shape, f32),
+        ),
+        in_specs=[VMEM] * (half + 1),
+        out_specs=(VMEM,) * 3,
+        input_output_aliases={half: 2},
         compiler_params=params,
         cost_estimate=small,
         name="sort",
-    )(*packs)
+    )(*packs, p)
     got = swap(own, 1)
     pieces = [v_piece]
     for back in range(1, nband):
@@ -702,24 +723,33 @@
     padded = pltpu.VMEM((half * 6 * (NY + 16), 128), f32)
     row_scratch = pltpu.VMEM((half * lanes, 128), f32)
     ints = [pltpu.SMEM((8, 128), jnp.int32), pltpu.SemaphoreType.DMA(())]
-    part, previous, v, w, c, table = pl.pallas_call(
-        functools.partial(begin_kernel, dims, nband),
+    part, previous, w, c, table = pl.pallas_call(
+        functools.partial(begin_kernel, dims),
         out_shape=(
-            shape(half * SLAB),
             shape(half * SLAB),
             shape(half * SLAB),
             shape(half * lanes),
             shape(n),
             shape(8, jnp.int32),
         ),
-        in_specs=[SMEM] + [VMEM] * (2 + nband),
-        out_specs=(VMEM,) * 6,
+        in_specs=[SMEM] + [VMEM] * 2,
+        out_specs=(VMEM,) * 5,
         scratch_shapes=[other, padded, pltpu.VMEM((n, 2 * nproj, 128), f32)],
         compiler_params=params,
         cost_estimate=small,
         name="begin",
-    )(info, own, got, *pieces)
+    )(info, own, got)
     sent = shape(half * SLAB + 8)
+    part, v = pl.pallas_call(
+        functools.partial(potential_kernel, nband),
+        out_shape=(shape(half * SLAB), shape(half * SLAB)),
+        in_specs=[VMEM] * (3 + nband),
+        out_specs=(VMEM, VMEM),
+        scratch_shapes=ints,
+        compiler_params=params,
+        cost_estimate=larger,
+        name="potential",
+    )(table, part, previous, *pieces)
     y = pl.pallas_call(
         functools.partial(first_kernel, dims),
         out_shape=sent,

time: 55.2 us -> 49 us (0.89)
  waiting for transfers between devices: 27.1 us -> 20.5 us
  Pallas kernels: 12.7 us -> 13.4 us
    ppermute x3, waiting for transfers between devices: 9.34 us -> 0.01 us  [chip_form(): pieces.append(lax.ppermute(v_piece, 'band', ring))]
    ppermute x11, waiting for transfers between devices: 17.8 us -> 20.5 us  [swap(): return lax.ppermute(x, 'domain', [(i, i ^ step) for i in range(n)])]
    ppermute x11, starting transfers between devices: 10.6 us -> 9.34 us  [swap(): return lax.ppermute(x, 'domain', [(i, i ^ step) for i in range(n)])]
    ppermute x3, starting transfers between devices: 3.61 us -> 4.73 us  [chip_form(): pieces.append(lax.ppermute(v_piece, 'band', ring))]
    pallas_call x2 -> x3, Pallas kernels: 3.95 us -> 4.61 us  [the longest x1 2.47 us: chip_form(): pl.pallas_call(functools.partial(begin_kernel, dims), out_shape=(shape(ha...]
  transfers between devices with their start and end apart: 14 -> 14, of which waited for: 9 -> 10; matrix products, arithmetic and copies ran while one was open for 1% -> 2% of each run, Pallas kernels for 7% -> 7%
where the time goes in v5:
time: 49 us; the launch traced here: 48.9 us
  waiting for transfers between devices  20.5 us (42%)
  starting transfers between devices  14.1 us (29%)
  Pallas kernels  13.4 us (27%)
  local copies, waits for them, and re-layouts  0.69 us (1%)
    ppermute x11, waiting for transfers between devices, swap(): return lax.ppermute(x, 'domain', [(i, i ^ step) for i in range(n)])  20.5 us
    ppermute x11, starting transfers between devices, swap(): return lax.ppermute(x, 'domain', [(i, i ^ step) for i in range(n)])  9.34 us
    pallas_call x3, Pallas kernels, chip_form(): pl.pallas_call(functools.partial(chip_kernel, dims, last), out_shape=shap...  6.9 us
    ppermute x3, starting transfers between devices, chip_form(): pieces.append(lax.ppermute(v_piece, 'band', ring))  4.73 us
    pallas_call x1, Pallas kernels, chip_form(): pl.pallas_call(functools.partial(begin_kernel, dims), out_shape=(shape(ha...  2.47 us
    pallas_call x1, Pallas kernels, chip_form(): pl.pallas_call(functools.partial(first_kernel, dims), out_shape=sent, in_...  1.83 us
    pallas_call x1, Pallas kernels, chip_form(): pl.pallas_call(functools.partial(pack_kernel, dims), out_shape=(shape(SLA...  1.4 us
  transfers between devices with their start and end apart: 14, of which 10 were waited for; matrix products, arithmetic and copies ran while one was open for 2% of the time, Pallas kernels for 7%

profile of v5, /device:TPU:0, one launch (start us, length us, event | category | flops | bytes accessed | tf_op | source)
XLA Modules:
  0.0 48.9 jit_solution(165116546514617915)
XLA Ops:
  0.0 1.4 %pack.1 = (f32[264,128]{1,0:T(8,128)S(1)}, f32[128,1024]{1,0:T(8,128)S(1)}) custom-call(f32[192,128]{1,0:T(8,128)} %bitcast.17, f32[128,1024]{1,0:T(8,128)} %bitcast.16, s32[2,8]{1,0:T(2,128)} %bitcast.20, s32[2,8]{1,0:T(2,128)} %bitcast.21, f32[64,32]{1,0:T(8,128)} %bitcast.18, f32[48,128]{1,0:T(8,128)} %bitcast.19), custom_call_target="tpu_custom_call" | custom-call | flops 1 | bytes 1 | tf_op jit(solution)/shard_map/pack/pallas_call | solution.py:671
  1.4 4.0 %collective-permute-start.2 = (f32[264,128]{1,0:T(8,128)S(1)}, f32[264,128]{1,0:T(8,128)S(1)}, u32[]{:S(2)}, u32[]{:S(2)}) collective-permute-start(f32[264,128]{1,0:T(8,128)S(1)} %get-tuple-element.19.refs_0_), channel_id=1, source_target_pairs={{0,24},{4,28},{8,16},{12,20},{16,8},{20,12},{24,0},{28,4},{1,25},{... | collective-permute-start | bytes 405512 | tf_op jit(solution)/shard_map/ppermute | solution.py:667
  5.4 0.5 %collective-permute-start.1 = (f32[264,128]{1,0:T(8,128)S(1)}, f32[264,128]{1,0:T(8,128)S(1)}, u32[]{:S(2)}, u32[]{:S(2)}) collective-permute-start(f32[264,128]{1,0:T(8,128)S(1)} %get-tuple-element.19.refs_0_), channel_id=1, source_target_pairs={{0,16},{4,20},{8,24},{12,28},{16,0},{20,4},{24,8},{28,12},{1,17},{... | collective-permute-start | bytes 405512 | tf_op jit(solution)/shard_map/ppermute | solution.py:667
  6.0 3.3 %collective-permute-done.2.refs_3_ = f32[264,128]{1,0:T(8,128)S(1)} collective-permute-done((f32[264,128]{1,0:T(8,128)S(1)}, f32[264,128]{1,0:T(8,128)S(1)}, u32[]{:S(2)}, u32[]{:S(2)}) %collective-permute-start.2) | collective-permute-done | bytes 135200 | tf_op jit(solution)/shard_map/ppermute | solution.py:667
  9.4 2.5 %collective-permute-done.1.refs_2_ = f32[264,128]{1,0:T(8,128)S(1)} collective-permute-done((f32[264,128]{1,0:T(8,128)S(1)}, f32[264,128]{1,0:T(8,128)S(1)}, u32[]{:S(2)}, u32[]{:S(2)}) %collective-permute-start.1) | collective-permute-done | bytes 135200 | tf_op jit(solution)/shard_map/ppermute | solution.py:667
  12.1 1.5 %collective-permute-start.8 = (f32[128,1024]{1,0:T(8,128)S(1)}, f32[128,1024]{1,0:T(8,128)S(1)}, u32[]{:S(2)}, u32[]{:S(2)}) collective-permute-start(f32[128,1024]{1,0:T(8,128)S(1)} %get-tuple-element.29.refs_4_.refs_6_), channel_id=1, source_target_pairs={{0,16},{4,20},{8,24},{12,28},{16,0},{20,4},{24,8},{28,12},{1,17},{... | collective-permute-start | bytes 1572872 | tf_op jit(solution)/shard_map/ppermute | solution.py:667
  13.7 0.7 %collective-permute-start.7 = (f32[128,1024]{1,0:T(8,128)S(1)}, f32[128,1024]{1,0:T(8,128)S(1)}, u32[]{:S(2)}, u32[]{:S(2)}) collective-permute-start(f32[128,1024]{1,0:T(8,128)S(1)} %get-tuple-element.29.refs_4_.refs_6_), channel_id=1, source_target_pairs={{0,8},{4,12},{8,0},{12,4},{16,24},{20,28},{24,16},{28,20},{1,9},{5... | collective-permute-start | bytes 1572872 | tf_op jit(solution)/shard_map/ppermute | solution.py:667
  14.4 0.7 %dynamic-slice_bitcast_fusion = s32[24]{0:T(128)S(1)} fusion(s32[8,24]{1,0:T(8,128)} %constant.15.clone, s32[]{:T(128)S(6)} %select_n.3), kind=kLoop, calls=%fused_computation.1 | loop fusion | bytes 196 | tf_op jit(solution)/shard_map/squeeze | solution.py:653
  15.1 3.7 %collective-permute-start.6 = (f32[192,128]{1,0:T(8,128)S(1)}, f32[192,128]{1,0:T(8,128)S(1)}, u32[]{:S(2)}, u32[]{:S(2)}) collective-permute-start(f32[192,128]{1,0:T(8,128)S(1)} %get-tuple-element.25.refs_0_), channel_id=1, source_target_pairs={{0,3},{1,0},{2,1},{3,2},{4,7},{5,4},{6,5},{7,6},{8,11},{9,8},{10,9... | collective-permute-start | bytes 294920 | tf_op jit(solution)/shard_map/ppermute | solution.py:709
  18.8 1.0 %collective-permute-start.4 = (f32[192,128]{1,0:T(8,128)S(1)}, f32[192,128]{1,0:T(8,128)S(1)}, u32[]{:S(2)}, u32[]{:S(2)}) collective-permute-start(f32[192,128]{1,0:T(8,128)S(1)} %get-tuple-element.25.refs_0_), channel_id=1, source_target_pairs={{0,1},{1,2},{2,3},{3,0},{4,5},{5,6},{6,7},{7,4},{8,9},{9,10},{10,1... | collective-permute-start | bytes 294920 | tf_op jit(solution)/shard_map/ppermute | solution.py:709
  19.9 2.5 %begin.1 = (f32[768,128]{1,0:T(8,128)S(1)}, f32[768,128]{1,0:T(8,128)S(1)}, f32[512,128]{1,0:T(8,128)S(1)}, f32[8,128]{1,0:T(8,128)S(1)}, s32[8,128]{1,0:T(8,128)S(1)}) custom-call(s32[25]{0:T(128)S(1)} %pad_add_fusion.info_ref, f32[864,128]{1,0:T(8,128)S(1)} %get-tuple-element.21.own_ref, f32[864,128]{1,0:T(8,128)S(1)} %collective-permute-done.3.got_ref), custom_call_target="tpu_custom_call" | custom-call | flops 1 | bytes 1 | tf_op jit(solution)/shard_map/begin/pallas_call | solution.py:726
  22.3 3.5 %collective-permute-done.8.y_ref.refs_6_.refs_8_ = f32[128,1024]{1,0:T(8,128)S(1)} collective-permute-done((f32[128,1024]{1,0:T(8,128)S(1)}, f32[128,1024]{1,0:T(8,128)S(1)}, u32[]{:S(2)}, u32[]{:S(2)}) %collective-permute-start.8) | collective-permute-done | bytes 524320 | tf_op jit(solution)/shard_map/ppermute | solution.py:667
  25.8 1.4 %collective-permute-done.7.x_ref.refs_5_.refs_7_ = f32[128,1024]{1,0:T(8,128)S(1)} collective-permute-done((f32[128,1024]{1,0:T(8,128)S(1)}, f32[128,1024]{1,0:T(8,128)S(1)}, u32[]{:S(2)}, u32[]{:S(2)}) %collective-permute-start.7) | collective-permute-done | bytes 524320 | tf_op jit(solution)/shard_map/ppermute | solution.py:667
  27.3 0.4 collective-permute-start.9
  27.7 1.6 %collective-permute-start.10 = (f32[64,1024]{1,0:T(8,128)S(1)}, f32[64,1024]{1,0:T(8,128)S(1)}, u32[]{:S(2)}, u32[]{:S(2)}) collective-permute-start(f32[64,1024]{1,0:T(8,128)S(1)} %get-tuple-element.31), channel_id=1, source_target_pairs={{0,8},{4,12},{8,0},{12,4},{16,24},{20,28},{24,16},{28,20},{1,9},{5... | collective-permute-start | bytes 786440 | tf_op jit(solution)/shard_map/ppermute | solution.py:667
  29.4 0.7 %potential.1 = (f32[768,128]{1,0:T(8,128)S(1)}, f32[768,128]{1,0:T(8,128)S(1)}) custom-call(s32[8,128]{1,0:T(8,128)S(1)} %get-tuple-element.22.table_ref.refs_0_, f32[768,128]{1,0:T(8,128)S(1)} %get-tuple-element.23.part_ref, f32[768,128]{1,0:T(8,128)S(1)} %get-tuple-element.24.y_ref.refs_3_, f32[192,128]{1,0:T(8,128)S(1)} %get-tuple-element.25.refs_0_, ...), custom_call_target="tpu_custom_call" | custom-call | flops 10000000000 | bytes 1 | tf_op jit(solution)/shard_map/potential/pallas_call | solution.py:743
  30.1 4.3 %collective-permute-done.9.refs_7_.refs_9_ = f32[64,1024]{1,0:T(8,128)S(1)} collective-permute-done((f32[64,1024]{1,0:T(8,128)S(1)}, f32[64,1024]{1,0:T(8,128)S(1)}, u32[]{:S(2)}, u32[]{:S(2)}) %collective-permute-start.9) | collective-permute-done | bytes 262176 | tf_op jit(solution)/shard_map/ppermute | solution.py:667
  34.7 1.8 %first.1.refs_1_.refs_3_ = f32[776,128]{1,0:T(8,128)S(1)} custom-call(s32[8,128]{1,0:T(8,128)S(1)} %get-tuple-element.22.table_ref.refs_0_, f32[768,128]{1,0:T(8,128)S(1)} %get-tuple-element.26.refs_1_, f32[512,128]{1,0:T(8,128)S(1)} %get-tuple-element.27.refs_2_.refs_5_, f32[8,128]{1,0:T(8,128)S(1)} %get-tuple-element.28.refs_3_, ...), custom_call_target="tpu_custom_call" | custom-call | tf_op jit(solution)/shard_map/first/pallas_call | solution.py:753
  36.6 1.7 %collective-permute-done.11.refs_2_ = f32[776,128]{1,0:T(8,128)S(1)} collective-permute-done((f32[776,128]{1,0:T(8,128)S(1)}, f32[776,128]{1,0:T(8,128)S(1)}, u32[]{:S(2)}, u32[]{:S(2)}) %collective-permute-start.11) | collective-permute-done | bytes 397344 | tf_op jit(solution)/shard_map/ppermute | solution.py:667
  38.4 2.6 %next.2.refs_1_.refs_3_ = f32[776,128]{1,0:T(8,128)S(1)} custom-call(s32[8,128]{1,0:T(8,128)S(1)} %get-tuple-element.22.table_ref.refs_0_, f32[776,128]{1,0:T(8,128)S(1)} %first.1.refs_1_.refs_3_, f32[776,128]{1,0:T(8,128)S(1)} %collective-permute-done.11.refs_2_, f32[768,128]{1,0:T(8,128)S(1)} %get-tuple-element.24.y_ref.refs_3_, ...), custom_call_target="tpu_custom_call" | custom-call | tf_op jit(solution)/shard_map/next/pallas_call | solution.py:764
  41.2 1.6 %collective-permute-done.12.refs_2_ = f32[776,128]{1,0:T(8,128)S(1)} collective-permute-done((f32[776,128]{1,0:T(8,128)S(1)}, f32[776,128]{1,0:T(8,128)S(1)}, u32[]{:S(2)}, u32[]{:S(2)}) %collective-permute-start.12) | collective-permute-done | bytes 397344 | tf_op jit(solution)/shard_map/ppermute | solution.py:667
  42.8 2.6 %next.3.refs_1_ = f32[776,128]{1,0:T(8,128)S(1)} custom-call(s32[8,128]{1,0:T(8,128)S(1)} %get-tuple-element.22.table_ref.refs_0_, f32[776,128]{1,0:T(8,128)S(1)} %next.2.refs_1_.refs_3_, f32[776,128]{1,0:T(8,128)S(1)} %collective-permute-done.12.refs_2_, f32[776,128]{1,0:T(8,128)S(1)} %first.1.refs_1_.refs_3_, f32[768,128]{1,0:T(8,128)S(1)} %get-tuple-element.32.refs_4_, ...), custom_call_target="tpu_custom_call" | custom-call | tf_op jit(solution)/shard_map/next/pallas_call | solution.py:764
  45.6 1.6 %collective-permute-done.13.refs_2_ = f32[776,128]{1,0:T(8,128)S(1)} collective-permute-done((f32[776,128]{1,0:T(8,128)S(1)}, f32[776,128]{1,0:T(8,128)S(1)}, u32[]{:S(2)}, u32[]{:S(2)}) %collective-permute-start.13) | collective-permute-done | bytes 397344 | tf_op jit(solution)/shard_map/ppermute | solution.py:667
  47.2 1.7 %last.1 = f32[192,128]{1,0:T(8,128)} custom-call(s32[8,128]{1,0:T(8,128)S(1)} %get-tuple-element.22.table_ref.refs_0_, f32[776,128]{1,0:T(8,128)S(1)} %next.3.refs_1_, f32[776,128]{1,0:T(8,128)S(1)} %collective-permute-done.13.refs_2_, f32[776,128]{1,0:T(8,128)S(1)} %next.2.refs_1_.refs_3_, f32[768,128]{1,0:T(8,128)S(1)} %get-tuple-element.32.refs_4_, ...), custom_call_target="tpu_custom_call" | custom-call | tf_op jit(solution)/shard_map/last/pallas_call | solution.py:764
  (15 shorter events, 1.3 us)
Async XLA Ops:
  1.4 8.0 %collective-permute-start.2 = (f32[264,128]{1,0:T(8,128)S(1)}, f32[264,128]{1,0:T(8,128)S(1)}, u32[]{:S(2)}, u32[]{:S(2)}) collective-permute-start(f32[264,128]{1,0:T(8,128)S(1)} %get-tuple-element.19.refs_0_), channel_id=1, source_target_pairs={{0,24},{4,28},{8,16},{12,20},{16,8},{20,12},{24,0},{28,4},{1,25},{... | collective-permute-start | bytes 405512 | tf_op jit(solution)/shard_map/ppermute | solution.py:667
  5.4 6.5 %collective-permute-start.1 = (f32[264,128]{1,0:T(8,128)S(1)}, f32[264,128]{1,0:T(8,128)S(1)}, u32[]{:S(2)}, u32[]{:S(2)}) collective-permute-start(f32[264,128]{1,0:T(8,128)S(1)} %get-tuple-element.19.refs_0_), channel_id=1, source_target_pairs={{0,16},{4,20},{8,24},{12,28},{16,0},{20,4},{24,8},{28,12},{1,17},{... | collective-permute-start | bytes 405512 | tf_op jit(solution)/shard_map/ppermute | solution.py:667
  5.9 6.2 %collective-permute-start = (f32[264,128]{1,0:T(8,128)S(1)}, f32[264,128]{1,0:T(8,128)S(1)}, u32[]{:S(2)}, u32[]{:S(2)}) collective-permute-start(f32[264,128]{1,0:T(8,128)S(1)} %get-tuple-element.19.refs_0_), channel_id=1, source_target_pairs={{0,8},{4,12},{8,0},{12,4},{16,24},{20,28},{24,16},{28,20},{1,9},{5... | collective-permute-start | bytes 405512 | tf_op jit(solution)/shard_map/ppermute | solution.py:667
  12.1 13.7 %collective-permute-start.8 = (f32[128,1024]{1,0:T(8,128)S(1)}, f32[128,1024]{1,0:T(8,128)S(1)}, u32[]{:S(2)}, u32[]{:S(2)}) collective-permute-start(f32[128,1024]{1,0:T(8,128)S(1)} %get-tuple-element.29.refs_4_.refs_6_), channel_id=1, source_target_pairs={{0,16},{4,20},{8,24},{12,28},{16,0},{20,4},{24,8},{28,12},{1,17},{... | collective-permute-start | bytes 1572872 | tf_op jit(solution)/shard_map/ppermute | solution.py:667
  13.7 13.6 %collective-permute-start.7 = (f32[128,1024]{1,0:T(8,128)S(1)}, f32[128,1024]{1,0:T(8,128)S(1)}, u32[]{:S(2)}, u32[]{:S(2)}) collective-permute-start(f32[128,1024]{1,0:T(8,128)S(1)} %get-tuple-element.29.refs_4_.refs_6_), channel_id=1, source_target_pairs={{0,8},{4,12},{8,0},{12,4},{16,24},{20,28},{24,16},{28,20},{1,9},{5... | collective-permute-start | bytes 1572872 | tf_op jit(solution)/shard_map/ppermute | solution.py:667
  14.3 4.5 %collective-permute-start.3 = (f32[864,128]{1,0:T(8,128)S(1)}, f32[864,128]{1,0:T(8,128)S(1)}, u32[]{:S(2)}, u32[]{:S(2)}) collective-permute-start(f32[864,128]{1,0:T(8,128)S(1)} %get-tuple-element.21.own_ref), channel_id=1, source_target_pairs={{0,4},{4,0},{8,12},{12,8},{16,20},{20,16},{24,28},{28,24},{1,5},{5... | collective-permute-start | bytes 1327112 | tf_op jit(solution)/shard_map/ppermute | solution.py:667
  15.1 14.2 %collective-permute-start.6 = (f32[192,128]{1,0:T(8,128)S(1)}, f32[192,128]{1,0:T(8,128)S(1)}, u32[]{:S(2)}, u32[]{:S(2)}) collective-permute-start(f32[192,128]{1,0:T(8,128)S(1)} %get-tuple-element.25.refs_0_), channel_id=1, source_target_pairs={{0,3},{1,0},{2,1},{3,2},{4,7},{5,4},{6,5},{7,6},{8,11},{9,8},{10,9... | collective-permute-start | bytes 294920 | tf_op jit(solution)/shard_map/ppermute | solution.py:709
  18.8 10.5 %collective-permute-start.5 = (f32[192,128]{1,0:T(8,128)S(1)}, f32[192,128]{1,0:T(8,128)S(1)}, u32[]{:S(2)}, u32[]{:S(2)}) collective-permute-start(f32[192,128]{1,0:T(8,128)S(1)} %get-tuple-element.25.refs_0_), channel_id=1, source_target_pairs={{0,2},{1,3},{2,0},{3,1},{4,6},{5,7},{6,4},{7,5},{8,10},{9,11},{10,... | collective-permute-start | bytes 294920 | tf_op jit(solution)/shard_map/ppermute | solution.py:709
  18.8 10.5 %collective-permute-start.4 = (f32[192,128]{1,0:T(8,128)S(1)}, f32[192,128]{1,0:T(8,128)S(1)}, u32[]{:S(2)}, u32[]{:S(2)}) collective-permute-start(f32[192,128]{1,0:T(8,128)S(1)} %get-tuple-element.25.refs_0_), channel_id=1, source_target_pairs={{0,1},{1,2},{2,3},{3,0},{4,5},{5,6},{6,7},{7,4},{8,9},{9,10},{10,1... | collective-permute-start | bytes 294920 | tf_op jit(solution)/shard_map/ppermute | solution.py:709
  27.3 7.1 %collective-permute-start.9 = (f32[64,1024]{1,0:T(8,128)S(1)}, f32[64,1024]{1,0:T(8,128)S(1)}, u32[]{:S(2)}, u32[]{:S(2)}) collective-permute-start(f32[64,1024]{1,0:T(8,128)S(1)} %get-tuple-element.30), channel_id=1, source_target_pairs={{0,16},{4,20},{8,24},{12,28},{16,0},{20,4},{24,8},{28,12},{1,17},{... | collective-permute-start | bytes 786440 | tf_op jit(solution)/shard_map/ppermute | solution.py:667
  27.7 7.0 %collective-permute-start.10 = (f32[64,1024]{1,0:T(8,128)S(1)}, f32[64,1024]{1,0:T(8,128)S(1)}, u32[]{:S(2)}, u32[]{:S(2)}) collective-permute-start(f32[64,1024]{1,0:T(8,128)S(1)} %get-tuple-element.31), channel_id=1, source_target_pairs={{0,8},{4,12},{8,0},{12,4},{16,24},{20,28},{24,16},{28,20},{1,9},{5... | collective-permute-start | bytes 786440 | tf_op jit(solution)/shard_map/ppermute | solution.py:667
  36.6 1.8 %collective-permute-start.11 = (f32[776,128]{1,0:T(8,128)S(1)}, f32[776,128]{1,0:T(8,128)S(1)}, u32[]{:S(2)}, u32[]{:S(2)}) collective-permute-start(f32[776,128]{1,0:T(8,128)S(1)} %first.1.refs_1_.refs_3_), channel_id=1, source_target_pairs={{0,4},{4,0},{8,12},{12,8},{16,20},{20,16},{24,28},{28,24},{1,5},{5... | collective-permute-start | bytes 1191944 | tf_op jit(solution)/shard_map/ppermute | solution.py:667
  41.0 1.8 %collective-permute-start.12 = (f32[776,128]{1,0:T(8,128)S(1)}, f32[776,128]{1,0:T(8,128)S(1)}, u32[]{:S(2)}, u32[]{:S(2)}) collective-permute-start(f32[776,128]{1,0:T(8,128)S(1)} %next.2.refs_1_.refs_3_), channel_id=1, source_target_pairs={{0,4},{4,0},{8,12},{12,8},{16,20},{20,16},{24,28},{28,24},{1,5},{5... | collective-permute-start | bytes 1191944 | tf_op jit(solution)/shard_map/ppermute | solution.py:667
  45.4 1.8 %collective-permute-start.13 = (f32[776,128]{1,0:T(8,128)S(1)}, f32[776,128]{1,0:T(8,128)S(1)}, u32[]{:S(2)}, u32[]{:S(2)}) collective-permute-start(f32[776,128]{1,0:T(8,128)S(1)} %next.3.refs_1_), channel_id=1, source_target_pairs={{0,4},{4,0},{8,12},{12,8},{16,20},{20,16},{24,28},{28,24},{1,5},{5... | collective-permute-start | bytes 1191944 | tf_op jit(solution)/shard_map/ppermute | solution.py:667

commit v6 on v5

--- a/solution.py
+++ b/solution.py
@@ -364,24 +364,28 @@
 def pack_kernel(dims, *refs):
     n, cap, nproj, foot, chunk = dims
     lanes = n * chunk
-    sources, (pack_ref, p_ref), scratch = refs[:6], refs[6:8], refs[8:]
+    sources, (pack_ref, top_ref, bottom_ref), scratch = refs[:6], refs[6:9], refs[9:]
     off_ref, atom_ref, dmat_ref, r_ref, sems = scratch
     small = pack_ref.shape[0] - SMALL
     targets = (
         pack_ref.at[0:SLAB, :],
-        p_ref,
+        top_ref,
+        bottom_ref,
         off_ref,
         atom_ref,
         dmat_ref,
         pack_ref.at[SLAB:small, :],
     )
+    rows = top_ref.shape[0]
+    p_ref = sources[1]
+    sources = (sources[0], p_ref.at[0:rows, :], p_ref.at[rows:, :], *sources[2:6])
     copies = [
         pltpu.make_async_copy(source, target, sems.at[index])
         for index, (source, target) in enumerate(zip(sources, targets))
     ]
     for copy in copies:
         copy.start()
-    for copy in copies[2:]:
+    for copy in copies[3:]:
         copy.wait()
     lane = iota((1, lanes), 1) // nproj
     atoms = jnp.zeros((1, lanes), f32)
@@ -397,13 +401,15 @@
     for group in range(128 // count):
         block = dmat_ref[group * 2 * nproj : (group + 1) * 2 * nproj, :]
         pack_ref[small + 8 :, group * count : (group + 1) * count] = block
-    copies[0].wait()
-    copies[1].wait()
-    pack_ref[small : small + 1, :] = partials(pack_ref, p_ref, off_ref, r_ref, dims)[0:1]
+    for copy in copies[:3]:
+        copy.wait()
+    p_refs, at = [top_ref, bottom_ref], lambda slab, slot: off_ref[slot % cap, slot // cap]
+    fill_rows(dims, 0, pack_ref, p_refs, at, r_ref)
+    pack_ref[small : small + 1, :] = row_sums(r_ref)[0:1, :]
 
 
 def sort_kernel(*refs):
-    packs, (pair_ref, v_ref) = refs[:-4], refs[-3:-1]
+    packs, (pair_ref, v_ref) = refs[:-2], refs[-2:]
     small = packs[0].shape[0] - SMALL
     size = SLAB + SMALL
     for local, pack in enumerate(packs):
@@ -412,10 +418,8 @@
         v_ref[local * (small - SLAB) : (local + 1) * (small - SLAB), :] = pack[SLAB:small, :]
 
 
-def relay_kernel(x_ref, y_ref, top_ref, bottom_ref):
-    rows = top_ref.shape[0]
-    top_ref[...] = x_ref[0:rows, :]
-    bottom_ref[...] = y_ref[rows:, :]
+def relay_kernel(x_ref, out_ref):
+    out_ref[...] = x_ref[...]
 
 
 def begin_kernel(dims, info_ref, own_ref, got_ref, *refs):
@@ -495,10 +499,10 @@
 
 
 def p_rows(p_refs, slab, slot, nproj, tile):
-    ref, at = p_refs[slab], slot * nproj
-    if at >= ref.shape[0]:
-        ref, at = p_refs[slab + 1], at - ref.shape[0]
-    return ref[at : at + nproj, tile * 128 : (tile + 1) * 128]
+    at = slot * nproj
+    rows = p_refs[2 * slab].shape[0]
+    ref = p_refs[2 * slab + at // rows]
+    return ref[at % rows : at % rows + nproj, tile * 128 : (tile + 1) * 128]
 
 
 def couple(dims, slabs, half, coefficients, w_ref, p_refs, start_of, out_ref, scale):
@@ -526,25 +530,35 @@
             out_ref[spot, :] = out_ref[spot, :] + contrib
 
 
-def next_partials(dims, half, send_ref, p_refs, start_of, r_ref):
-    n, cap, nproj, foot, chunk = dims
-    lanes = n * chunk
-    for slab in range(half):
-        for slot in range(n * cap):
-            start = start_of(slab, slot)
-            total = None
-            for tile in range(foot):
-                cells = jnp.broadcast_to(send_ref[pl.ds(start + tile, 1), :], (nproj, 128))
-                term = p_rows(p_refs, slab, slot, nproj, tile) * cells
-                total = term if total is None else total + term
-            r_ref[slab * lanes + slot * nproj : slab * lanes + (slot + 1) * nproj, :] = total
-    row = lax.dot_general(
+def fill_rows(dims, slab, y_ref, p_refs, start_of, r_ref):
+    n, cap, nproj, foot, chunk = dims
+    for slot in range(n * cap):
+        start = start_of(slab, slot)
+        total = None
+        for tile in range(foot):
+            cells = jnp.broadcast_to(y_ref[pl.ds(start + tile, 1), :], (nproj, 128))
+            term = p_rows(p_refs, slab, slot, nproj, tile) * cells
+            total = term if total is None else total + term
+        at = (slab * n * cap + slot) * nproj
+        r_ref[at : at + nproj, :] = total
+
+
+def row_sums(r_ref):
+    return lax.dot_general(
         jnp.ones((8, 128), f32),
         r_ref[...],
         (((1,), (1,)), ((), ())),
         precision=highest,
         preferred_element_type=f32,
     )
+
+
+def next_partials(dims, half, send_ref, p_refs, start_of, r_ref):
+    n, cap, nproj, foot, chunk = dims
+    lanes = n * chunk
+    for slab in range(half):
+        fill_rows(dims, slab, send_ref, p_refs, start_of, r_ref)
+    row = row_sums(r_ref)
     for slab in range(half):
         send_ref[half * SLAB + slab : half * SLAB + slab + 1, :] = row[
             0:1, slab * lanes : (slab + 1) * lanes
@@ -576,7 +590,7 @@
     n, cap, nproj, foot, chunk = dims
     half = n // 2
     int_ref, part_ref, w_ref, c_ref = refs[:4]
-    p_refs, (send_ref, r_ref, int_s, sem) = refs[4 : 5 + half], refs[5 + half :]
+    p_refs, (send_ref, r_ref, int_s, sem) = refs[4 : 4 + 2 * half], refs[4 + 2 * half :]
     copy = pltpu.make_async_copy(int_ref, int_s, sem)
     copy.start()
     send_ref[0 : half * SLAB, :] = part_ref[...]
@@ -591,8 +605,8 @@
     n, cap, nproj, foot, chunk = dims
     half = n // 2
     int_ref, y_ref, got_ref, prev_ref, v_ref, w_ref = refs[:6]
-    p_refs = refs[6 : 7 + half]
-    out_ref, other_ref, pad_ref, int_s, sem = refs[7 + half : 12 + half]
+    p_refs, refs = refs[6 : 6 + 2 * half], refs[6 + 2 * half :]
+    out_ref, other_ref, pad_ref, int_s, sem = refs[:5]
     copy = pltpu.make_async_copy(int_ref, int_s, sem)
     copy.start()
     other_ref[0 : half * SLAB, :] = got_ref[0 : half * SLAB, :]
@@ -614,7 +628,7 @@
     start_of = starts_from(int_s, nproj)
     couple(dims, slabs, half, coefficients, w_ref, p_refs, start_of, out_ref, scale)
     if not last:
-        next_partials(dims, half, out_ref, p_refs, start_of, refs[12 + half])
+        next_partials(dims, half, out_ref, p_refs, start_of, refs[5])
 
 
 def chip_table(n):
@@ -668,57 +682,54 @@
 
     sources = (psi.reshape(SLAB, 128), p, offsets[0].T, intersection[0].T, couplings, v_piece)
     sources = [pltpu.with_memory_space_constraint(x, pltpu.HBM) for x in sources]
-    pack, p = pl.pallas_call(
+    half_p = jax.ShapeDtypeStruct((lanes // 2, foot * 128), f32)
+    pack, top, bottom = pl.pallas_call(
         functools.partial(pack_kernel, dims),
-        out_shape=(
-            shape(SLAB + v_piece.shape[0] + SMALL),
-            jax.ShapeDtypeStruct(p.shape, f32),
-        ),
+        out_shape=(shape(SLAB + v_piece.shape[0] + SMALL), half_p, half_p),
         in_specs=[HBM] * 6,
-        out_specs=(VMEM, VMEM),
+        out_specs=(VMEM,) * 3,
         scratch_shapes=[
             pltpu.SMEM((cap, n), jnp.int32),
             pltpu.SMEM((cap, n), jnp.int32),
             pltpu.VMEM(couplings.shape, f32),
             pltpu.VMEM((lanes, 128), f32),
-            pltpu.SemaphoreType.DMA((6,)),
+            pltpu.SemaphoreType.DMA((7,)),
         ],
         compiler_params=params,
         cost_estimate=small,
         name="pack",
     )(*sources)
     packs = [pack] + [swap(pack, 2 * local) for local in range(1, half)]
-    own, v_piece, p = pl.pallas_call(
+    own, v_piece = pl.pallas_call(
         sort_kernel,
-        out_shape=(
-            shape(half * (SLAB + SMALL)),
-            shape(half * v_piece.shape[0]),
-            jax.ShapeDtypeStruct(p.shape, f32),
-        ),
-        in_specs=[VMEM] * (half + 1),
-        out_specs=(VMEM,) * 3,
-        input_output_aliases={half: 2},
+        out_shape=(shape(half * (SLAB + SMALL)), shape(half * v_piece.shape[0])),
+        in_specs=[VMEM] * half,
+        out_specs=(VMEM, VMEM),
         compiler_params=params,
         cost_estimate=small,
         name="sort",
-    )(*packs, p)
+    )(*packs)
     got = swap(own, 1)
     pieces = [v_piece]
     for back in range(1, nband):
         ring = [(i, (i + back) % nband) for i in range(nband)]
         pieces.append(lax.ppermute(v_piece, "band", ring))
-    p_x, p_y = swap(p, 2), swap(p, 4)
-    halves = (jax.ShapeDtypeStruct((lanes // 2, foot * 128), f32),) * 2
-    top, bottom = pl.pallas_call(
-        relay_kernel,
-        out_shape=halves,
-        in_specs=[VMEM] * 2,
-        out_specs=(VMEM, VMEM),
-        compiler_params=params,
-        cost_estimate=large,
-        name="relay",
-    )(p_x, p_y)
-    all_p = [p, p_x, p_y, swap(top, 4), swap(bottom, 2)]
+    x_top, y_bottom = swap(top, 2), swap(bottom, 4)
+    x_bottom, y_top = swap(bottom, 2), swap(top, 4)
+
+    def relay(x, name):
+        return pl.pallas_call(
+            relay_kernel,
+            out_shape=half_p,
+            in_specs=[VMEM],
+            out_specs=VMEM,
+            compiler_params=params,
+            cost_estimate=large,
+            name=name,
+        )(x)
+
+    far_top, far_bottom = swap(relay(x_top, "relay_x"), 4), swap(relay(y_bottom, "relay_y"), 2)
+    all_p = [top, bottom, x_top, x_bottom, y_top, y_bottom, far_top, far_bottom]
     other = pltpu.VMEM(((half + 1) * SLAB, 128), f32)
     padded = pltpu.VMEM((half * 6 * (NY + 16), 128), f32)
     row_scratch = pltpu.VMEM((half * lanes, 128), f32)
@@ -753,7 +764,7 @@
     y = pl.pallas_call(
         functools.partial(first_kernel, dims),
         out_shape=sent,
-        in_specs=[VMEM] * (5 + half),
+        in_specs=[VMEM] * (4 + 2 * half),
         out_specs=VMEM,
         scratch_shapes=[row_scratch] + ints,
         compiler_params=params,
@@ -764,7 +775,7 @@
         following = pl.pallas_call(
             functools.partial(chip_kernel, dims, last),
             out_shape=shape(SLAB) if last else sent,
-            in_specs=[VMEM] * (7 + half),
+            in_specs=[VMEM] * (6 + 2 * half),
             out_specs=VMEM,
             scratch_shapes=[other, padded] + ints + ([] if last else [row_scratch]),
             compiler_params=params,

time: 49 us -> 54.6 us (1.11)
  starting transfers between devices: 14.1 us -> 19.7 us
    ppermute x11 -> x13, starting transfers between devices: 9.34 us -> 14.2 us  [swap(): return lax.ppermute(x, 'domain', [(i, i ^ step) for i in range(n)])]
    ppermute x3, starting transfers between devices: 4.73 us -> 5.57 us  [chip_form(): pieces.append(lax.ppermute(v_piece, 'band', ring))]
    ppermute x11 -> x13, waiting for transfers between devices: 20.5 us -> 20.4 us  [swap(): return lax.ppermute(x, 'domain', [(i, i ^ step) for i in range(n)])]
  transfers between devices with their start and end apart: 14 -> 16, of which waited for: 10 -> 8; matrix products, arithmetic and copies ran while one was open for 2% -> 1% of each run, Pallas kernels for 7% -> 6%
where the time goes in v6:
time: 54.6 us; the launch traced here: 54.4 us
  waiting for transfers between devices  20.4 us (37%)
  starting transfers between devices  19.7 us (36%)
  Pallas kernels  13.4 us (25%)
  local copies, waits for them, and re-layouts  0.69 us (1%)
    ppermute x13, waiting for transfers between devices, swap(): return lax.ppermute(x, 'domain', [(i, i ^ step) for i in range(n)])  20.4 us
    ppermute x13, starting transfers between devices, swap(): return lax.ppermute(x, 'domain', [(i, i ^ step) for i in range(n)])  14.2 us
    pallas_call x3, Pallas kernels, chip_form(): pl.pallas_call(functools.partial(chip_kernel, dims, last), out_shape=shap...  6.89 us
    ppermute x3, starting transfers between devices, chip_form(): pieces.append(lax.ppermute(v_piece, 'band', ring))  5.57 us
    pallas_call x1, Pallas kernels, chip_form(): pl.pallas_call(functools.partial(begin_kernel, dims), out_shape=(shape(ha...  2.47 us
    pallas_call x1, Pallas kernels, chip_form(): pl.pallas_call(functools.partial(first_kernel, dims), out_shape=sent, in_...  1.82 us
    pallas_call x1, Pallas kernels, chip_form(): pl.pallas_call(functools.partial(pack_kernel, dims), out_shape=(shape(SLA...  1.4 us
  transfers between devices with their start and end apart: 16, of which 8 were waited for; matrix products, arithmetic and copies ran while one was open for 1% of the time, Pallas kernels for 6%

profile of v6, /device:TPU:0, one launch (start us, length us, event | category | flops | bytes accessed | tf_op | source)
XLA Modules:
  0.0 54.4 jit_solution(2676617845131774172)
XLA Ops:
  0.0 1.4 %pack.1 = (f32[264,128]{1,0:T(8,128)S(1)}, f32[64,1024]{1,0:T(8,128)S(1)}, f32[64,1024]{1,0:T(8,128)S(1)}) custom-call(f32[192,128]{1,0:T(8,128)} %bitcast.17, f32[128,1024]{1,0:T(8,128)} %bitcast.16, s32[2,8]{1,0:T(2,128)} %bitcast.20, s32[2,8]{1,0:T(2,128)} %bitcast.21, f32[64,32]{1,0:T(8,128)} %bitcast.18, f32[48,128]{1,0:T(8,128)} %bitcast.19), custom_call_target="tpu_custom_call" | custom-call | flops 1 | bytes 1 | tf_op jit(solution)/shard_map/pack/pallas_call | solution.py:686
  1.4 3.0 %collective-permute-start.7 = (f32[64,1024]{1,0:T(8,128)S(1)}, f32[64,1024]{1,0:T(8,128)S(1)}, u32[]{:S(2)}, u32[]{:S(2)}) collective-permute-start(f32[64,1024]{1,0:T(8,128)S(1)} %get-tuple-element.26.refs_4_.refs_6_), channel_id=1, source_target_pairs={{0,8},{4,12},{8,0},{12,4},{16,24},{20,28},{24,16},{28,20},{1,9},{5... | collective-permute-start | bytes 786440 | tf_op jit(solution)/shard_map/ppermute | solution.py:681
  4.5 2.0 %collective-permute-start.1 = (f32[264,128]{1,0:T(8,128)S(1)}, f32[264,128]{1,0:T(8,128)S(1)}, u32[]{:S(2)}, u32[]{:S(2)}) collective-permute-start(f32[264,128]{1,0:T(8,128)S(1)} %get-tuple-element.17.refs_0_), channel_id=1, source_target_pairs={{0,16},{4,20},{8,24},{12,28},{16,0},{20,4},{24,8},{28,12},{1,17},{... | collective-permute-start | bytes 405512 | tf_op jit(solution)/shard_map/ppermute | solution.py:681
  6.5 1.4 %collective-permute-start.2 = (f32[264,128]{1,0:T(8,128)S(1)}, f32[264,128]{1,0:T(8,128)S(1)}, u32[]{:S(2)}, u32[]{:S(2)}) collective-permute-start(f32[264,128]{1,0:T(8,128)S(1)} %get-tuple-element.17.refs_0_), channel_id=1, source_target_pairs={{0,24},{4,28},{8,16},{12,20},{16,8},{20,12},{24,0},{28,4},{1,25},{... | collective-permute-start | bytes 405512 | tf_op jit(solution)/shard_map/ppermute | solution.py:681
  7.9 1.5 %collective-permute-start.10 = (f32[64,1024]{1,0:T(8,128)S(1)}, f32[64,1024]{1,0:T(8,128)S(1)}, u32[]{:S(2)}, u32[]{:S(2)}) collective-permute-start(f32[64,1024]{1,0:T(8,128)S(1)} %get-tuple-element.27.refs_5_.refs_7_), channel_id=1, source_target_pairs={{0,16},{4,20},{8,24},{12,28},{16,0},{20,4},{24,8},{28,12},{1,17},{... | collective-permute-start | bytes 786440 | tf_op jit(solution)/shard_map/ppermute | solution.py:681
  10.2 4.2 %collective-permute-done.refs_1_ = f32[264,128]{1,0:T(8,128)S(1)} collective-permute-done((f32[264,128]{1,0:T(8,128)S(1)}, f32[264,128]{1,0:T(8,128)S(1)}, u32[]{:S(2)}, u32[]{:S(2)}) %collective-permute-start) | collective-permute-done | bytes 135200 | tf_op jit(solution)/shard_map/ppermute | solution.py:681
  14.4 2.1 %collective-permute-start.8 = (f32[64,1024]{1,0:T(8,128)S(1)}, f32[64,1024]{1,0:T(8,128)S(1)}, u32[]{:S(2)}, u32[]{:S(2)}) collective-permute-start(f32[64,1024]{1,0:T(8,128)S(1)} %get-tuple-element.27.refs_5_.refs_7_), channel_id=1, source_target_pairs={{0,8},{4,12},{8,0},{12,4},{16,24},{20,28},{24,16},{28,20},{1,9},{5... | collective-permute-start | bytes 786440 | tf_op jit(solution)/shard_map/ppermute | solution.py:681
  16.5 2.4 %collective-permute-done.2.refs_3_ = f32[264,128]{1,0:T(8,128)S(1)} collective-permute-done((f32[264,128]{1,0:T(8,128)S(1)}, f32[264,128]{1,0:T(8,128)S(1)}, u32[]{:S(2)}, u32[]{:S(2)}) %collective-permute-start.2) | collective-permute-done | bytes 135200 | tf_op jit(solution)/shard_map/ppermute | solution.py:681
  18.9 1.6 %collective-permute-start.4 = (f32[192,128]{1,0:T(8,128)S(1)}, f32[192,128]{1,0:T(8,128)S(1)}, u32[]{:S(2)}, u32[]{:S(2)}) collective-permute-start(f32[192,128]{1,0:T(8,128)S(1)} %get-tuple-element.22.refs_0_), channel_id=1, source_target_pairs={{0,1},{1,2},{2,3},{3,0},{4,5},{5,6},{6,7},{7,4},{8,9},{9,10},{10,1... | collective-permute-start | bytes 294920 | tf_op jit(solution)/shard_map/ppermute | solution.py:716
  20.5 2.6 %collective-permute-start.5 = (f32[192,128]{1,0:T(8,128)S(1)}, f32[192,128]{1,0:T(8,128)S(1)}, u32[]{:S(2)}, u32[]{:S(2)}) collective-permute-start(f32[192,128]{1,0:T(8,128)S(1)} %get-tuple-element.22.refs_0_), channel_id=1, source_target_pairs={{0,2},{1,3},{2,0},{3,1},{4,6},{5,7},{6,4},{7,5},{8,10},{9,11},{10,... | collective-permute-start | bytes 294920 | tf_op jit(solution)/shard_map/ppermute | solution.py:716
  23.1 1.3 %collective-permute-start.6 = (f32[192,128]{1,0:T(8,128)S(1)}, f32[192,128]{1,0:T(8,128)S(1)}, u32[]{:S(2)}, u32[]{:S(2)}) collective-permute-start(f32[192,128]{1,0:T(8,128)S(1)} %get-tuple-element.22.refs_0_), channel_id=1, source_target_pairs={{0,3},{1,0},{2,1},{3,2},{4,7},{5,4},{6,5},{7,6},{8,11},{9,8},{10,9... | collective-permute-start | bytes 294920 | tf_op jit(solution)/shard_map/ppermute | solution.py:716
  24.6 1.8 %collective-permute-done.3.got_ref = f32[864,128]{1,0:T(8,128)S(1)} collective-permute-done((f32[864,128]{1,0:T(8,128)S(1)}, f32[864,128]{1,0:T(8,128)S(1)}, u32[]{:S(2)}, u32[]{:S(2)}) %collective-permute-start.3) | collective-permute-done | bytes 442400 | tf_op jit(solution)/shard_map/ppermute | solution.py:681
  26.9 2.5 %begin.1 = (f32[768,128]{1,0:T(8,128)S(1)}, f32[768,128]{1,0:T(8,128)S(1)}, f32[512,128]{1,0:T(8,128)S(1)}, f32[8,128]{1,0:T(8,128)S(1)}, s32[8,128]{1,0:T(8,128)S(1)}) custom-call(s32[25]{0:T(128)S(1)} %pad_add_fusion.info_ref, f32[864,128]{1,0:T(8,128)S(1)} %get-tuple-element.18.own_ref, f32[864,128]{1,0:T(8,128)S(1)} %collective-permute-done.3.got_ref), custom_call_target="tpu_custom_call" | custom-call | flops 1 | bytes 1 | tf_op jit(solution)/shard_map/begin/pallas_call | solution.py:737
  29.4 1.6 %collective-permute-start.11 = (f32[64,1024]{1,0:T(8,128)S(1)}, f32[64,1024]{1,0:T(8,128)S(1)}, u32[]{:S(2)}, u32[]{:S(2)}) collective-permute-start(f32[64,1024]{1,0:T(8,128)S(1)} %relay_x.1), channel_id=1, source_target_pairs={{0,16},{4,20},{8,24},{12,28},{16,0},{20,4},{24,8},{28,12},{1,17},{... | collective-permute-start | bytes 786440 | tf_op jit(solution)/shard_map/ppermute | solution.py:681
  30.9 1.5 %collective-permute-start.12 = (f32[64,1024]{1,0:T(8,128)S(1)}, f32[64,1024]{1,0:T(8,128)S(1)}, u32[]{:S(2)}, u32[]{:S(2)}) collective-permute-start(f32[64,1024]{1,0:T(8,128)S(1)} %relay_y.1), channel_id=1, source_target_pairs={{0,8},{4,12},{8,0},{12,4},{16,24},{20,28},{24,16},{28,20},{1,9},{5... | collective-permute-start | bytes 786440 | tf_op jit(solution)/shard_map/ppermute | solution.py:681
  33.2 2.3 %collective-permute-done.9.refs_8_.refs_10_ = f32[64,1024]{1,0:T(8,128)S(1)} collective-permute-done((f32[64,1024]{1,0:T(8,128)S(1)}, f32[64,1024]{1,0:T(8,128)S(1)}, u32[]{:S(2)}, u32[]{:S(2)}) %collective-permute-start.9) | collective-permute-done | bytes 262176 | tf_op jit(solution)/shard_map/ppermute | solution.py:681
  35.5 4.8 %collective-permute-done.11.refs_10_.refs_12_ = f32[64,1024]{1,0:T(8,128)S(1)} collective-permute-done((f32[64,1024]{1,0:T(8,128)S(1)}, f32[64,1024]{1,0:T(8,128)S(1)}, u32[]{:S(2)}, u32[]{:S(2)}) %collective-permute-start.11) | collective-permute-done | bytes 262176 | tf_op jit(solution)/shard_map/ppermute | solution.py:681
  40.3 1.8 %first.1.refs_1_.refs_3_ = f32[776,128]{1,0:T(8,128)S(1)} custom-call(s32[8,128]{1,0:T(8,128)S(1)} %get-tuple-element.19.table_ref.refs_0_, f32[768,128]{1,0:T(8,128)S(1)} %get-tuple-element.23.refs_1_, f32[512,128]{1,0:T(8,128)S(1)} %get-tuple-element.24.refs_2_.refs_5_, f32[8,128]{1,0:T(8,128)S(1)} %get-tuple-element.25.refs_3_, ...), custom_call_target="tpu_custom_call" | custom-call | tf_op jit(solution)/shard_map/first/pallas_call | solution.py:764
  42.2 1.7 %collective-permute-done.13.refs_2_ = f32[776,128]{1,0:T(8,128)S(1)} collective-permute-done((f32[776,128]{1,0:T(8,128)S(1)}, f32[776,128]{1,0:T(8,128)S(1)}, u32[]{:S(2)}, u32[]{:S(2)}) %collective-permute-start.13) | collective-permute-done | bytes 397344 | tf_op jit(solution)/shard_map/ppermute | solution.py:681
  43.9 2.6 %next.2.refs_1_.refs_3_ = f32[776,128]{1,0:T(8,128)S(1)} custom-call(s32[8,128]{1,0:T(8,128)S(1)} %get-tuple-element.19.table_ref.refs_0_, f32[776,128]{1,0:T(8,128)S(1)} %first.1.refs_1_.refs_3_, f32[776,128]{1,0:T(8,128)S(1)} %collective-permute-done.13.refs_2_, f32[768,128]{1,0:T(8,128)S(1)} %get-tuple-element.21.y_ref.refs_3_, ...), custom_call_target="tpu_custom_call" | custom-call | tf_op jit(solution)/shard_map/next/pallas_call | solution.py:775
  46.8 1.6 %collective-permute-done.14.refs_2_ = f32[776,128]{1,0:T(8,128)S(1)} collective-permute-done((f32[776,128]{1,0:T(8,128)S(1)}, f32[776,128]{1,0:T(8,128)S(1)}, u32[]{:S(2)}, u32[]{:S(2)}) %collective-permute-start.14) | collective-permute-done | bytes 397344 | tf_op jit(solution)/shard_map/ppermute | solution.py:681
  48.4 2.6 %next.3.refs_1_ = f32[776,128]{1,0:T(8,128)S(1)} custom-call(s32[8,128]{1,0:T(8,128)S(1)} %get-tuple-element.19.table_ref.refs_0_, f32[776,128]{1,0:T(8,128)S(1)} %next.2.refs_1_.refs_3_, f32[776,128]{1,0:T(8,128)S(1)} %collective-permute-done.14.refs_2_, f32[776,128]{1,0:T(8,128)S(1)} %first.1.refs_1_.refs_3_, f32[768,128]{1,0:T(8,128)S(1)} %get-tuple-element.28.refs_4_, ...), custom_call_target="tpu_custom_call" | custom-call | tf_op jit(solution)/shard_map/next/pallas_call | solution.py:775
  51.2 1.6 %collective-permute-done.15.refs_2_ = f32[776,128]{1,0:T(8,128)S(1)} collective-permute-done((f32[776,128]{1,0:T(8,128)S(1)}, f32[776,128]{1,0:T(8,128)S(1)}, u32[]{:S(2)}, u32[]{:S(2)}) %collective-permute-start.15) | collective-permute-done | bytes 397344 | tf_op jit(solution)/shard_map/ppermute | solution.py:681
  52.8 1.7 %last.1 = f32[192,128]{1,0:T(8,128)} custom-call(s32[8,128]{1,0:T(8,128)S(1)} %get-tuple-element.19.table_ref.refs_0_, f32[776,128]{1,0:T(8,128)S(1)} %next.3.refs_1_, f32[776,128]{1,0:T(8,128)S(1)} %collective-permute-done.15.refs_2_, f32[776,128]{1,0:T(8,128)S(1)} %next.2.refs_1_.refs_3_, f32[768,128]{1,0:T(8,128)S(1)} %get-tuple-element.28.refs_4_, ...), custom_call_target="tpu_custom_call" | custom-call | tf_op jit(solution)/shard_map/last/pallas_call | solution.py:775
  (20 shorter events, 2.7 us)
Async XLA Ops:
  1.4 21.7 %collective-permute-start.7 = (f32[64,1024]{1,0:T(8,128)S(1)}, f32[64,1024]{1,0:T(8,128)S(1)}, u32[]{:S(2)}, u32[]{:S(2)}) collective-permute-start(f32[64,1024]{1,0:T(8,128)S(1)} %get-tuple-element.26.refs_4_.refs_6_), channel_id=1, source_target_pairs={{0,8},{4,12},{8,0},{12,4},{16,24},{20,28},{24,16},{28,20},{1,9},{5... | collective-permute-start | bytes 786440 | tf_op jit(solution)/shard_map/ppermute | solution.py:681
  4.4 10.0 %collective-permute-start = (f32[264,128]{1,0:T(8,128)S(1)}, f32[264,128]{1,0:T(8,128)S(1)}, u32[]{:S(2)}, u32[]{:S(2)}) collective-permute-start(f32[264,128]{1,0:T(8,128)S(1)} %get-tuple-element.17.refs_0_), channel_id=1, source_target_pairs={{0,8},{4,12},{8,0},{12,4},{16,24},{20,28},{24,16},{28,20},{1,9},{5... | collective-permute-start | bytes 405512 | tf_op jit(solution)/shard_map/ppermute | solution.py:681
  4.5 12.0 %collective-permute-start.1 = (f32[264,128]{1,0:T(8,128)S(1)}, f32[264,128]{1,0:T(8,128)S(1)}, u32[]{:S(2)}, u32[]{:S(2)}) collective-permute-start(f32[264,128]{1,0:T(8,128)S(1)} %get-tuple-element.17.refs_0_), channel_id=1, source_target_pairs={{0,16},{4,20},{8,24},{12,28},{16,0},{20,4},{24,8},{28,12},{1,17},{... | collective-permute-start | bytes 405512 | tf_op jit(solution)/shard_map/ppermute | solution.py:681
  6.5 12.4 %collective-permute-start.2 = (f32[264,128]{1,0:T(8,128)S(1)}, f32[264,128]{1,0:T(8,128)S(1)}, u32[]{:S(2)}, u32[]{:S(2)}) collective-permute-start(f32[264,128]{1,0:T(8,128)S(1)} %get-tuple-element.17.refs_0_), channel_id=1, source_target_pairs={{0,24},{4,28},{8,16},{12,20},{16,8},{20,12},{24,0},{28,4},{1,25},{... | collective-permute-start | bytes 405512 | tf_op jit(solution)/shard_map/ppermute | solution.py:681
  7.9 16.6 %collective-permute-start.10 = (f32[64,1024]{1,0:T(8,128)S(1)}, f32[64,1024]{1,0:T(8,128)S(1)}, u32[]{:S(2)}, u32[]{:S(2)}) collective-permute-start(f32[64,1024]{1,0:T(8,128)S(1)} %get-tuple-element.27.refs_5_.refs_7_), channel_id=1, source_target_pairs={{0,16},{4,20},{8,24},{12,28},{16,0},{20,4},{24,8},{28,12},{1,17},{... | collective-permute-start | bytes 786440 | tf_op jit(solution)/shard_map/ppermute | solution.py:681
  14.4 18.7 %collective-permute-start.8 = (f32[64,1024]{1,0:T(8,128)S(1)}, f32[64,1024]{1,0:T(8,128)S(1)}, u32[]{:S(2)}, u32[]{:S(2)}) collective-permute-start(f32[64,1024]{1,0:T(8,128)S(1)} %get-tuple-element.27.refs_5_.refs_7_), channel_id=1, source_target_pairs={{0,8},{4,12},{8,0},{12,4},{16,24},{20,28},{24,16},{28,20},{1,9},{5... | collective-permute-start | bytes 786440 | tf_op jit(solution)/shard_map/ppermute | solution.py:681
  18.9 10.5 %collective-permute-start.4 = (f32[192,128]{1,0:T(8,128)S(1)}, f32[192,128]{1,0:T(8,128)S(1)}, u32[]{:S(2)}, u32[]{:S(2)}) collective-permute-start(f32[192,128]{1,0:T(8,128)S(1)} %get-tuple-element.22.refs_0_), channel_id=1, source_target_pairs={{0,1},{1,2},{2,3},{3,0},{4,5},{5,6},{6,7},{7,4},{8,9},{9,10},{10,1... | collective-permute-start | bytes 294920 | tf_op jit(solution)/shard_map/ppermute | solution.py:716
  20.5 10.4 %collective-permute-start.5 = (f32[192,128]{1,0:T(8,128)S(1)}, f32[192,128]{1,0:T(8,128)S(1)}, u32[]{:S(2)}, u32[]{:S(2)}) collective-permute-start(f32[192,128]{1,0:T(8,128)S(1)} %get-tuple-element.22.refs_0_), channel_id=1, source_target_pairs={{0,2},{1,3},{2,0},{3,1},{4,6},{5,7},{6,4},{7,5},{8,10},{9,11},{10,... | collective-permute-start | bytes 294920 | tf_op jit(solution)/shard_map/ppermute | solution.py:716
  23.1 9.3 %collective-permute-start.6 = (f32[192,128]{1,0:T(8,128)S(1)}, f32[192,128]{1,0:T(8,128)S(1)}, u32[]{:S(2)}, u32[]{:S(2)}) collective-permute-start(f32[192,128]{1,0:T(8,128)S(1)} %get-tuple-element.22.refs_0_), channel_id=1, source_target_pairs={{0,3},{1,0},{2,1},{3,2},{4,7},{5,4},{6,5},{7,6},{8,11},{9,8},{10,9... | collective-permute-start | bytes 294920 | tf_op jit(solution)/shard_map/ppermute | solution.py:716
  24.5 1.9 %collective-permute-start.3 = (f32[864,128]{1,0:T(8,128)S(1)}, f32[864,128]{1,0:T(8,128)S(1)}, u32[]{:S(2)}, u32[]{:S(2)}) collective-permute-start(f32[864,128]{1,0:T(8,128)S(1)} %get-tuple-element.18.own_ref), channel_id=1, source_target_pairs={{0,4},{4,0},{8,12},{12,8},{16,20},{20,16},{24,28},{28,24},{1,5},{5... | collective-permute-start | bytes 1327112 | tf_op jit(solution)/shard_map/ppermute | solution.py:681
  26.4 9.1 %collective-permute-start.9 = (f32[64,1024]{1,0:T(8,128)S(1)}, f32[64,1024]{1,0:T(8,128)S(1)}, u32[]{:S(2)}, u32[]{:S(2)}) collective-permute-start(f32[64,1024]{1,0:T(8,128)S(1)} %get-tuple-element.26.refs_4_.refs_6_), channel_id=1, source_target_pairs={{0,16},{4,20},{8,24},{12,28},{16,0},{20,4},{24,8},{28,12},{1,17},{... | collective-permute-start | bytes 786440 | tf_op jit(solution)/shard_map/ppermute | solution.py:681
  29.4 11.0 %collective-permute-start.11 = (f32[64,1024]{1,0:T(8,128)S(1)}, f32[64,1024]{1,0:T(8,128)S(1)}, u32[]{:S(2)}, u32[]{:S(2)}) collective-permute-start(f32[64,1024]{1,0:T(8,128)S(1)} %relay_x.1), channel_id=1, source_target_pairs={{0,16},{4,20},{8,24},{12,28},{16,0},{20,4},{24,8},{28,12},{1,17},{... | collective-permute-start | bytes 786440 | tf_op jit(solution)/shard_map/ppermute | solution.py:681
  30.9 9.4 %collective-permute-start.12 = (f32[64,1024]{1,0:T(8,128)S(1)}, f32[64,1024]{1,0:T(8,128)S(1)}, u32[]{:S(2)}, u32[]{:S(2)}) collective-permute-start(f32[64,1024]{1,0:T(8,128)S(1)} %relay_y.1), channel_id=1, source_target_pairs={{0,8},{4,12},{8,0},{12,4},{16,24},{20,28},{24,16},{28,20},{1,9},{5... | collective-permute-start | bytes 786440 | tf_op jit(solution)/shard_map/ppermute | solution.py:681
  42.2 1.8 %collective-permute-start.13 = (f32[776,128]{1,0:T(8,128)S(1)}, f32[776,128]{1,0:T(8,128)S(1)}, u32[]{:S(2)}, u32[]{:S(2)}) collective-permute-start(f32[776,128]{1,0:T(8,128)S(1)} %first.1.refs_1_.refs_3_), channel_id=1, source_target_pairs={{0,4},{4,0},{8,12},{12,8},{16,20},{20,16},{24,28},{28,24},{1,5},{5... | collective-permute-start | bytes 1191944 | tf_op jit(solution)/shard_map/ppermute | solution.py:681
  46.6 1.8 %collective-permute-start.14 = (f32[776,128]{1,0:T(8,128)S(1)}, f32[776,128]{1,0:T(8,128)S(1)}, u32[]{:S(2)}, u32[]{:S(2)}) collective-permute-start(f32[776,128]{1,0:T(8,128)S(1)} %next.2.refs_1_.refs_3_), channel_id=1, source_target_pairs={{0,4},{4,0},{8,12},{12,8},{16,20},{20,16},{24,28},{28,24},{1,5},{5... | collective-permute-start | bytes 1191944 | tf_op jit(solution)/shard_map/ppermute | solution.py:681
  51.0 1.8 %collective-permute-start.15 = (f32[776,128]{1,0:T(8,128)S(1)}, f32[776,128]{1,0:T(8,128)S(1)}, u32[]{:S(2)}, u32[]{:S(2)}) collective-permute-start(f32[776,128]{1,0:T(8,128)S(1)} %next.3.refs_1_), channel_id=1, source_target_pairs={{0,4},{4,0},{8,12},{12,8},{16,20},{20,16},{24,28},{28,24},{1,5},{5... | collective-permute-start | bytes 1191944 | tf_op jit(solution)/shard_map/ppermute | solution.py:681

commit v7 on v5

--- a/solution.py
+++ b/solution.py
@@ -501,35 +501,46 @@
     return ref[at : at + nproj, tile * 128 : (tile + 1) * 128]
 
 
+def swap_rows(x, step):
+    if step == 4:
+        return pltpu.roll(x, 4, 0)
+    low = iota(x.shape, 0) // step % 2 == 0
+    return jnp.where(low, pltpu.roll(x, 8 - step, 0), pltpu.roll(x, step, 0))
+
+
+def column_sums(tiles):
+    step = 4
+    while step:
+        low = iota(tiles[0].shape, 0) // step % 2 == 0
+        pairs = [(tiles[t], tiles[t + step]) for t in range(step)]
+        tiles = [
+            jnp.where(low, a, b) + swap_rows(jnp.where(low, b, a), step) for a, b in pairs
+        ]
+        step //= 2
+    return tiles[0]
+
+
 def couple(dims, slabs, half, coefficients, w_ref, p_refs, start_of, out_ref, scale):
     n, cap, nproj, foot, chunk = dims
-    sublane = iota((foot, 128), 0)
-    for slab in range(slabs):
+    for slab in slabs:
         for slot in range(n * cap):
             owner, k = slot // cap, slot % cap
             at = (owner * half + slab) * chunk + k * nproj
-            returned = jnp.sum(
+            back = jnp.sum(
                 w_ref[at : at + nproj, :] * coefficients[owner : owner + 1, :],
                 axis=1,
                 keepdims=True,
             )
-            returned = jnp.broadcast_to(returned * scale, (nproj, 128))
-            contrib = jnp.zeros((foot, 128), f32)
-            for tile in range(foot):
-                term = jnp.sum(
-                    p_rows(p_refs, slab, slot, nproj, tile) * returned,
-                    axis=0,
-                    keepdims=True,
-                )
-                contrib = jnp.where(sublane == tile, term, contrib)
+            back = jnp.broadcast_to(back * scale, (nproj, 128))
+            tiles = [p_rows(p_refs, slab, slot, nproj, tile) * back for tile in range(foot)]
             spot = pl.ds(start_of(slab, slot), foot)
-            out_ref[spot, :] = out_ref[spot, :] + contrib
-
-
-def next_partials(dims, half, send_ref, p_refs, start_of, r_ref):
+            out_ref[spot, :] = out_ref[spot, :] + column_sums(tiles)
+
+
+def next_partials(dims, slabs, half, send_ref, p_refs, start_of, r_ref):
     n, cap, nproj, foot, chunk = dims
     lanes = n * chunk
-    for slab in range(half):
+    for index, slab in enumerate(slabs):
         for slot in range(n * cap):
             start = start_of(slab, slot)
             total = None
@@ -537,7 +548,8 @@
                 cells = jnp.broadcast_to(send_ref[pl.ds(start + tile, 1), :], (nproj, 128))
                 term = p_rows(p_refs, slab, slot, nproj, tile) * cells
                 total = term if total is None else total + term
-            r_ref[slab * lanes + slot * nproj : slab * lanes + (slot + 1) * nproj, :] = total
+            at = index * lanes + slot * nproj
+            r_ref[at : at + nproj, :] = total
     row = lax.dot_general(
         jnp.ones((8, 128), f32),
         r_ref[...],
@@ -545,11 +557,10 @@
         precision=highest,
         preferred_element_type=f32,
     )
-    for slab in range(half):
+    for index, slab in enumerate(slabs):
         send_ref[half * SLAB + slab : half * SLAB + slab + 1, :] = row[
-            0:1, slab * lanes : (slab + 1) * lanes
+            0:1, index * lanes : (index + 1) * lanes
         ]
-    send_ref[half * SLAB + half :, :] = jnp.zeros((8 - half, 128), f32)
 
 
 def starts_from(int_s, nproj):
@@ -572,19 +583,22 @@
             out_ref[spot, :] = part_ref[spot, :] + scale * (value * y_ref[spot, :])
 
 
-def first_kernel(dims, *refs):
+def first_kernel(dims, slabs, *refs):
     n, cap, nproj, foot, chunk = dims
     half = n // 2
     int_ref, part_ref, w_ref, c_ref = refs[:4]
-    p_refs, (send_ref, r_ref, int_s, sem) = refs[4 : 5 + half], refs[5 + half :]
+    p_refs, (send_ref, r_ref, int_s, sem) = refs[4:-4], refs[-4:]
+    p_refs = (None,) * slabs[0] + tuple(p_refs)
     copy = pltpu.make_async_copy(int_ref, int_s, sem)
     copy.start()
-    send_ref[0 : half * SLAB, :] = part_ref[...]
+    if slabs[0] == 0:
+        send_ref[0 : half * SLAB, :] = part_ref[...]
+        send_ref[half * SLAB :, :] = jnp.zeros((8, 128), f32)
     copy.wait()
     start_of = starts_from(int_s, nproj)
     scale = 1.0 / filter_half_width
-    couple(dims, half, half, c_ref[...], w_ref, p_refs, start_of, send_ref, scale)
-    next_partials(dims, half, send_ref, p_refs, start_of, r_ref)
+    couple(dims, slabs, half, c_ref[...], w_ref, p_refs, start_of, send_ref, scale)
+    next_partials(dims, slabs, half, send_ref, p_refs, start_of, r_ref)
 
 
 def chip_kernel(dims, last, *refs):
@@ -597,7 +611,7 @@
     copy.start()
     other_ref[0 : half * SLAB, :] = got_ref[0 : half * SLAB, :]
     other_ref[half * SLAB :, :] = jnp.zeros((SLAB, 128), f32)
-    slabs = 1 if last else half
+    slabs = range(1 if last else half)
     scale = 2.0 / filter_half_width
 
     def bases():
@@ -607,14 +621,15 @@
             [int_s[half, half + local] for local in range(half)],
         )
 
-    stencil(y_ref, other_ref, v_ref, prev_ref, out_ref, pad_ref, slabs, scale, bases)
+    stencil(y_ref, other_ref, v_ref, prev_ref, out_ref, pad_ref, len(slabs), scale, bases)
     below = slice(half * SLAB, half * SLAB + half)
     rows = jnp.concatenate([y_ref[below, :], got_ref[below, :]], 0)
     coefficients = by_owner(rows, n, chunk)
     start_of = starts_from(int_s, nproj)
     couple(dims, slabs, half, coefficients, w_ref, p_refs, start_of, out_ref, scale)
     if not last:
-        next_partials(dims, half, out_ref, p_refs, start_of, refs[12 + half])
+        out_ref[half * SLAB :, :] = jnp.zeros((8, 128), f32)
+        next_partials(dims, slabs, half, out_ref, p_refs, start_of, refs[12 + half])
 
 
 def chip_table(n):
@@ -750,15 +765,21 @@
         cost_estimate=larger,
         name="potential",
     )(table, part, previous, *pieces)
-    y = pl.pallas_call(
-        functools.partial(first_kernel, dims),
-        out_shape=sent,
-        in_specs=[VMEM] * (5 + half),
-        out_specs=VMEM,
-        scratch_shapes=[row_scratch] + ints,
-        compiler_params=params,
-        name="first",
-    )(table, part, w, c, *all_p)
+    y = part
+    for slabs in (range(half - 1), range(half - 1, half)):
+        start, late = slabs[0], slabs[0] > 0
+        some_p = all_p[start:] if late else all_p[: half - 1]
+        y = pl.pallas_call(
+            functools.partial(first_kernel, dims, slabs),
+            out_shape=sent,
+            in_specs=[VMEM] * (4 + len(some_p)),
+            out_specs=VMEM,
+            scratch_shapes=[pltpu.VMEM((len(slabs) * lanes, 128), f32)] + ints,
+            input_output_aliases={1: 0} if late else {},
+            compiler_params=params,
+            cost_estimate=small,
+            name="first_late" if late else "first",
+        )(table, y, w, c, *some_p)
     for degree in range(1, DEGREE):
         last = degree == DEGREE - 1
         following = pl.pallas_call(

time: 49 us -> 47.8 us (0.976)
  waiting for transfers between devices: 20.5 us -> 19.1 us
    ppermute x11, waiting for transfers between devices: 20.5 us -> 19.1 us  [swap(): return lax.ppermute(x, 'domain', [(i, i ^ step) for i in range(n)])]
    pallas_call x1 -> x2, Pallas kernels: 1.83 us -> 2.49 us  [chip_form(): pl.pallas_call(functools.partial(first_kernel, dims, slabs), out_shape=se...]
  transfers between devices with their start and end apart: 14 -> 14, of which waited for: 10 -> 10; matrix products, arithmetic and copies ran while one was open for 2% -> 2% of each run, Pallas kernels for 7% -> 10%
where the time goes in v7:
time: 47.8 us; the launch traced here: 47.6 us
  waiting for transfers between devices  19.1 us (40%)
  starting transfers between devices  14.1 us (29%)
  Pallas kernels  13.6 us (28%)
  local copies, waits for them, and re-layouts  0.69 us (1%)
    ppermute x11, waiting for transfers between devices, swap(): return lax.ppermute(x, 'domain', [(i, i ^ step) for i in range(n)])  19.1 us
    ppermute x11, starting transfers between devices, swap(): return lax.ppermute(x, 'domain', [(i, i ^ step) for i in range(n)])  9.34 us
    pallas_call x3, Pallas kernels, chip_form(): pl.pallas_call(functools.partial(chip_kernel, dims, last), out_shape=shap...  6.45 us
    ppermute x3, starting transfers between devices, chip_form(): pieces.append(lax.ppermute(v_piece, 'band', ring))  4.73 us
    pallas_call x2, Pallas kernels, chip_form(): pl.pallas_call(functools.partial(first_kernel, dims, slabs), out_shape=se...  2.49 us
    pallas_call x1, Pallas kernels, chip_form(): pl.pallas_call(functools.partial(begin_kernel, dims), out_shape=(shape(ha...  2.47 us
    pallas_call x1, Pallas kernels, chip_form(): pl.pallas_call(functools.partial(pack_kernel, dims), out_shape=(shape(SLA...  1.4 us
  transfers between devices with their start and end apart: 14, of which 10 were waited for; matrix products, arithmetic and copies ran while one was open for 2% of the time, Pallas kernels for 10%

profile of v7, /device:TPU:0, one launch (start us, length us, event | category | flops | bytes accessed | tf_op | source)
XLA Modules:
  0.0 47.6 jit_solution(9357648068476634068)
XLA Ops:
  0.0 1.4 %pack.1 = (f32[264,128]{1,0:T(8,128)S(1)}, f32[128,1024]{1,0:T(8,128)S(1)}) custom-call(f32[192,128]{1,0:T(8,128)} %bitcast.17, f32[128,1024]{1,0:T(8,128)} %bitcast.16, s32[2,8]{1,0:T(2,128)} %bitcast.20, s32[2,8]{1,0:T(2,128)} %bitcast.21, f32[64,32]{1,0:T(8,128)} %bitcast.18, f32[48,128]{1,0:T(8,128)} %bitcast.19), custom_call_target="tpu_custom_call" | custom-call | flops 1 | bytes 1 | tf_op jit(solution)/shard_map/pack/pallas_call | solution.py:686
  1.4 4.0 %collective-permute-start.2 = (f32[264,128]{1,0:T(8,128)S(1)}, f32[264,128]{1,0:T(8,128)S(1)}, u32[]{:S(2)}, u32[]{:S(2)}) collective-permute-start(f32[264,128]{1,0:T(8,128)S(1)} %get-tuple-element.19.refs_0_), channel_id=1, source_target_pairs={{0,24},{4,28},{8,16},{12,20},{16,8},{20,12},{24,0},{28,4},{1,25},{... | collective-permute-start | bytes 405512 | tf_op jit(solution)/shard_map/ppermute | solution.py:682
  5.4 0.5 %collective-permute-start.1 = (f32[264,128]{1,0:T(8,128)S(1)}, f32[264,128]{1,0:T(8,128)S(1)}, u32[]{:S(2)}, u32[]{:S(2)}) collective-permute-start(f32[264,128]{1,0:T(8,128)S(1)} %get-tuple-element.19.refs_0_), channel_id=1, source_target_pairs={{0,16},{4,20},{8,24},{12,28},{16,0},{20,4},{24,8},{28,12},{1,17},{... | collective-permute-start | bytes 405512 | tf_op jit(solution)/shard_map/ppermute | solution.py:682
  6.0 3.3 %collective-permute-done.2.refs_3_ = f32[264,128]{1,0:T(8,128)S(1)} collective-permute-done((f32[264,128]{1,0:T(8,128)S(1)}, f32[264,128]{1,0:T(8,128)S(1)}, u32[]{:S(2)}, u32[]{:S(2)}) %collective-permute-start.2) | collective-permute-done | bytes 135200 | tf_op jit(solution)/shard_map/ppermute | solution.py:682
  9.4 2.5 %collective-permute-done.1.refs_2_ = f32[264,128]{1,0:T(8,128)S(1)} collective-permute-done((f32[264,128]{1,0:T(8,128)S(1)}, f32[264,128]{1,0:T(8,128)S(1)}, u32[]{:S(2)}, u32[]{:S(2)}) %collective-permute-start.1) | collective-permute-done | bytes 135200 | tf_op jit(solution)/shard_map/ppermute | solution.py:682
  12.1 1.5 %collective-permute-start.8 = (f32[128,1024]{1,0:T(8,128)S(1)}, f32[128,1024]{1,0:T(8,128)S(1)}, u32[]{:S(2)}, u32[]{:S(2)}) collective-permute-start(f32[128,1024]{1,0:T(8,128)S(1)} %get-tuple-element.29.refs_4_.refs_6_), channel_id=1, source_target_pairs={{0,16},{4,20},{8,24},{12,28},{16,0},{20,4},{24,8},{28,12},{1,17},{... | collective-permute-start | bytes 1572872 | tf_op jit(solution)/shard_map/ppermute | solution.py:682
  13.7 0.7 %collective-permute-start.7 = (f32[128,1024]{1,0:T(8,128)S(1)}, f32[128,1024]{1,0:T(8,128)S(1)}, u32[]{:S(2)}, u32[]{:S(2)}) collective-permute-start(f32[128,1024]{1,0:T(8,128)S(1)} %get-tuple-element.29.refs_4_.refs_6_), channel_id=1, source_target_pairs={{0,8},{4,12},{8,0},{12,4},{16,24},{20,28},{24,16},{28,20},{1,9},{5... | collective-permute-start | bytes 1572872 | tf_op jit(solution)/shard_map/ppermute | solution.py:682
  14.4 0.7 %dynamic-slice_bitcast_fusion = s32[24]{0:T(128)S(1)} fusion(s32[8,24]{1,0:T(8,128)} %constant.15.clone, s32[]{:T(128)S(6)} %select_n.3), kind=kLoop, calls=%fused_computation.1 | loop fusion | bytes 196 | tf_op jit(solution)/shard_map/squeeze | solution.py:668
  15.1 3.7 %collective-permute-start.6 = (f32[192,128]{1,0:T(8,128)S(1)}, f32[192,128]{1,0:T(8,128)S(1)}, u32[]{:S(2)}, u32[]{:S(2)}) collective-permute-start(f32[192,128]{1,0:T(8,128)S(1)} %get-tuple-element.25.refs_0_), channel_id=1, source_target_pairs={{0,3},{1,0},{2,1},{3,2},{4,7},{5,4},{6,5},{7,6},{8,11},{9,8},{10,9... | collective-permute-start | bytes 294920 | tf_op jit(solution)/shard_map/ppermute | solution.py:724
  18.8 1.0 %collective-permute-start.4 = (f32[192,128]{1,0:T(8,128)S(1)}, f32[192,128]{1,0:T(8,128)S(1)}, u32[]{:S(2)}, u32[]{:S(2)}) collective-permute-start(f32[192,128]{1,0:T(8,128)S(1)} %get-tuple-element.25.refs_0_), channel_id=1, source_target_pairs={{0,1},{1,2},{2,3},{3,0},{4,5},{5,6},{6,7},{7,4},{8,9},{9,10},{10,1... | collective-permute-start | bytes 294920 | tf_op jit(solution)/shard_map/ppermute | solution.py:724
  19.9 2.5 %begin.1 = (f32[768,128]{1,0:T(8,128)S(1)}, f32[768,128]{1,0:T(8,128)S(1)}, f32[512,128]{1,0:T(8,128)S(1)}, f32[8,128]{1,0:T(8,128)S(1)}, s32[8,128]{1,0:T(8,128)S(1)}) custom-call(s32[25]{0:T(128)S(1)} %pad_add_fusion.info_ref, f32[864,128]{1,0:T(8,128)S(1)} %get-tuple-element.21.own_ref, f32[864,128]{1,0:T(8,128)S(1)} %collective-permute-done.3.got_ref), custom_call_target="tpu_custom_call" | custom-call | flops 1 | bytes 1 | tf_op jit(solution)/shard_map/begin/pallas_call | solution.py:741
  22.3 3.5 %collective-permute-done.8.refs_6_.y_ref.refs_8_ = f32[128,1024]{1,0:T(8,128)S(1)} collective-permute-done((f32[128,1024]{1,0:T(8,128)S(1)}, f32[128,1024]{1,0:T(8,128)S(1)}, u32[]{:S(2)}, u32[]{:S(2)}) %collective-permute-start.8) | collective-permute-done | bytes 524320 | tf_op jit(solution)/shard_map/ppermute | solution.py:682
  25.8 1.4 %collective-permute-done.7.refs_5_.x_ref.refs_7_ = f32[128,1024]{1,0:T(8,128)S(1)} collective-permute-done((f32[128,1024]{1,0:T(8,128)S(1)}, f32[128,1024]{1,0:T(8,128)S(1)}, u32[]{:S(2)}, u32[]{:S(2)}) %collective-permute-start.7) | collective-permute-done | bytes 524320 | tf_op jit(solution)/shard_map/ppermute | solution.py:682
  27.7 1.6 %collective-permute-start.10 = (f32[64,1024]{1,0:T(8,128)S(1)}, f32[64,1024]{1,0:T(8,128)S(1)}, u32[]{:S(2)}, u32[]{:S(2)}) collective-permute-start(f32[64,1024]{1,0:T(8,128)S(1)} %get-tuple-element.31), channel_id=1, source_target_pairs={{0,8},{4,12},{8,0},{12,4},{16,24},{20,28},{24,16},{28,20},{1,9},{5... | collective-permute-start | bytes 786440 | tf_op jit(solution)/shard_map/ppermute | solution.py:682
  29.4 0.7 %potential.1 = (f32[768,128]{1,0:T(8,128)S(1)}, f32[768,128]{1,0:T(8,128)S(1)}) custom-call(s32[8,128]{1,0:T(8,128)S(1)} %get-tuple-element.22.table_ref.refs_0_, f32[768,128]{1,0:T(8,128)S(1)} %get-tuple-element.23.part_ref, f32[768,128]{1,0:T(8,128)S(1)} %get-tuple-element.24.y_ref.refs_3_, f32[192,128]{1,0:T(8,128)S(1)} %get-tuple-element.25.refs_0_, ...), custom_call_target="tpu_custom_call" | custom-call | flops 10000000000 | bytes 1 | tf_op jit(solution)/shard_map/potential/pallas_call | solution.py:758
  30.1 1.5 %first.1.refs_1_ = f32[776,128]{1,0:T(8,128)S(1)} custom-call(s32[8,128]{1,0:T(8,128)S(1)} %get-tuple-element.22.table_ref.refs_0_, f32[768,128]{1,0:T(8,128)S(1)} %get-tuple-element.26.refs_1_, f32[512,128]{1,0:T(8,128)S(1)} %get-tuple-element.27.refs_2_.refs_5_, f32[8,128]{1,0:T(8,128)S(1)} %get-tuple-element.28.refs_3_, ...), custom_call_target="tpu_custom_call" | custom-call | flops 1 | bytes 1 | tf_op jit(solution)/shard_map/first/pallas_call | solution.py:772
  31.6 2.8 %collective-permute-done.9.refs_4_.refs_9_ = f32[64,1024]{1,0:T(8,128)S(1)} collective-permute-done((f32[64,1024]{1,0:T(8,128)S(1)}, f32[64,1024]{1,0:T(8,128)S(1)}, u32[]{:S(2)}, u32[]{:S(2)}) %collective-permute-start.9) | collective-permute-done | bytes 262176 | tf_op jit(solution)/shard_map/ppermute | solution.py:682
  34.7 1.0 %first_late.1.refs_1_.refs_3_ = f32[776,128]{1,0:T(8,128)S(1)} custom-call(s32[8,128]{1,0:T(8,128)S(1)} %get-tuple-element.22.table_ref.refs_0_, f32[776,128]{1,0:T(8,128)S(1)} %first.1.refs_1_, f32[512,128]{1,0:T(8,128)S(1)} %get-tuple-element.27.refs_2_.refs_5_, f32[8,128]{1,0:T(8,128)S(1)} %get-tuple-element.28.refs_3_, ...), custom_call_target="tpu_custom_call", output_to_operand_aliasing={{}: (1, {})} | custom-call | flops 1 | bytes 1 | tf_op jit(solution)/shard_map/first_late/pallas_call | solution.py:772
  35.8 1.7 %collective-permute-done.11.refs_2_ = f32[776,128]{1,0:T(8,128)S(1)} collective-permute-done((f32[776,128]{1,0:T(8,128)S(1)}, f32[776,128]{1,0:T(8,128)S(1)}, u32[]{:S(2)}, u32[]{:S(2)}) %collective-permute-start.11) | collective-permute-done | bytes 397344 | tf_op jit(solution)/shard_map/ppermute | solution.py:682
  37.6 2.4 %next.2.refs_1_.refs_3_ = f32[776,128]{1,0:T(8,128)S(1)} custom-call(s32[8,128]{1,0:T(8,128)S(1)} %get-tuple-element.22.table_ref.refs_0_, f32[776,128]{1,0:T(8,128)S(1)} %first_late.1.refs_1_.refs_3_, f32[776,128]{1,0:T(8,128)S(1)} %collective-permute-done.11.refs_2_, f32[768,128]{1,0:T(8,128)S(1)} %get-tuple-element.24.y_ref.refs_3_, ...), custom_call_target="tpu_custom_call" | custom-call | tf_op jit(solution)/shard_map/next/pallas_call | solution.py:785
  40.2 1.6 %collective-permute-done.12.refs_2_ = f32[776,128]{1,0:T(8,128)S(1)} collective-permute-done((f32[776,128]{1,0:T(8,128)S(1)}, f32[776,128]{1,0:T(8,128)S(1)}, u32[]{:S(2)}, u32[]{:S(2)}) %collective-permute-start.12) | collective-permute-done | bytes 397344 | tf_op jit(solution)/shard_map/ppermute | solution.py:682
  41.8 2.4 %next.3.refs_1_ = f32[776,128]{1,0:T(8,128)S(1)} custom-call(s32[8,128]{1,0:T(8,128)S(1)} %get-tuple-element.22.table_ref.refs_0_, f32[776,128]{1,0:T(8,128)S(1)} %next.2.refs_1_.refs_3_, f32[776,128]{1,0:T(8,128)S(1)} %collective-permute-done.12.refs_2_, f32[776,128]{1,0:T(8,128)S(1)} %first_late.1.refs_1_.refs_3_, ...), custom_call_target="tpu_custom_call" | custom-call | tf_op jit(solution)/shard_map/next/pallas_call | solution.py:785
  44.4 1.6 %collective-permute-done.13.refs_2_ = f32[776,128]{1,0:T(8,128)S(1)} collective-permute-done((f32[776,128]{1,0:T(8,128)S(1)}, f32[776,128]{1,0:T(8,128)S(1)}, u32[]{:S(2)}, u32[]{:S(2)}) %collective-permute-start.13) | collective-permute-done | bytes 397344 | tf_op jit(solution)/shard_map/ppermute | solution.py:682
  46.0 1.6 %last.1 = f32[192,128]{1,0:T(8,128)} custom-call(s32[8,128]{1,0:T(8,128)S(1)} %get-tuple-element.22.table_ref.refs_0_, f32[776,128]{1,0:T(8,128)S(1)} %next.3.refs_1_, f32[776,128]{1,0:T(8,128)S(1)} %collective-permute-done.13.refs_2_, f32[776,128]{1,0:T(8,128)S(1)} %next.2.refs_1_.refs_3_, f32[768,128]{1,0:T(8,128)S(1)} %get-tuple-element.32.refs_4_, ...), custom_call_target="tpu_custom_call" | custom-call | tf_op jit(solution)/shard_map/last/pallas_call | solution.py:785
  (16 shorter events, 1.8 us)
Async XLA Ops:
  1.4 7.9 %collective-permute-start.2 = (f32[264,128]{1,0:T(8,128)S(1)}, f32[264,128]{1,0:T(8,128)S(1)}, u32[]{:S(2)}, u32[]{:S(2)}) collective-permute-start(f32[264,128]{1,0:T(8,128)S(1)} %get-tuple-element.19.refs_0_), channel_id=1, source_target_pairs={{0,24},{4,28},{8,16},{12,20},{16,8},{20,12},{24,0},{28,4},{1,25},{... | collective-permute-start | bytes 405512 | tf_op jit(solution)/shard_map/ppermute | solution.py:682
  5.4 6.5 %collective-permute-start.1 = (f32[264,128]{1,0:T(8,128)S(1)}, f32[264,128]{1,0:T(8,128)S(1)}, u32[]{:S(2)}, u32[]{:S(2)}) collective-permute-start(f32[264,128]{1,0:T(8,128)S(1)} %get-tuple-element.19.refs_0_), channel_id=1, source_target_pairs={{0,16},{4,20},{8,24},{12,28},{16,0},{20,4},{24,8},{28,12},{1,17},{... | collective-permute-start | bytes 405512 | tf_op jit(solution)/shard_map/ppermute | solution.py:682
  5.9 6.2 %collective-permute-start = (f32[264,128]{1,0:T(8,128)S(1)}, f32[264,128]{1,0:T(8,128)S(1)}, u32[]{:S(2)}, u32[]{:S(2)}) collective-permute-start(f32[264,128]{1,0:T(8,128)S(1)} %get-tuple-element.19.refs_0_), channel_id=1, source_target_pairs={{0,8},{4,12},{8,0},{12,4},{16,24},{20,28},{24,16},{28,20},{1,9},{5... | collective-permute-start | bytes 405512 | tf_op jit(solution)/shard_map/ppermute | solution.py:682
  12.1 13.7 %collective-permute-start.8 = (f32[128,1024]{1,0:T(8,128)S(1)}, f32[128,1024]{1,0:T(8,128)S(1)}, u32[]{:S(2)}, u32[]{:S(2)}) collective-permute-start(f32[128,1024]{1,0:T(8,128)S(1)} %get-tuple-element.29.refs_4_.refs_6_), channel_id=1, source_target_pairs={{0,16},{4,20},{8,24},{12,28},{16,0},{20,4},{24,8},{28,12},{1,17},{... | collective-permute-start | bytes 1572872 | tf_op jit(solution)/shard_map/ppermute | solution.py:682
  13.7 13.6 %collective-permute-start.7 = (f32[128,1024]{1,0:T(8,128)S(1)}, f32[128,1024]{1,0:T(8,128)S(1)}, u32[]{:S(2)}, u32[]{:S(2)}) collective-permute-start(f32[128,1024]{1,0:T(8,128)S(1)} %get-tuple-element.29.refs_4_.refs_6_), channel_id=1, source_target_pairs={{0,8},{4,12},{8,0},{12,4},{16,24},{20,28},{24,16},{28,20},{1,9},{5... | collective-permute-start | bytes 1572872 | tf_op jit(solution)/shard_map/ppermute | solution.py:682
  14.3 4.5 %collective-permute-start.3 = (f32[864,128]{1,0:T(8,128)S(1)}, f32[864,128]{1,0:T(8,128)S(1)}, u32[]{:S(2)}, u32[]{:S(2)}) collective-permute-start(f32[864,128]{1,0:T(8,128)S(1)} %get-tuple-element.21.own_ref), channel_id=1, source_target_pairs={{0,4},{4,0},{8,12},{12,8},{16,20},{20,16},{24,28},{28,24},{1,5},{5... | collective-permute-start | bytes 1327112 | tf_op jit(solution)/shard_map/ppermute | solution.py:682
  15.1 14.2 %collective-permute-start.6 = (f32[192,128]{1,0:T(8,128)S(1)}, f32[192,128]{1,0:T(8,128)S(1)}, u32[]{:S(2)}, u32[]{:S(2)}) collective-permute-start(f32[192,128]{1,0:T(8,128)S(1)} %get-tuple-element.25.refs_0_), channel_id=1, source_target_pairs={{0,3},{1,0},{2,1},{3,2},{4,7},{5,4},{6,5},{7,6},{8,11},{9,8},{10,9... | collective-permute-start | bytes 294920 | tf_op jit(solution)/shard_map/ppermute | solution.py:724
  18.8 10.5 %collective-permute-start.5 = (f32[192,128]{1,0:T(8,128)S(1)}, f32[192,128]{1,0:T(8,128)S(1)}, u32[]{:S(2)}, u32[]{:S(2)}) collective-permute-start(f32[192,128]{1,0:T(8,128)S(1)} %get-tuple-element.25.refs_0_), channel_id=1, source_target_pairs={{0,2},{1,3},{2,0},{3,1},{4,6},{5,7},{6,4},{7,5},{8,10},{9,11},{10,... | collective-permute-start | bytes 294920 | tf_op jit(solution)/shard_map/ppermute | solution.py:724
  18.8 10.5 %collective-permute-start.4 = (f32[192,128]{1,0:T(8,128)S(1)}, f32[192,128]{1,0:T(8,128)S(1)}, u32[]{:S(2)}, u32[]{:S(2)}) collective-permute-start(f32[192,128]{1,0:T(8,128)S(1)} %get-tuple-element.25.refs_0_), channel_id=1, source_target_pairs={{0,1},{1,2},{2,3},{3,0},{4,5},{5,6},{6,7},{7,4},{8,9},{9,10},{10,1... | collective-permute-start | bytes 294920 | tf_op jit(solution)/shard_map/ppermute | solution.py:724
  27.3 7.1 %collective-permute-start.9 = (f32[64,1024]{1,0:T(8,128)S(1)}, f32[64,1024]{1,0:T(8,128)S(1)}, u32[]{:S(2)}, u32[]{:S(2)}) collective-permute-start(f32[64,1024]{1,0:T(8,128)S(1)} %get-tuple-element.30), channel_id=1, source_target_pairs={{0,16},{4,20},{8,24},{12,28},{16,0},{20,4},{24,8},{28,12},{1,17},{... | collective-permute-start | bytes 786440 | tf_op jit(solution)/shard_map/ppermute | solution.py:682
  27.7 7.0 %collective-permute-start.10 = (f32[64,1024]{1,0:T(8,128)S(1)}, f32[64,1024]{1,0:T(8,128)S(1)}, u32[]{:S(2)}, u32[]{:S(2)}) collective-permute-start(f32[64,1024]{1,0:T(8,128)S(1)} %get-tuple-element.31), channel_id=1, source_target_pairs={{0,8},{4,12},{8,0},{12,4},{16,24},{20,28},{24,16},{28,20},{1,9},{5... | collective-permute-start | bytes 786440 | tf_op jit(solution)/shard_map/ppermute | solution.py:682
  35.8 1.8 %collective-permute-start.11 = (f32[776,128]{1,0:T(8,128)S(1)}, f32[776,128]{1,0:T(8,128)S(1)}, u32[]{:S(2)}, u32[]{:S(2)}) collective-permute-start(f32[776,128]{1,0:T(8,128)S(1)} %first_late.1.refs_1_.refs_3_), channel_id=1, source_target_pairs={{0,4},{4,0},{8,12},{12,8},{16,20},{20,16},{24,28},{28,24},{1,5},{5... | collective-permute-start | bytes 1191944 | tf_op jit(solution)/shard_map/ppermute | solution.py:682
  40.0 1.8 %collective-permute-start.12 = (f32[776,128]{1,0:T(8,128)S(1)}, f32[776,128]{1,0:T(8,128)S(1)}, u32[]{:S(2)}, u32[]{:S(2)}) collective-permute-start(f32[776,128]{1,0:T(8,128)S(1)} %next.2.refs_1_.refs_3_), channel_id=1, source_target_pairs={{0,4},{4,0},{8,12},{12,8},{16,20},{20,16},{24,28},{28,24},{1,5},{5... | collective-permute-start | bytes 1191944 | tf_op jit(solution)/shard_map/ppermute | solution.py:682
  44.2 1.8 %collective-permute-start.13 = (f32[776,128]{1,0:T(8,128)S(1)}, f32[776,128]{1,0:T(8,128)S(1)}, u32[]{:S(2)}, u32[]{:S(2)}) collective-permute-start(f32[776,128]{1,0:T(8,128)S(1)} %next.3.refs_1_), channel_id=1, source_target_pairs={{0,4},{4,0},{8,12},{12,8},{16,20},{20,16},{24,28},{28,24},{1,5},{5... | collective-permute-start | bytes 1191944 | tf_op jit(solution)/shard_map/ppermute | solution.py:682

commit v8 on v7

--- a/solution.py
+++ b/solution.py
@@ -402,8 +402,12 @@
     pack_ref[small : small + 1, :] = partials(pack_ref, p_ref, off_ref, r_ref, dims)[0:1]
 
 
+def gate_kernel(*refs):
+    pass
+
+
 def sort_kernel(*refs):
-    packs, (pair_ref, v_ref) = refs[:-4], refs[-3:-1]
+    packs, (pair_ref, v_ref) = refs[:-2], refs[-2:]
     small = packs[0].shape[0] - SMALL
     size = SLAB + SMALL
     for local, pack in enumerate(packs):
@@ -703,20 +707,25 @@
         name="pack",
     )(*sources)
     packs = [pack] + [swap(pack, 2 * local) for local in range(1, half)]
-    own, v_piece, p = pl.pallas_call(
+    p = pl.pallas_call(
+        gate_kernel,
+        out_shape=jax.ShapeDtypeStruct(p.shape, f32),
+        in_specs=[VMEM, VMEM],
+        out_specs=VMEM,
+        input_output_aliases={1: 0},
+        compiler_params=params,
+        cost_estimate=small,
+        name="gate",
+    )(packs[3], p)
+    own, v_piece = pl.pallas_call(
         sort_kernel,
-        out_shape=(
-            shape(half * (SLAB + SMALL)),
-            shape(half * v_piece.shape[0]),
-            jax.ShapeDtypeStruct(p.shape, f32),
-        ),
-        in_specs=[VMEM] * (half + 1),
-        out_specs=(VMEM,) * 3,
-        input_output_aliases={half: 2},
+        out_shape=(shape(half * (SLAB + SMALL)), shape(half * v_piece.shape[0])),
+        in_specs=[VMEM] * half,
+        out_specs=(VMEM, VMEM),
         compiler_params=params,
         cost_estimate=small,
         name="sort",
-    )(*packs, p)
+    )(*packs)
     got = swap(own, 1)
     pieces = [v_piece]
     for back in range(1, nband):

time: 47.8 us -> 44.4 us (0.929)
  waiting for transfers between devices: 19.1 us -> 13.7 us
  starting transfers between devices: 14.1 us -> 15.9 us
    ppermute x11, waiting for transfers between devices: 19.1 us -> 11.7 us  [swap(): return lax.ppermute(x, 'domain', [(i, i ^ step) for i in range(n)])]
    ppermute x3, waiting for transfers between devices: 0.01 us -> 2.01 us  [chip_form(): pieces.append(lax.ppermute(v_piece, 'band', ring))]
    ppermute x11, starting transfers between devices: 9.34 us -> 11.3 us  [swap(): return lax.ppermute(x, 'domain', [(i, i ^ step) for i in range(n)])]
  transfers between devices with their start and end apart: 14 -> 14, of which waited for: 10 -> 9; matrix products, arithmetic and copies ran while one was open for 2% -> 2% of each run, Pallas kernels for 10% -> 11%
where the time goes in v8:
time: 44.4 us; the launch traced here: 44.2 us
  starting transfers between devices  15.9 us (36%)
  waiting for transfers between devices  13.7 us (31%)
  Pallas kernels  13.6 us (31%)
  local copies, waits for them, and re-layouts  0.7 us (2%)
    ppermute x11, waiting for transfers between devices, swap(): return lax.ppermute(x, 'domain', [(i, i ^ step) for i in range(n)])  11.7 us
    ppermute x11, starting transfers between devices, swap(): return lax.ppermute(x, 'domain', [(i, i ^ step) for i in range(n)])  11.3 us
    pallas_call x3, Pallas kernels, chip_form(): pl.pallas_call(functools.partial(chip_kernel, dims, last), out_shape=shap...  6.47 us
    ppermute x3, starting transfers between devices, chip_form(): pieces.append(lax.ppermute(v_piece, 'band', ring))  4.62 us
    pallas_call x2, Pallas kernels, chip_form(): pl.pallas_call(functools.partial(first_kernel, dims, slabs), out_shape=se...  2.5 us
    pallas_call x1, Pallas kernels, chip_form(): pl.pallas_call(functools.partial(begin_kernel, dims), out_shape=(shape(ha...  2.47 us
    ppermute x3, waiting for transfers between devices, chip_form(): pieces.append(lax.ppermute(v_piece, 'band', ring))  2.01 us
    pallas_call x1, Pallas kernels, chip_form(): pl.pallas_call(functools.partial(pack_kernel, dims), out_shape=(shape(SLA...  1.4 us
  transfers between devices with their start and end apart: 14, of which 9 were waited for; matrix products, arithmetic and copies ran while one was open for 2% of the time, Pallas kernels for 11%

profile of v8, /device:TPU:0, one launch (start us, length us, event | category | flops | bytes accessed | tf_op | source)
XLA Modules:
  0.0 44.2 jit_solution(15283214500903792377)
XLA Ops:
  0.0 1.4 %pack.1 = (f32[264,128]{1,0:T(8,128)S(1)}, f32[128,1024]{1,0:T(8,128)S(1)}) custom-call(f32[192,128]{1,0:T(8,128)} %bitcast.17, f32[128,1024]{1,0:T(8,128)} %bitcast.16, s32[2,8]{1,0:T(2,128)} %bitcast.20, s32[2,8]{1,0:T(2,128)} %bitcast.21, f32[64,32]{1,0:T(8,128)} %bitcast.18, f32[48,128]{1,0:T(8,128)} %bitcast.19), custom_call_target="tpu_custom_call" | custom-call | flops 1 | bytes 1 | tf_op jit(solution)/shard_map/pack/pallas_call | solution.py:690
  1.4 4.0 %collective-permute-start.2 = (f32[264,128]{1,0:T(8,128)S(1)}, f32[264,128]{1,0:T(8,128)S(1)}, u32[]{:S(2)}, u32[]{:S(2)}) collective-permute-start(f32[264,128]{1,0:T(8,128)S(1)} %get-tuple-element.18.refs_0_), channel_id=1, source_target_pairs={{0,24},{4,28},{8,16},{12,20},{16,8},{20,12},{24,0},{28,4},{1,25},{... | collective-permute-start | bytes 405512 | tf_op jit(solution)/shard_map/ppermute | solution.py:686
  5.4 0.5 %collective-permute-start.1 = (f32[264,128]{1,0:T(8,128)S(1)}, f32[264,128]{1,0:T(8,128)S(1)}, u32[]{:S(2)}, u32[]{:S(2)}) collective-permute-start(f32[264,128]{1,0:T(8,128)S(1)} %get-tuple-element.18.refs_0_), channel_id=1, source_target_pairs={{0,16},{4,20},{8,24},{12,28},{16,0},{20,4},{24,8},{28,12},{1,17},{... | collective-permute-start | bytes 405512 | tf_op jit(solution)/shard_map/ppermute | solution.py:686
  6.0 3.3 %collective-permute-done.2.refs_3_.refs_0_ = f32[264,128]{1,0:T(8,128)S(1)} collective-permute-done((f32[264,128]{1,0:T(8,128)S(1)}, f32[264,128]{1,0:T(8,128)S(1)}, u32[]{:S(2)}, u32[]{:S(2)}) %collective-permute-start.2) | collective-permute-done | bytes 135200 | tf_op jit(solution)/shard_map/ppermute | solution.py:686
  9.4 2.4 %collective-permute-start.8 = (f32[128,1024]{1,0:T(8,128)S(1)}, f32[128,1024]{1,0:T(8,128)S(1)}, u32[]{:S(2)}, u32[]{:S(2)}) collective-permute-start(f32[128,1024]{1,0:T(8,128)S(1)} %gate.1.refs_4_.refs_6_), channel_id=1, source_target_pairs={{0,16},{4,20},{8,24},{12,28},{16,0},{20,4},{24,8},{28,12},{1,17},{... | collective-permute-start | bytes 1572872 | tf_op jit(solution)/shard_map/ppermute | solution.py:686
  11.8 1.5 %collective-permute-start.7 = (f32[128,1024]{1,0:T(8,128)S(1)}, f32[128,1024]{1,0:T(8,128)S(1)}, u32[]{:S(2)}, u32[]{:S(2)}) collective-permute-start(f32[128,1024]{1,0:T(8,128)S(1)} %gate.1.refs_4_.refs_6_), channel_id=1, source_target_pairs={{0,8},{4,12},{8,0},{12,4},{16,24},{20,28},{24,16},{28,20},{1,9},{5... | collective-permute-start | bytes 1572872 | tf_op jit(solution)/shard_map/ppermute | solution.py:686
  13.4 0.7 %dynamic-slice_bitcast_fusion = s32[24]{0:T(128)S(1)} fusion(s32[8,24]{1,0:T(8,128)} %constant.15.clone, s32[]{:T(128)S(6)} %select_n.3), kind=kLoop, calls=%fused_computation.1 | loop fusion | bytes 196 | tf_op jit(solution)/shard_map/squeeze | solution.py:672
  14.2 3.6 %collective-permute-start.6 = (f32[192,128]{1,0:T(8,128)S(1)}, f32[192,128]{1,0:T(8,128)S(1)}, u32[]{:S(2)}, u32[]{:S(2)}) collective-permute-start(f32[192,128]{1,0:T(8,128)S(1)} %get-tuple-element.23.refs_0_), channel_id=1, source_target_pairs={{0,3},{1,0},{2,1},{3,2},{4,7},{5,4},{6,5},{7,6},{8,11},{9,8},{10,9... | collective-permute-start | bytes 294920 | tf_op jit(solution)/shard_map/ppermute | solution.py:733
  17.8 1.0 %collective-permute-start.4 = (f32[192,128]{1,0:T(8,128)S(1)}, f32[192,128]{1,0:T(8,128)S(1)}, u32[]{:S(2)}, u32[]{:S(2)}) collective-permute-start(f32[192,128]{1,0:T(8,128)S(1)} %get-tuple-element.23.refs_0_), channel_id=1, source_target_pairs={{0,1},{1,2},{2,3},{3,0},{4,5},{5,6},{6,7},{7,4},{8,9},{9,10},{10,1... | collective-permute-start | bytes 294920 | tf_op jit(solution)/shard_map/ppermute | solution.py:733
  18.8 2.5 %begin.1 = (f32[768,128]{1,0:T(8,128)S(1)}, f32[768,128]{1,0:T(8,128)S(1)}, f32[512,128]{1,0:T(8,128)S(1)}, f32[8,128]{1,0:T(8,128)S(1)}, s32[8,128]{1,0:T(8,128)S(1)}) custom-call(s32[25]{0:T(128)S(1)} %pad_add_fusion.info_ref, f32[864,128]{1,0:T(8,128)S(1)} %get-tuple-element.19.own_ref, f32[864,128]{1,0:T(8,128)S(1)} %collective-permute-done.3.got_ref), custom_call_target="tpu_custom_call" | custom-call | flops 1 | bytes 1 | tf_op jit(solution)/shard_map/begin/pallas_call | solution.py:750
  21.3 1.8 %collective-permute-done.8.refs_6_.y_ref.refs_8_ = f32[128,1024]{1,0:T(8,128)S(1)} collective-permute-done((f32[128,1024]{1,0:T(8,128)S(1)}, f32[128,1024]{1,0:T(8,128)S(1)}, u32[]{:S(2)}, u32[]{:S(2)}) %collective-permute-start.8) | collective-permute-done | bytes 524320 | tf_op jit(solution)/shard_map/ppermute | solution.py:686
  23.4 1.5 %collective-permute-start.9 = (f32[64,1024]{1,0:T(8,128)S(1)}, f32[64,1024]{1,0:T(8,128)S(1)}, u32[]{:S(2)}, u32[]{:S(2)}) collective-permute-start(f32[64,1024]{1,0:T(8,128)S(1)} %get-tuple-element.28), channel_id=1, source_target_pairs={{0,16},{4,20},{8,24},{12,28},{16,0},{20,4},{24,8},{28,12},{1,17},{... | collective-permute-start | bytes 786440 | tf_op jit(solution)/shard_map/ppermute | solution.py:686
  24.9 0.7 %collective-permute-start.10 = (f32[64,1024]{1,0:T(8,128)S(1)}, f32[64,1024]{1,0:T(8,128)S(1)}, u32[]{:S(2)}, u32[]{:S(2)}) collective-permute-start(f32[64,1024]{1,0:T(8,128)S(1)} %get-tuple-element.29), channel_id=1, source_target_pairs={{0,8},{4,12},{8,0},{12,4},{16,24},{20,28},{24,16},{28,20},{1,9},{5... | collective-permute-start | bytes 786440 | tf_op jit(solution)/shard_map/ppermute | solution.py:686
  25.6 2.0 %collective-permute-done.5.refs_2_ = f32[192,128]{1,0:T(8,128)S(1)} collective-permute-done((f32[192,128]{1,0:T(8,128)S(1)}, f32[192,128]{1,0:T(8,128)S(1)}, u32[]{:S(2)}, u32[]{:S(2)}) %collective-permute-start.5) | collective-permute-done | bytes 98336 | tf_op jit(solution)/shard_map/ppermute | solution.py:733
  27.6 0.7 %potential.1 = (f32[768,128]{1,0:T(8,128)S(1)}, f32[768,128]{1,0:T(8,128)S(1)}) custom-call(s32[8,128]{1,0:T(8,128)S(1)} %get-tuple-element.20.table_ref.refs_0_, f32[768,128]{1,0:T(8,128)S(1)} %get-tuple-element.21.part_ref, f32[768,128]{1,0:T(8,128)S(1)} %get-tuple-element.22.y_ref.refs_3_, f32[192,128]{1,0:T(8,128)S(1)} %get-tuple-element.23.refs_0_, ...), custom_call_target="tpu_custom_call" | custom-call | flops 10000000000 | bytes 1 | tf_op jit(solution)/shard_map/potential/pallas_call | solution.py:767
  28.3 1.5 %first.1.refs_1_ = f32[776,128]{1,0:T(8,128)S(1)} custom-call(s32[8,128]{1,0:T(8,128)S(1)} %get-tuple-element.20.table_ref.refs_0_, f32[768,128]{1,0:T(8,128)S(1)} %get-tuple-element.24.refs_1_, f32[512,128]{1,0:T(8,128)S(1)} %get-tuple-element.25.refs_2_.refs_5_, f32[8,128]{1,0:T(8,128)S(1)} %get-tuple-element.26.refs_3_, ...), custom_call_target="tpu_custom_call" | custom-call | flops 1 | bytes 1 | tf_op jit(solution)/shard_map/first/pallas_call | solution.py:781
  30.0 1.3 %collective-permute-done.10.refs_5_.refs_10_ = f32[64,1024]{1,0:T(8,128)S(1)} collective-permute-done((f32[64,1024]{1,0:T(8,128)S(1)}, f32[64,1024]{1,0:T(8,128)S(1)}, u32[]{:S(2)}, u32[]{:S(2)}) %collective-permute-start.10) | collective-permute-done | bytes 262176 | tf_op jit(solution)/shard_map/ppermute | solution.py:686
  31.3 1.0 %first_late.1.refs_1_.refs_3_ = f32[776,128]{1,0:T(8,128)S(1)} custom-call(s32[8,128]{1,0:T(8,128)S(1)} %get-tuple-element.20.table_ref.refs_0_, f32[776,128]{1,0:T(8,128)S(1)} %first.1.refs_1_, f32[512,128]{1,0:T(8,128)S(1)} %get-tuple-element.25.refs_2_.refs_5_, f32[8,128]{1,0:T(8,128)S(1)} %get-tuple-element.26.refs_3_, ...), custom_call_target="tpu_custom_call", output_to_operand_aliasing={{}: (1, {})} | custom-call | flops 1 | bytes 1 | tf_op jit(solution)/shard_map/first_late/pallas_call | solution.py:781
  32.4 1.7 %collective-permute-done.11.refs_2_ = f32[776,128]{1,0:T(8,128)S(1)} collective-permute-done((f32[776,128]{1,0:T(8,128)S(1)}, f32[776,128]{1,0:T(8,128)S(1)}, u32[]{:S(2)}, u32[]{:S(2)}) %collective-permute-start.11) | collective-permute-done | bytes 397344 | tf_op jit(solution)/shard_map/ppermute | solution.py:686
  34.1 2.5 %next.2.refs_1_.refs_3_ = f32[776,128]{1,0:T(8,128)S(1)} custom-call(s32[8,128]{1,0:T(8,128)S(1)} %get-tuple-element.20.table_ref.refs_0_, f32[776,128]{1,0:T(8,128)S(1)} %first_late.1.refs_1_.refs_3_, f32[776,128]{1,0:T(8,128)S(1)} %collective-permute-done.11.refs_2_, f32[768,128]{1,0:T(8,128)S(1)} %get-tuple-element.22.y_ref.refs_3_, ...), custom_call_target="tpu_custom_call" | custom-call | tf_op jit(solution)/shard_map/next/pallas_call | solution.py:794
  36.8 1.6 %collective-permute-done.12.refs_2_ = f32[776,128]{1,0:T(8,128)S(1)} collective-permute-done((f32[776,128]{1,0:T(8,128)S(1)}, f32[776,128]{1,0:T(8,128)S(1)}, u32[]{:S(2)}, u32[]{:S(2)}) %collective-permute-start.12) | collective-permute-done | bytes 397344 | tf_op jit(solution)/shard_map/ppermute | solution.py:686
  38.4 2.4 %next.3.refs_1_ = f32[776,128]{1,0:T(8,128)S(1)} custom-call(s32[8,128]{1,0:T(8,128)S(1)} %get-tuple-element.20.table_ref.refs_0_, f32[776,128]{1,0:T(8,128)S(1)} %next.2.refs_1_.refs_3_, f32[776,128]{1,0:T(8,128)S(1)} %collective-permute-done.12.refs_2_, f32[776,128]{1,0:T(8,128)S(1)} %first_late.1.refs_1_.refs_3_, ...), custom_call_target="tpu_custom_call" | custom-call | tf_op jit(solution)/shard_map/next/pallas_call | solution.py:794
  41.0 1.6 %collective-permute-done.13.refs_2_ = f32[776,128]{1,0:T(8,128)S(1)} collective-permute-done((f32[776,128]{1,0:T(8,128)S(1)}, f32[776,128]{1,0:T(8,128)S(1)}, u32[]{:S(2)}, u32[]{:S(2)}) %collective-permute-start.13) | collective-permute-done | bytes 397344 | tf_op jit(solution)/shard_map/ppermute | solution.py:686
  42.6 1.6 %last.1 = f32[192,128]{1,0:T(8,128)} custom-call(s32[8,128]{1,0:T(8,128)S(1)} %get-tuple-element.20.table_ref.refs_0_, f32[776,128]{1,0:T(8,128)S(1)} %next.3.refs_1_, f32[776,128]{1,0:T(8,128)S(1)} %collective-permute-done.13.refs_2_, f32[776,128]{1,0:T(8,128)S(1)} %next.2.refs_1_.refs_3_, f32[768,128]{1,0:T(8,128)S(1)} %get-tuple-element.30.refs_4_, ...), custom_call_target="tpu_custom_call" | custom-call | tf_op jit(solution)/shard_map/last/pallas_call | solution.py:794
  (17 shorter events, 1.2 us)
Async XLA Ops:
  1.4 8.0 %collective-permute-start.2 = (f32[264,128]{1,0:T(8,128)S(1)}, f32[264,128]{1,0:T(8,128)S(1)}, u32[]{:S(2)}, u32[]{:S(2)}) collective-permute-start(f32[264,128]{1,0:T(8,128)S(1)} %get-tuple-element.18.refs_0_), channel_id=1, source_target_pairs={{0,24},{4,28},{8,16},{12,20},{16,8},{20,12},{24,0},{28,4},{1,25},{... | collective-permute-start | bytes 405512 | tf_op jit(solution)/shard_map/ppermute | solution.py:686
  5.4 7.9 %collective-permute-start.1 = (f32[264,128]{1,0:T(8,128)S(1)}, f32[264,128]{1,0:T(8,128)S(1)}, u32[]{:S(2)}, u32[]{:S(2)}) collective-permute-start(f32[264,128]{1,0:T(8,128)S(1)} %get-tuple-element.18.refs_0_), channel_id=1, source_target_pairs={{0,16},{4,20},{8,24},{12,28},{16,0},{20,4},{24,8},{28,12},{1,17},{... | collective-permute-start | bytes 405512 | tf_op jit(solution)/shard_map/ppermute | solution.py:686
  5.9 7.4 %collective-permute-start = (f32[264,128]{1,0:T(8,128)S(1)}, f32[264,128]{1,0:T(8,128)S(1)}, u32[]{:S(2)}, u32[]{:S(2)}) collective-permute-start(f32[264,128]{1,0:T(8,128)S(1)} %get-tuple-element.18.refs_0_), channel_id=1, source_target_pairs={{0,8},{4,12},{8,0},{12,4},{16,24},{20,28},{24,16},{28,20},{1,9},{5... | collective-permute-start | bytes 405512 | tf_op jit(solution)/shard_map/ppermute | solution.py:686
  9.4 13.7 %collective-permute-start.8 = (f32[128,1024]{1,0:T(8,128)S(1)}, f32[128,1024]{1,0:T(8,128)S(1)}, u32[]{:S(2)}, u32[]{:S(2)}) collective-permute-start(f32[128,1024]{1,0:T(8,128)S(1)} %gate.1.refs_4_.refs_6_), channel_id=1, source_target_pairs={{0,16},{4,20},{8,24},{12,28},{16,0},{20,4},{24,8},{28,12},{1,17},{... | collective-permute-start | bytes 1572872 | tf_op jit(solution)/shard_map/ppermute | solution.py:686
  11.8 11.5 %collective-permute-start.7 = (f32[128,1024]{1,0:T(8,128)S(1)}, f32[128,1024]{1,0:T(8,128)S(1)}, u32[]{:S(2)}, u32[]{:S(2)}) collective-permute-start(f32[128,1024]{1,0:T(8,128)S(1)} %gate.1.refs_4_.refs_6_), channel_id=1, source_target_pairs={{0,8},{4,12},{8,0},{12,4},{16,24},{20,28},{24,16},{28,20},{1,9},{5... | collective-permute-start | bytes 1572872 | tf_op jit(solution)/shard_map/ppermute | solution.py:686
  13.4 4.5 %collective-permute-start.3 = (f32[864,128]{1,0:T(8,128)S(1)}, f32[864,128]{1,0:T(8,128)S(1)}, u32[]{:S(2)}, u32[]{:S(2)}) collective-permute-start(f32[864,128]{1,0:T(8,128)S(1)} %get-tuple-element.19.own_ref), channel_id=1, source_target_pairs={{0,4},{4,0},{8,12},{12,8},{16,20},{20,16},{24,28},{28,24},{1,5},{5... | collective-permute-start | bytes 1327112 | tf_op jit(solution)/shard_map/ppermute | solution.py:686
  14.2 11.4 %collective-permute-start.6 = (f32[192,128]{1,0:T(8,128)S(1)}, f32[192,128]{1,0:T(8,128)S(1)}, u32[]{:S(2)}, u32[]{:S(2)}) collective-permute-start(f32[192,128]{1,0:T(8,128)S(1)} %get-tuple-element.23.refs_0_), channel_id=1, source_target_pairs={{0,3},{1,0},{2,1},{3,2},{4,7},{5,4},{6,5},{7,6},{8,11},{9,8},{10,9... | collective-permute-start | bytes 294920 | tf_op jit(solution)/shard_map/ppermute | solution.py:733
  17.8 9.8 %collective-permute-start.5 = (f32[192,128]{1,0:T(8,128)S(1)}, f32[192,128]{1,0:T(8,128)S(1)}, u32[]{:S(2)}, u32[]{:S(2)}) collective-permute-start(f32[192,128]{1,0:T(8,128)S(1)} %get-tuple-element.23.refs_0_), channel_id=1, source_target_pairs={{0,2},{1,3},{2,0},{3,1},{4,6},{5,7},{6,4},{7,5},{8,10},{9,11},{10,... | collective-permute-start | bytes 294920 | tf_op jit(solution)/shard_map/ppermute | solution.py:733
  17.8 9.8 %collective-permute-start.4 = (f32[192,128]{1,0:T(8,128)S(1)}, f32[192,128]{1,0:T(8,128)S(1)}, u32[]{:S(2)}, u32[]{:S(2)}) collective-permute-start(f32[192,128]{1,0:T(8,128)S(1)} %get-tuple-element.23.refs_0_), channel_id=1, source_target_pairs={{0,1},{1,2},{2,3},{3,0},{4,5},{5,6},{6,7},{7,4},{8,9},{9,10},{10,1... | collective-permute-start | bytes 294920 | tf_op jit(solution)/shard_map/ppermute | solution.py:733
  23.4 6.6 %collective-permute-start.9 = (f32[64,1024]{1,0:T(8,128)S(1)}, f32[64,1024]{1,0:T(8,128)S(1)}, u32[]{:S(2)}, u32[]{:S(2)}) collective-permute-start(f32[64,1024]{1,0:T(8,128)S(1)} %get-tuple-element.28), channel_id=1, source_target_pairs={{0,16},{4,20},{8,24},{12,28},{16,0},{20,4},{24,8},{28,12},{1,17},{... | collective-permute-start | bytes 786440 | tf_op jit(solution)/shard_map/ppermute | solution.py:686
  24.9 6.4 %collective-permute-start.10 = (f32[64,1024]{1,0:T(8,128)S(1)}, f32[64,1024]{1,0:T(8,128)S(1)}, u32[]{:S(2)}, u32[]{:S(2)}) collective-permute-start(f32[64,1024]{1,0:T(8,128)S(1)} %get-tuple-element.29), channel_id=1, source_target_pairs={{0,8},{4,12},{8,0},{12,4},{16,24},{20,28},{24,16},{28,20},{1,9},{5... | collective-permute-start | bytes 786440 | tf_op jit(solution)/shard_map/ppermute | solution.py:686
  32.3 1.8 %collective-permute-start.11 = (f32[776,128]{1,0:T(8,128)S(1)}, f32[776,128]{1,0:T(8,128)S(1)}, u32[]{:S(2)}, u32[]{:S(2)}) collective-permute-start(f32[776,128]{1,0:T(8,128)S(1)} %first_late.1.refs_1_.refs_3_), channel_id=1, source_target_pairs={{0,4},{4,0},{8,12},{12,8},{16,20},{20,16},{24,28},{28,24},{1,5},{5... | collective-permute-start | bytes 1191944 | tf_op jit(solution)/shard_map/ppermute | solution.py:686
  36.6 1.8 %collective-permute-start.12 = (f32[776,128]{1,0:T(8,128)S(1)}, f32[776,128]{1,0:T(8,128)S(1)}, u32[]{:S(2)}, u32[]{:S(2)}) collective-permute-start(f32[776,128]{1,0:T(8,128)S(1)} %next.2.refs_1_.refs_3_), channel_id=1, source_target_pairs={{0,4},{4,0},{8,12},{12,8},{16,20},{20,16},{24,28},{28,24},{1,5},{5... | collective-permute-start | bytes 1191944 | tf_op jit(solution)/shard_map/ppermute | solution.py:686
  40.8 1.8 %collective-permute-start.13 = (f32[776,128]{1,0:T(8,128)S(1)}, f32[776,128]{1,0:T(8,128)S(1)}, u32[]{:S(2)}, u32[]{:S(2)}) collective-permute-start(f32[776,128]{1,0:T(8,128)S(1)} %next.3.refs_1_), channel_id=1, source_target_pairs={{0,4},{4,0},{8,12},{12,8},{16,20},{20,16},{24,28},{28,24},{1,5},{5... | collective-permute-start | bytes 1191944 | tf_op jit(solution)/shard_map/ppermute | solution.py:686

commit v9 on v8

--- a/solution.py
+++ b/solution.py
@@ -327,7 +327,7 @@
     along_z = jnp.dot(
         y_ref[0 : slabs * SLAB, :],
         circulant_z(),
-        precision=highest,
+        precision=lax.Precision.HIGH,
         preferred_element_type=f32,
     )
     below, above = bases()

time: 44.4 us -> 43.9 us (0.989)
  Pallas kernels: 13.6 us -> 13 us
  transfers between devices with their start and end apart: 14 -> 14, of which waited for: 9 -> 9; matrix products, arithmetic and copies ran while one was open for 2% -> 2% of each run, Pallas kernels for 11% -> 10%
where the time goes in v9:
time: 43.9 us; the launch traced here: 43.8 us
  starting transfers between devices  15.9 us (36%)
  waiting for transfers between devices  14 us (32%)
  Pallas kernels  13 us (30%)
  local copies, waits for them, and re-layouts  0.7 us (2%)
    ppermute x11, waiting for transfers between devices, swap(): return lax.ppermute(x, 'domain', [(i, i ^ step) for i in range(n)])  12 us
    ppermute x11, starting transfers between devices, swap(): return lax.ppermute(x, 'domain', [(i, i ^ step) for i in range(n)])  11.3 us
    pallas_call x3, Pallas kernels, chip_form(): pl.pallas_call(functools.partial(chip_kernel, dims, last), out_shape=shap...  6.06 us
    ppermute x3, starting transfers between devices, chip_form(): pieces.append(lax.ppermute(v_piece, 'band', ring))  4.62 us
    pallas_call x2, Pallas kernels, chip_form(): pl.pallas_call(functools.partial(first_kernel, dims, slabs), out_shape=se...  2.5 us
    pallas_call x1, Pallas kernels, chip_form(): pl.pallas_call(functools.partial(begin_kernel, dims), out_shape=(shape(ha...  2.2 us
    ppermute x3, waiting for transfers between devices, chip_form(): pieces.append(lax.ppermute(v_piece, 'band', ring))  2.01 us
    pallas_call x1, Pallas kernels, chip_form(): pl.pallas_call(functools.partial(pack_kernel, dims), out_shape=(shape(SLA...  1.4 us
  transfers between devices with their start and end apart: 14, of which 9 were waited for; matrix products, arithmetic and copies ran while one was open for 2% of the time, Pallas kernels for 10%

profile of v9, /device:TPU:0, one launch (start us, length us, event | category | flops | bytes accessed | tf_op | source)
XLA Modules:
  0.0 43.8 jit_solution(8148187250249749523)
XLA Ops:
  0.0 1.4 %pack.1 = (f32[264,128]{1,0:T(8,128)S(1)}, f32[128,1024]{1,0:T(8,128)S(1)}) custom-call(f32[192,128]{1,0:T(8,128)} %bitcast.17, f32[128,1024]{1,0:T(8,128)} %bitcast.16, s32[2,8]{1,0:T(2,128)} %bitcast.20, s32[2,8]{1,0:T(2,128)} %bitcast.21, f32[64,32]{1,0:T(8,128)} %bitcast.18, f32[48,128]{1,0:T(8,128)} %bitcast.19), custom_call_target="tpu_custom_call" | custom-call | flops 1 | bytes 1 | tf_op jit(solution)/shard_map/pack/pallas_call | solution.py:690
  1.4 4.0 %collective-permute-start.2 = (f32[264,128]{1,0:T(8,128)S(1)}, f32[264,128]{1,0:T(8,128)S(1)}, u32[]{:S(2)}, u32[]{:S(2)}) collective-permute-start(f32[264,128]{1,0:T(8,128)S(1)} %get-tuple-element.18.refs_0_), channel_id=1, source_target_pairs={{0,24},{4,28},{8,16},{12,20},{16,8},{20,12},{24,0},{28,4},{1,25},{... | collective-permute-start | bytes 405512 | tf_op jit(solution)/shard_map/ppermute | solution.py:686
  5.4 0.5 %collective-permute-start.1 = (f32[264,128]{1,0:T(8,128)S(1)}, f32[264,128]{1,0:T(8,128)S(1)}, u32[]{:S(2)}, u32[]{:S(2)}) collective-permute-start(f32[264,128]{1,0:T(8,128)S(1)} %get-tuple-element.18.refs_0_), channel_id=1, source_target_pairs={{0,16},{4,20},{8,24},{12,28},{16,0},{20,4},{24,8},{28,12},{1,17},{... | collective-permute-start | bytes 405512 | tf_op jit(solution)/shard_map/ppermute | solution.py:686
  6.0 3.3 %collective-permute-done.2.refs_3_.refs_0_ = f32[264,128]{1,0:T(8,128)S(1)} collective-permute-done((f32[264,128]{1,0:T(8,128)S(1)}, f32[264,128]{1,0:T(8,128)S(1)}, u32[]{:S(2)}, u32[]{:S(2)}) %collective-permute-start.2) | collective-permute-done | bytes 135200 | tf_op jit(solution)/shard_map/ppermute | solution.py:686
  9.4 2.5 %collective-permute-start.8 = (f32[128,1024]{1,0:T(8,128)S(1)}, f32[128,1024]{1,0:T(8,128)S(1)}, u32[]{:S(2)}, u32[]{:S(2)}) collective-permute-start(f32[128,1024]{1,0:T(8,128)S(1)} %gate.1.refs_4_.refs_6_), channel_id=1, source_target_pairs={{0,16},{4,20},{8,24},{12,28},{16,0},{20,4},{24,8},{28,12},{1,17},{... | collective-permute-start | bytes 1572872 | tf_op jit(solution)/shard_map/ppermute | solution.py:686
  11.8 1.5 %collective-permute-start.7 = (f32[128,1024]{1,0:T(8,128)S(1)}, f32[128,1024]{1,0:T(8,128)S(1)}, u32[]{:S(2)}, u32[]{:S(2)}) collective-permute-start(f32[128,1024]{1,0:T(8,128)S(1)} %gate.1.refs_4_.refs_6_), channel_id=1, source_target_pairs={{0,8},{4,12},{8,0},{12,4},{16,24},{20,28},{24,16},{28,20},{1,9},{5... | collective-permute-start | bytes 1572872 | tf_op jit(solution)/shard_map/ppermute | solution.py:686
  13.4 0.7 %dynamic-slice_bitcast_fusion = s32[24]{0:T(128)S(1)} fusion(s32[8,24]{1,0:T(8,128)} %constant.15.clone, s32[]{:T(128)S(6)} %select_n.3), kind=kLoop, calls=%fused_computation.1 | loop fusion | bytes 196 | tf_op jit(solution)/shard_map/squeeze | solution.py:672
  14.2 3.6 %collective-permute-start.6 = (f32[192,128]{1,0:T(8,128)S(1)}, f32[192,128]{1,0:T(8,128)S(1)}, u32[]{:S(2)}, u32[]{:S(2)}) collective-permute-start(f32[192,128]{1,0:T(8,128)S(1)} %get-tuple-element.23.refs_0_), channel_id=1, source_target_pairs={{0,3},{1,0},{2,1},{3,2},{4,7},{5,4},{6,5},{7,6},{8,11},{9,8},{10,9... | collective-permute-start | bytes 294920 | tf_op jit(solution)/shard_map/ppermute | solution.py:733
  17.8 1.0 %collective-permute-start.4 = (f32[192,128]{1,0:T(8,128)S(1)}, f32[192,128]{1,0:T(8,128)S(1)}, u32[]{:S(2)}, u32[]{:S(2)}) collective-permute-start(f32[192,128]{1,0:T(8,128)S(1)} %get-tuple-element.23.refs_0_), channel_id=1, source_target_pairs={{0,1},{1,2},{2,3},{3,0},{4,5},{5,6},{6,7},{7,4},{8,9},{9,10},{10,1... | collective-permute-start | bytes 294920 | tf_op jit(solution)/shard_map/ppermute | solution.py:733
  18.8 2.2 %begin.1 = (f32[768,128]{1,0:T(8,128)S(1)}, f32[768,128]{1,0:T(8,128)S(1)}, f32[512,128]{1,0:T(8,128)S(1)}, f32[8,128]{1,0:T(8,128)S(1)}, s32[8,128]{1,0:T(8,128)S(1)}) custom-call(s32[25]{0:T(128)S(1)} %pad_add_fusion.info_ref, f32[864,128]{1,0:T(8,128)S(1)} %get-tuple-element.19.own_ref, f32[864,128]{1,0:T(8,128)S(1)} %collective-permute-done.3.got_ref), custom_call_target="tpu_custom_call" | custom-call | flops 1 | bytes 1 | tf_op jit(solution)/shard_map/begin/pallas_call | solution.py:750
  21.0 2.0 %collective-permute-done.8.refs_6_.y_ref.refs_8_ = f32[128,1024]{1,0:T(8,128)S(1)} collective-permute-done((f32[128,1024]{1,0:T(8,128)S(1)}, f32[128,1024]{1,0:T(8,128)S(1)}, u32[]{:S(2)}, u32[]{:S(2)}) %collective-permute-start.8) | collective-permute-done | bytes 524320 | tf_op jit(solution)/shard_map/ppermute | solution.py:686
  23.4 1.5 %collective-permute-start.9 = (f32[64,1024]{1,0:T(8,128)S(1)}, f32[64,1024]{1,0:T(8,128)S(1)}, u32[]{:S(2)}, u32[]{:S(2)}) collective-permute-start(f32[64,1024]{1,0:T(8,128)S(1)} %get-tuple-element.28), channel_id=1, source_target_pairs={{0,16},{4,20},{8,24},{12,28},{16,0},{20,4},{24,8},{28,12},{1,17},{... | collective-permute-start | bytes 786440 | tf_op jit(solution)/shard_map/ppermute | solution.py:686
  24.9 0.7 %collective-permute-start.10 = (f32[64,1024]{1,0:T(8,128)S(1)}, f32[64,1024]{1,0:T(8,128)S(1)}, u32[]{:S(2)}, u32[]{:S(2)}) collective-permute-start(f32[64,1024]{1,0:T(8,128)S(1)} %get-tuple-element.29), channel_id=1, source_target_pairs={{0,8},{4,12},{8,0},{12,4},{16,24},{20,28},{24,16},{28,20},{1,9},{5... | collective-permute-start | bytes 786440 | tf_op jit(solution)/shard_map/ppermute | solution.py:686
  25.6 2.0 %collective-permute-done.5.refs_2_ = f32[192,128]{1,0:T(8,128)S(1)} collective-permute-done((f32[192,128]{1,0:T(8,128)S(1)}, f32[192,128]{1,0:T(8,128)S(1)}, u32[]{:S(2)}, u32[]{:S(2)}) %collective-permute-start.5) | collective-permute-done | bytes 98336 | tf_op jit(solution)/shard_map/ppermute | solution.py:733
  27.6 0.7 %potential.1 = (f32[768,128]{1,0:T(8,128)S(1)}, f32[768,128]{1,0:T(8,128)S(1)}) custom-call(s32[8,128]{1,0:T(8,128)S(1)} %get-tuple-element.20.table_ref.refs_0_, f32[768,128]{1,0:T(8,128)S(1)} %get-tuple-element.21.part_ref, f32[768,128]{1,0:T(8,128)S(1)} %get-tuple-element.22.y_ref.refs_3_, f32[192,128]{1,0:T(8,128)S(1)} %get-tuple-element.23.refs_0_, ...), custom_call_target="tpu_custom_call" | custom-call | flops 10000000000 | bytes 1 | tf_op jit(solution)/shard_map/potential/pallas_call | solution.py:767
  28.3 1.5 %first.1.refs_1_ = f32[776,128]{1,0:T(8,128)S(1)} custom-call(s32[8,128]{1,0:T(8,128)S(1)} %get-tuple-element.20.table_ref.refs_0_, f32[768,128]{1,0:T(8,128)S(1)} %get-tuple-element.24.refs_1_, f32[512,128]{1,0:T(8,128)S(1)} %get-tuple-element.25.refs_2_.refs_5_, f32[8,128]{1,0:T(8,128)S(1)} %get-tuple-element.26.refs_3_, ...), custom_call_target="tpu_custom_call" | custom-call | flops 1 | bytes 1 | tf_op jit(solution)/shard_map/first/pallas_call | solution.py:781
  29.9 1.3 %collective-permute-done.10.refs_5_.refs_10_ = f32[64,1024]{1,0:T(8,128)S(1)} collective-permute-done((f32[64,1024]{1,0:T(8,128)S(1)}, f32[64,1024]{1,0:T(8,128)S(1)}, u32[]{:S(2)}, u32[]{:S(2)}) %collective-permute-start.10) | collective-permute-done | bytes 262176 | tf_op jit(solution)/shard_map/ppermute | solution.py:686
  31.3 1.0 %first_late.1.refs_1_.refs_3_ = f32[776,128]{1,0:T(8,128)S(1)} custom-call(s32[8,128]{1,0:T(8,128)S(1)} %get-tuple-element.20.table_ref.refs_0_, f32[776,128]{1,0:T(8,128)S(1)} %first.1.refs_1_, f32[512,128]{1,0:T(8,128)S(1)} %get-tuple-element.25.refs_2_.refs_5_, f32[8,128]{1,0:T(8,128)S(1)} %get-tuple-element.26.refs_3_, ...), custom_call_target="tpu_custom_call", output_to_operand_aliasing={{}: (1, {})} | custom-call | flops 1 | bytes 1 | tf_op jit(solution)/shard_map/first_late/pallas_call | solution.py:781
  32.4 1.7 %collective-permute-done.11.refs_2_ = f32[776,128]{1,0:T(8,128)S(1)} collective-permute-done((f32[776,128]{1,0:T(8,128)S(1)}, f32[776,128]{1,0:T(8,128)S(1)}, u32[]{:S(2)}, u32[]{:S(2)}) %collective-permute-start.11) | collective-permute-done | bytes 397344 | tf_op jit(solution)/shard_map/ppermute | solution.py:686
  34.1 2.3 %next.2.refs_1_.refs_3_ = f32[776,128]{1,0:T(8,128)S(1)} custom-call(s32[8,128]{1,0:T(8,128)S(1)} %get-tuple-element.20.table_ref.refs_0_, f32[776,128]{1,0:T(8,128)S(1)} %first_late.1.refs_1_.refs_3_, f32[776,128]{1,0:T(8,128)S(1)} %collective-permute-done.11.refs_2_, f32[768,128]{1,0:T(8,128)S(1)} %get-tuple-element.22.y_ref.refs_3_, ...), custom_call_target="tpu_custom_call" | custom-call | tf_op jit(solution)/shard_map/next/pallas_call | solution.py:794
  36.6 1.6 %collective-permute-done.12.refs_2_ = f32[776,128]{1,0:T(8,128)S(1)} collective-permute-done((f32[776,128]{1,0:T(8,128)S(1)}, f32[776,128]{1,0:T(8,128)S(1)}, u32[]{:S(2)}, u32[]{:S(2)}) %collective-permute-start.12) | collective-permute-done | bytes 397344 | tf_op jit(solution)/shard_map/ppermute | solution.py:686
  38.2 2.2 %next.3.refs_1_ = f32[776,128]{1,0:T(8,128)S(1)} custom-call(s32[8,128]{1,0:T(8,128)S(1)} %get-tuple-element.20.table_ref.refs_0_, f32[776,128]{1,0:T(8,128)S(1)} %next.2.refs_1_.refs_3_, f32[776,128]{1,0:T(8,128)S(1)} %collective-permute-done.12.refs_2_, f32[776,128]{1,0:T(8,128)S(1)} %first_late.1.refs_1_.refs_3_, ...), custom_call_target="tpu_custom_call" | custom-call | tf_op jit(solution)/shard_map/next/pallas_call | solution.py:794
  40.6 1.6 %collective-permute-done.13.refs_2_ = f32[776,128]{1,0:T(8,128)S(1)} collective-permute-done((f32[776,128]{1,0:T(8,128)S(1)}, f32[776,128]{1,0:T(8,128)S(1)}, u32[]{:S(2)}, u32[]{:S(2)}) %collective-permute-start.13) | collective-permute-done | bytes 397344 | tf_op jit(solution)/shard_map/ppermute | solution.py:686
  42.2 1.6 %last.1 = f32[192,128]{1,0:T(8,128)} custom-call(s32[8,128]{1,0:T(8,128)S(1)} %get-tuple-element.20.table_ref.refs_0_, f32[776,128]{1,0:T(8,128)S(1)} %next.3.refs_1_, f32[776,128]{1,0:T(8,128)S(1)} %collective-permute-done.13.refs_2_, f32[776,128]{1,0:T(8,128)S(1)} %next.2.refs_1_.refs_3_, f32[768,128]{1,0:T(8,128)S(1)} %get-tuple-element.30.refs_4_, ...), custom_call_target="tpu_custom_call" | custom-call | tf_op jit(solution)/shard_map/last/pallas_call | solution.py:794
  (17 shorter events, 1.2 us)
Async XLA Ops:
  1.4 7.9 %collective-permute-start.2 = (f32[264,128]{1,0:T(8,128)S(1)}, f32[264,128]{1,0:T(8,128)S(1)}, u32[]{:S(2)}, u32[]{:S(2)}) collective-permute-start(f32[264,128]{1,0:T(8,128)S(1)} %get-tuple-element.18.refs_0_), channel_id=1, source_target_pairs={{0,24},{4,28},{8,16},{12,20},{16,8},{20,12},{24,0},{28,4},{1,25},{... | collective-permute-start | bytes 405512 | tf_op jit(solution)/shard_map/ppermute | solution.py:686
  5.4 7.9 %collective-permute-start.1 = (f32[264,128]{1,0:T(8,128)S(1)}, f32[264,128]{1,0:T(8,128)S(1)}, u32[]{:S(2)}, u32[]{:S(2)}) collective-permute-start(f32[264,128]{1,0:T(8,128)S(1)} %get-tuple-element.18.refs_0_), channel_id=1, source_target_pairs={{0,16},{4,20},{8,24},{12,28},{16,0},{20,4},{24,8},{28,12},{1,17},{... | collective-permute-start | bytes 405512 | tf_op jit(solution)/shard_map/ppermute | solution.py:686
  5.9 7.4 %collective-permute-start = (f32[264,128]{1,0:T(8,128)S(1)}, f32[264,128]{1,0:T(8,128)S(1)}, u32[]{:S(2)}, u32[]{:S(2)}) collective-permute-start(f32[264,128]{1,0:T(8,128)S(1)} %get-tuple-element.18.refs_0_), channel_id=1, source_target_pairs={{0,8},{4,12},{8,0},{12,4},{16,24},{20,28},{24,16},{28,20},{1,9},{5... | collective-permute-start | bytes 405512 | tf_op jit(solution)/shard_map/ppermute | solution.py:686
  9.4 13.7 %collective-permute-start.8 = (f32[128,1024]{1,0:T(8,128)S(1)}, f32[128,1024]{1,0:T(8,128)S(1)}, u32[]{:S(2)}, u32[]{:S(2)}) collective-permute-start(f32[128,1024]{1,0:T(8,128)S(1)} %gate.1.refs_4_.refs_6_), channel_id=1, source_target_pairs={{0,16},{4,20},{8,24},{12,28},{16,0},{20,4},{24,8},{28,12},{1,17},{... | collective-permute-start | bytes 1572872 | tf_op jit(solution)/shard_map/ppermute | solution.py:686
  11.8 11.5 %collective-permute-start.7 = (f32[128,1024]{1,0:T(8,128)S(1)}, f32[128,1024]{1,0:T(8,128)S(1)}, u32[]{:S(2)}, u32[]{:S(2)}) collective-permute-start(f32[128,1024]{1,0:T(8,128)S(1)} %gate.1.refs_4_.refs_6_), channel_id=1, source_target_pairs={{0,8},{4,12},{8,0},{12,4},{16,24},{20,28},{24,16},{28,20},{1,9},{5... | collective-permute-start | bytes 1572872 | tf_op jit(solution)/shard_map/ppermute | solution.py:686
  13.4 4.5 %collective-permute-start.3 = (f32[864,128]{1,0:T(8,128)S(1)}, f32[864,128]{1,0:T(8,128)S(1)}, u32[]{:S(2)}, u32[]{:S(2)}) collective-permute-start(f32[864,128]{1,0:T(8,128)S(1)} %get-tuple-element.19.own_ref), channel_id=1, source_target_pairs={{0,4},{4,0},{8,12},{12,8},{16,20},{20,16},{24,28},{28,24},{1,5},{5... | collective-permute-start | bytes 1327112 | tf_op jit(solution)/shard_map/ppermute | solution.py:686
  14.2 11.4 %collective-permute-start.6 = (f32[192,128]{1,0:T(8,128)S(1)}, f32[192,128]{1,0:T(8,128)S(1)}, u32[]{:S(2)}, u32[]{:S(2)}) collective-permute-start(f32[192,128]{1,0:T(8,128)S(1)} %get-tuple-element.23.refs_0_), channel_id=1, source_target_pairs={{0,3},{1,0},{2,1},{3,2},{4,7},{5,4},{6,5},{7,6},{8,11},{9,8},{10,9... | collective-permute-start | bytes 294920 | tf_op jit(solution)/shard_map/ppermute | solution.py:733
  17.8 9.8 %collective-permute-start.5 = (f32[192,128]{1,0:T(8,128)S(1)}, f32[192,128]{1,0:T(8,128)S(1)}, u32[]{:S(2)}, u32[]{:S(2)}) collective-permute-start(f32[192,128]{1,0:T(8,128)S(1)} %get-tuple-element.23.refs_0_), channel_id=1, source_target_pairs={{0,2},{1,3},{2,0},{3,1},{4,6},{5,7},{6,4},{7,5},{8,10},{9,11},{10,... | collective-permute-start | bytes 294920 | tf_op jit(solution)/shard_map/ppermute | solution.py:733
  17.8 9.8 %collective-permute-start.4 = (f32[192,128]{1,0:T(8,128)S(1)}, f32[192,128]{1,0:T(8,128)S(1)}, u32[]{:S(2)}, u32[]{:S(2)}) collective-permute-start(f32[192,128]{1,0:T(8,128)S(1)} %get-tuple-element.23.refs_0_), channel_id=1, source_target_pairs={{0,1},{1,2},{2,3},{3,0},{4,5},{5,6},{6,7},{7,4},{8,9},{9,10},{10,1... | collective-permute-start | bytes 294920 | tf_op jit(solution)/shard_map/ppermute | solution.py:733
  23.4 6.6 %collective-permute-start.9 = (f32[64,1024]{1,0:T(8,128)S(1)}, f32[64,1024]{1,0:T(8,128)S(1)}, u32[]{:S(2)}, u32[]{:S(2)}) collective-permute-start(f32[64,1024]{1,0:T(8,128)S(1)} %get-tuple-element.28), channel_id=1, source_target_pairs={{0,16},{4,20},{8,24},{12,28},{16,0},{20,4},{24,8},{28,12},{1,17},{... | collective-permute-start | bytes 786440 | tf_op jit(solution)/shard_map/ppermute | solution.py:686
  24.9 6.4 %collective-permute-start.10 = (f32[64,1024]{1,0:T(8,128)S(1)}, f32[64,1024]{1,0:T(8,128)S(1)}, u32[]{:S(2)}, u32[]{:S(2)}) collective-permute-start(f32[64,1024]{1,0:T(8,128)S(1)} %get-tuple-element.29), channel_id=1, source_target_pairs={{0,8},{4,12},{8,0},{12,4},{16,24},{20,28},{24,16},{28,20},{1,9},{5... | collective-permute-start | bytes 786440 | tf_op jit(solution)/shard_map/ppermute | solution.py:686
  32.3 1.8 %collective-permute-start.11 = (f32[776,128]{1,0:T(8,128)S(1)}, f32[776,128]{1,0:T(8,128)S(1)}, u32[]{:S(2)}, u32[]{:S(2)}) collective-permute-start(f32[776,128]{1,0:T(8,128)S(1)} %first_late.1.refs_1_.refs_3_), channel_id=1, source_target_pairs={{0,4},{4,0},{8,12},{12,8},{16,20},{20,16},{24,28},{28,24},{1,5},{5... | collective-permute-start | bytes 1191944 | tf_op jit(solution)/shard_map/ppermute | solution.py:686
  36.4 1.8 %collective-permute-start.12 = (f32[776,128]{1,0:T(8,128)S(1)}, f32[776,128]{1,0:T(8,128)S(1)}, u32[]{:S(2)}, u32[]{:S(2)}) collective-permute-start(f32[776,128]{1,0:T(8,128)S(1)} %next.2.refs_1_.refs_3_), channel_id=1, source_target_pairs={{0,4},{4,0},{8,12},{12,8},{16,20},{20,16},{24,28},{28,24},{1,5},{5... | collective-permute-start | bytes 1191944 | tf_op jit(solution)/shard_map/ppermute | solution.py:686
  40.4 1.8 %collective-permute-start.13 = (f32[776,128]{1,0:T(8,128)S(1)}, f32[776,128]{1,0:T(8,128)S(1)}, u32[]{:S(2)}, u32[]{:S(2)}) collective-permute-start(f32[776,128]{1,0:T(8,128)S(1)} %next.3.refs_1_), channel_id=1, source_target_pairs={{0,4},{4,0},{8,12},{12,8},{16,20},{20,16},{24,28},{28,24},{1,5},{5... | collective-permute-start | bytes 1191944 | tf_op jit(solution)/shard_map/ppermute | solution.py:686

commit v10 on v9

--- a/solution.py
+++ b/solution.py
@@ -558,7 +558,7 @@
         jnp.ones((8, 128), f32),
         r_ref[...],
         (((1,), (1,)), ((), ())),
-        precision=highest,
+        precision=lax.Precision.HIGH,
         preferred_element_type=f32,
     )
     for index, slab in enumerate(slabs):

time: 43.9 us -> 43.6 us (level)
  Pallas kernels: 13 us -> 12.5 us
where the time goes in v10:
time: 43.6 us; the launch traced here: 43.5 us
  starting transfers between devices  15.9 us (36%)
  waiting for transfers between devices  14.1 us (32%)
  Pallas kernels  12.5 us (29%)
  local copies, waits for them, and re-layouts  0.7 us (2%)
    ppermute x11, waiting for transfers between devices, swap(): return lax.ppermute(x, 'domain', [(i, i ^ step) for i in range(n)])  12.1 us
    ppermute x11, starting transfers between devices, swap(): return lax.ppermute(x, 'domain', [(i, i ^ step) for i in range(n)])  11.3 us
    pallas_call x3, Pallas kernels, chip_form(): pl.pallas_call(functools.partial(chip_kernel, dims, last), out_shape=shap...  5.78 us
    ppermute x3, starting transfers between devices, chip_form(): pieces.append(lax.ppermute(v_piece, 'band', ring))  4.61 us
    pallas_call x2, Pallas kernels, chip_form(): pl.pallas_call(functools.partial(first_kernel, dims, slabs), out_shape=se...  2.35 us
    pallas_call x1, Pallas kernels, chip_form(): pl.pallas_call(functools.partial(begin_kernel, dims), out_shape=(shape(ha...  2.2 us
    ppermute x3, waiting for transfers between devices, chip_form(): pieces.append(lax.ppermute(v_piece, 'band', ring))  2.01 us
    pallas_call x1, Pallas kernels, chip_form(): pl.pallas_call(functools.partial(pack_kernel, dims), out_shape=(shape(SLA...  1.41 us
  transfers between devices with their start and end apart: 14, of which 9 were waited for; matrix products, arithmetic and copies ran while one was open for 2% of the time, Pallas kernels for 10%

profile of v10, /device:TPU:0, one launch (start us, length us, event | category | flops | bytes accessed | tf_op | source)
XLA Modules:
  0.0 43.5 jit_solution(6691546026428294642)
XLA Ops:
  0.0 1.4 %pack.1 = (f32[264,128]{1,0:T(8,128)S(1)}, f32[128,1024]{1,0:T(8,128)S(1)}) custom-call(f32[192,128]{1,0:T(8,128)} %bitcast.17, f32[128,1024]{1,0:T(8,128)} %bitcast.16, s32[2,8]{1,0:T(2,128)} %bitcast.20, s32[2,8]{1,0:T(2,128)} %bitcast.21, f32[64,32]{1,0:T(8,128)} %bitcast.18, f32[48,128]{1,0:T(8,128)} %bitcast.19), custom_call_target="tpu_custom_call" | custom-call | flops 1 | bytes 1 | tf_op jit(solution)/shard_map/pack/pallas_call | solution.py:690
  1.4 4.0 %collective-permute-start.2 = (f32[264,128]{1,0:T(8,128)S(1)}, f32[264,128]{1,0:T(8,128)S(1)}, u32[]{:S(2)}, u32[]{:S(2)}) collective-permute-start(f32[264,128]{1,0:T(8,128)S(1)} %get-tuple-element.18.refs_0_), channel_id=1, source_target_pairs={{0,24},{4,28},{8,16},{12,20},{16,8},{20,12},{24,0},{28,4},{1,25},{... | collective-permute-start | bytes 405512 | tf_op jit(solution)/shard_map/ppermute | solution.py:686
  5.4 0.5 %collective-permute-start.1 = (f32[264,128]{1,0:T(8,128)S(1)}, f32[264,128]{1,0:T(8,128)S(1)}, u32[]{:S(2)}, u32[]{:S(2)}) collective-permute-start(f32[264,128]{1,0:T(8,128)S(1)} %get-tuple-element.18.refs_0_), channel_id=1, source_target_pairs={{0,16},{4,20},{8,24},{12,28},{16,0},{20,4},{24,8},{28,12},{1,17},{... | collective-permute-start | bytes 405512 | tf_op jit(solution)/shard_map/ppermute | solution.py:686
  6.0 3.3 %collective-permute-done.2.refs_3_.refs_0_ = f32[264,128]{1,0:T(8,128)S(1)} collective-permute-done((f32[264,128]{1,0:T(8,128)S(1)}, f32[264,128]{1,0:T(8,128)S(1)}, u32[]{:S(2)}, u32[]{:S(2)}) %collective-permute-start.2) | collective-permute-done | bytes 135200 | tf_op jit(solution)/shard_map/ppermute | solution.py:686
  9.4 2.5 %collective-permute-start.8 = (f32[128,1024]{1,0:T(8,128)S(1)}, f32[128,1024]{1,0:T(8,128)S(1)}, u32[]{:S(2)}, u32[]{:S(2)}) collective-permute-start(f32[128,1024]{1,0:T(8,128)S(1)} %gate.1.refs_4_.refs_6_), channel_id=1, source_target_pairs={{0,16},{4,20},{8,24},{12,28},{16,0},{20,4},{24,8},{28,12},{1,17},{... | collective-permute-start | bytes 1572872 | tf_op jit(solution)/shard_map/ppermute | solution.py:686
  11.8 1.5 %collective-permute-start.7 = (f32[128,1024]{1,0:T(8,128)S(1)}, f32[128,1024]{1,0:T(8,128)S(1)}, u32[]{:S(2)}, u32[]{:S(2)}) collective-permute-start(f32[128,1024]{1,0:T(8,128)S(1)} %gate.1.refs_4_.refs_6_), channel_id=1, source_target_pairs={{0,8},{4,12},{8,0},{12,4},{16,24},{20,28},{24,16},{28,20},{1,9},{5... | collective-permute-start | bytes 1572872 | tf_op jit(solution)/shard_map/ppermute | solution.py:686
  13.4 0.7 %dynamic-slice_bitcast_fusion = s32[24]{0:T(128)S(1)} fusion(s32[8,24]{1,0:T(8,128)} %constant.15.clone, s32[]{:T(128)S(6)} %select_n.3), kind=kLoop, calls=%fused_computation.1 | loop fusion | bytes 196 | tf_op jit(solution)/shard_map/squeeze | solution.py:672
  14.2 3.6 %collective-permute-start.6 = (f32[192,128]{1,0:T(8,128)S(1)}, f32[192,128]{1,0:T(8,128)S(1)}, u32[]{:S(2)}, u32[]{:S(2)}) collective-permute-start(f32[192,128]{1,0:T(8,128)S(1)} %get-tuple-element.23.refs_0_), channel_id=1, source_target_pairs={{0,3},{1,0},{2,1},{3,2},{4,7},{5,4},{6,5},{7,6},{8,11},{9,8},{10,9... | collective-permute-start | bytes 294920 | tf_op jit(solution)/shard_map/ppermute | solution.py:733
  17.8 1.0 %collective-permute-start.4 = (f32[192,128]{1,0:T(8,128)S(1)}, f32[192,128]{1,0:T(8,128)S(1)}, u32[]{:S(2)}, u32[]{:S(2)}) collective-permute-start(f32[192,128]{1,0:T(8,128)S(1)} %get-tuple-element.23.refs_0_), channel_id=1, source_target_pairs={{0,1},{1,2},{2,3},{3,0},{4,5},{5,6},{6,7},{7,4},{8,9},{9,10},{10,1... | collective-permute-start | bytes 294920 | tf_op jit(solution)/shard_map/ppermute | solution.py:733
  18.8 2.2 %begin.1 = (f32[768,128]{1,0:T(8,128)S(1)}, f32[768,128]{1,0:T(8,128)S(1)}, f32[512,128]{1,0:T(8,128)S(1)}, f32[8,128]{1,0:T(8,128)S(1)}, s32[8,128]{1,0:T(8,128)S(1)}) custom-call(s32[25]{0:T(128)S(1)} %pad_add_fusion.info_ref, f32[864,128]{1,0:T(8,128)S(1)} %get-tuple-element.19.own_ref, f32[864,128]{1,0:T(8,128)S(1)} %collective-permute-done.3.got_ref), custom_call_target="tpu_custom_call" | custom-call | flops 1 | bytes 1 | tf_op jit(solution)/shard_map/begin/pallas_call | solution.py:750
  21.0 2.0 %collective-permute-done.8.refs_6_.y_ref.refs_8_ = f32[128,1024]{1,0:T(8,128)S(1)} collective-permute-done((f32[128,1024]{1,0:T(8,128)S(1)}, f32[128,1024]{1,0:T(8,128)S(1)}, u32[]{:S(2)}, u32[]{:S(2)}) %collective-permute-start.8) | collective-permute-done | bytes 524320 | tf_op jit(solution)/shard_map/ppermute | solution.py:686
  23.4 1.5 %collective-permute-start.9 = (f32[64,1024]{1,0:T(8,128)S(1)}, f32[64,1024]{1,0:T(8,128)S(1)}, u32[]{:S(2)}, u32[]{:S(2)}) collective-permute-start(f32[64,1024]{1,0:T(8,128)S(1)} %get-tuple-element.28), channel_id=1, source_target_pairs={{0,16},{4,20},{8,24},{12,28},{16,0},{20,4},{24,8},{28,12},{1,17},{... | collective-permute-start | bytes 786440 | tf_op jit(solution)/shard_map/ppermute | solution.py:686
  24.9 0.7 %collective-permute-start.10 = (f32[64,1024]{1,0:T(8,128)S(1)}, f32[64,1024]{1,0:T(8,128)S(1)}, u32[]{:S(2)}, u32[]{:S(2)}) collective-permute-start(f32[64,1024]{1,0:T(8,128)S(1)} %get-tuple-element.29), channel_id=1, source_target_pairs={{0,8},{4,12},{8,0},{12,4},{16,24},{20,28},{24,16},{28,20},{1,9},{5... | collective-permute-start | bytes 786440 | tf_op jit(solution)/shard_map/ppermute | solution.py:686
  25.6 2.0 %collective-permute-done.5.refs_2_ = f32[192,128]{1,0:T(8,128)S(1)} collective-permute-done((f32[192,128]{1,0:T(8,128)S(1)}, f32[192,128]{1,0:T(8,128)S(1)}, u32[]{:S(2)}, u32[]{:S(2)}) %collective-permute-start.5) | collective-permute-done | bytes 98336 | tf_op jit(solution)/shard_map/ppermute | solution.py:733
  27.6 0.7 %potential.1 = (f32[768,128]{1,0:T(8,128)S(1)}, f32[768,128]{1,0:T(8,128)S(1)}) custom-call(s32[8,128]{1,0:T(8,128)S(1)} %get-tuple-element.20.table_ref.refs_0_, f32[768,128]{1,0:T(8,128)S(1)} %get-tuple-element.21.part_ref, f32[768,128]{1,0:T(8,128)S(1)} %get-tuple-element.22.y_ref.refs_3_, f32[192,128]{1,0:T(8,128)S(1)} %get-tuple-element.23.refs_0_, ...), custom_call_target="tpu_custom_call" | custom-call | flops 10000000000 | bytes 1 | tf_op jit(solution)/shard_map/potential/pallas_call | solution.py:767
  28.3 1.4 %first.1.refs_1_ = f32[776,128]{1,0:T(8,128)S(1)} custom-call(s32[8,128]{1,0:T(8,128)S(1)} %get-tuple-element.20.table_ref.refs_0_, f32[768,128]{1,0:T(8,128)S(1)} %get-tuple-element.24.refs_1_, f32[512,128]{1,0:T(8,128)S(1)} %get-tuple-element.25.refs_2_.refs_5_, f32[8,128]{1,0:T(8,128)S(1)} %get-tuple-element.26.refs_3_, ...), custom_call_target="tpu_custom_call" | custom-call | flops 1 | bytes 1 | tf_op jit(solution)/shard_map/first/pallas_call | solution.py:781
  29.9 1.3 %collective-permute-done.10.refs_5_.refs_10_ = f32[64,1024]{1,0:T(8,128)S(1)} collective-permute-done((f32[64,1024]{1,0:T(8,128)S(1)}, f32[64,1024]{1,0:T(8,128)S(1)}, u32[]{:S(2)}, u32[]{:S(2)}) %collective-permute-start.10) | collective-permute-done | bytes 262176 | tf_op jit(solution)/shard_map/ppermute | solution.py:686
  31.3 1.0 %first_late.1.refs_1_.refs_3_ = f32[776,128]{1,0:T(8,128)S(1)} custom-call(s32[8,128]{1,0:T(8,128)S(1)} %get-tuple-element.20.table_ref.refs_0_, f32[776,128]{1,0:T(8,128)S(1)} %first.1.refs_1_, f32[512,128]{1,0:T(8,128)S(1)} %get-tuple-element.25.refs_2_.refs_5_, f32[8,128]{1,0:T(8,128)S(1)} %get-tuple-element.26.refs_3_, ...), custom_call_target="tpu_custom_call", output_to_operand_aliasing={{}: (1, {})} | custom-call | flops 1 | bytes 1 | tf_op jit(solution)/shard_map/first_late/pallas_call | solution.py:781
  32.4 1.7 %collective-permute-done.11.refs_2_ = f32[776,128]{1,0:T(8,128)S(1)} collective-permute-done((f32[776,128]{1,0:T(8,128)S(1)}, f32[776,128]{1,0:T(8,128)S(1)}, u32[]{:S(2)}, u32[]{:S(2)}) %collective-permute-start.11) | collective-permute-done | bytes 397344 | tf_op jit(solution)/shard_map/ppermute | solution.py:686
  34.1 2.1 %next.2.refs_1_.refs_3_ = f32[776,128]{1,0:T(8,128)S(1)} custom-call(s32[8,128]{1,0:T(8,128)S(1)} %get-tuple-element.20.table_ref.refs_0_, f32[776,128]{1,0:T(8,128)S(1)} %first_late.1.refs_1_.refs_3_, f32[776,128]{1,0:T(8,128)S(1)} %collective-permute-done.11.refs_2_, f32[768,128]{1,0:T(8,128)S(1)} %get-tuple-element.22.y_ref.refs_3_, ...), custom_call_target="tpu_custom_call" | custom-call | tf_op jit(solution)/shard_map/next/pallas_call | solution.py:794
  36.4 1.6 %collective-permute-done.12.refs_2_ = f32[776,128]{1,0:T(8,128)S(1)} collective-permute-done((f32[776,128]{1,0:T(8,128)S(1)}, f32[776,128]{1,0:T(8,128)S(1)}, u32[]{:S(2)}, u32[]{:S(2)}) %collective-permute-start.12) | collective-permute-done | bytes 397344 | tf_op jit(solution)/shard_map/ppermute | solution.py:686
  38.0 2.1 %next.3.refs_1_ = f32[776,128]{1,0:T(8,128)S(1)} custom-call(s32[8,128]{1,0:T(8,128)S(1)} %get-tuple-element.20.table_ref.refs_0_, f32[776,128]{1,0:T(8,128)S(1)} %next.2.refs_1_.refs_3_, f32[776,128]{1,0:T(8,128)S(1)} %collective-permute-done.12.refs_2_, f32[776,128]{1,0:T(8,128)S(1)} %first_late.1.refs_1_.refs_3_, ...), custom_call_target="tpu_custom_call" | custom-call | tf_op jit(solution)/shard_map/next/pallas_call | solution.py:794
  40.3 1.6 %collective-permute-done.13.refs_2_ = f32[776,128]{1,0:T(8,128)S(1)} collective-permute-done((f32[776,128]{1,0:T(8,128)S(1)}, f32[776,128]{1,0:T(8,128)S(1)}, u32[]{:S(2)}, u32[]{:S(2)}) %collective-permute-start.13) | collective-permute-done | bytes 397344 | tf_op jit(solution)/shard_map/ppermute | solution.py:686
  41.9 1.6 %last.1 = f32[192,128]{1,0:T(8,128)} custom-call(s32[8,128]{1,0:T(8,128)S(1)} %get-tuple-element.20.table_ref.refs_0_, f32[776,128]{1,0:T(8,128)S(1)} %next.3.refs_1_, f32[776,128]{1,0:T(8,128)S(1)} %collective-permute-done.13.refs_2_, f32[776,128]{1,0:T(8,128)S(1)} %next.2.refs_1_.refs_3_, f32[768,128]{1,0:T(8,128)S(1)} %get-tuple-element.30.refs_4_, ...), custom_call_target="tpu_custom_call" | custom-call | tf_op jit(solution)/shard_map/last/pallas_call | solution.py:794
  (17 shorter events, 1.4 us)
Async XLA Ops:
  1.4 8.0 %collective-permute-start.2 = (f32[264,128]{1,0:T(8,128)S(1)}, f32[264,128]{1,0:T(8,128)S(1)}, u32[]{:S(2)}, u32[]{:S(2)}) collective-permute-start(f32[264,128]{1,0:T(8,128)S(1)} %get-tuple-element.18.refs_0_), channel_id=1, source_target_pairs={{0,24},{4,28},{8,16},{12,20},{16,8},{20,12},{24,0},{28,4},{1,25},{... | collective-permute-start | bytes 405512 | tf_op jit(solution)/shard_map/ppermute | solution.py:686
  5.4 7.9 %collective-permute-start.1 = (f32[264,128]{1,0:T(8,128)S(1)}, f32[264,128]{1,0:T(8,128)S(1)}, u32[]{:S(2)}, u32[]{:S(2)}) collective-permute-start(f32[264,128]{1,0:T(8,128)S(1)} %get-tuple-element.18.refs_0_), channel_id=1, source_target_pairs={{0,16},{4,20},{8,24},{12,28},{16,0},{20,4},{24,8},{28,12},{1,17},{... | collective-permute-start | bytes 405512 | tf_op jit(solution)/shard_map/ppermute | solution.py:686
  5.9 7.4 %collective-permute-start = (f32[264,128]{1,0:T(8,128)S(1)}, f32[264,128]{1,0:T(8,128)S(1)}, u32[]{:S(2)}, u32[]{:S(2)}) collective-permute-start(f32[264,128]{1,0:T(8,128)S(1)} %get-tuple-element.18.refs_0_), channel_id=1, source_target_pairs={{0,8},{4,12},{8,0},{12,4},{16,24},{20,28},{24,16},{28,20},{1,9},{5... | collective-permute-start | bytes 405512 | tf_op jit(solution)/shard_map/ppermute | solution.py:686
  9.4 13.7 %collective-permute-start.8 = (f32[128,1024]{1,0:T(8,128)S(1)}, f32[128,1024]{1,0:T(8,128)S(1)}, u32[]{:S(2)}, u32[]{:S(2)}) collective-permute-start(f32[128,1024]{1,0:T(8,128)S(1)} %gate.1.refs_4_.refs_6_), channel_id=1, source_target_pairs={{0,16},{4,20},{8,24},{12,28},{16,0},{20,4},{24,8},{28,12},{1,17},{... | collective-permute-start | bytes 1572872 | tf_op jit(solution)/shard_map/ppermute | solution.py:686
  11.8 11.5 %collective-permute-start.7 = (f32[128,1024]{1,0:T(8,128)S(1)}, f32[128,1024]{1,0:T(8,128)S(1)}, u32[]{:S(2)}, u32[]{:S(2)}) collective-permute-start(f32[128,1024]{1,0:T(8,128)S(1)} %gate.1.refs_4_.refs_6_), channel_id=1, source_target_pairs={{0,8},{4,12},{8,0},{12,4},{16,24},{20,28},{24,16},{28,20},{1,9},{5... | collective-permute-start | bytes 1572872 | tf_op jit(solution)/shard_map/ppermute | solution.py:686
  13.4 4.5 %collective-permute-start.3 = (f32[864,128]{1,0:T(8,128)S(1)}, f32[864,128]{1,0:T(8,128)S(1)}, u32[]{:S(2)}, u32[]{:S(2)}) collective-permute-start(f32[864,128]{1,0:T(8,128)S(1)} %get-tuple-element.19.own_ref), channel_id=1, source_target_pairs={{0,4},{4,0},{8,12},{12,8},{16,20},{20,16},{24,28},{28,24},{1,5},{5... | collective-permute-start | bytes 1327112 | tf_op jit(solution)/shard_map/ppermute | solution.py:686
  14.2 11.4 %collective-permute-start.6 = (f32[192,128]{1,0:T(8,128)S(1)}, f32[192,128]{1,0:T(8,128)S(1)}, u32[]{:S(2)}, u32[]{:S(2)}) collective-permute-start(f32[192,128]{1,0:T(8,128)S(1)} %get-tuple-element.23.refs_0_), channel_id=1, source_target_pairs={{0,3},{1,0},{2,1},{3,2},{4,7},{5,4},{6,5},{7,6},{8,11},{9,8},{10,9... | collective-permute-start | bytes 294920 | tf_op jit(solution)/shard_map/ppermute | solution.py:733
  17.8 9.8 %collective-permute-start.5 = (f32[192,128]{1,0:T(8,128)S(1)}, f32[192,128]{1,0:T(8,128)S(1)}, u32[]{:S(2)}, u32[]{:S(2)}) collective-permute-start(f32[192,128]{1,0:T(8,128)S(1)} %get-tuple-element.23.refs_0_), channel_id=1, source_target_pairs={{0,2},{1,3},{2,0},{3,1},{4,6},{5,7},{6,4},{7,5},{8,10},{9,11},{10,... | collective-permute-start | bytes 294920 | tf_op jit(solution)/shard_map/ppermute | solution.py:733
  17.8 9.8 %collective-permute-start.4 = (f32[192,128]{1,0:T(8,128)S(1)}, f32[192,128]{1,0:T(8,128)S(1)}, u32[]{:S(2)}, u32[]{:S(2)}) collective-permute-start(f32[192,128]{1,0:T(8,128)S(1)} %get-tuple-element.23.refs_0_), channel_id=1, source_target_pairs={{0,1},{1,2},{2,3},{3,0},{4,5},{5,6},{6,7},{7,4},{8,9},{9,10},{10,1... | collective-permute-start | bytes 294920 | tf_op jit(solution)/shard_map/ppermute | solution.py:733
  23.4 6.6 %collective-permute-start.9 = (f32[64,1024]{1,0:T(8,128)S(1)}, f32[64,1024]{1,0:T(8,128)S(1)}, u32[]{:S(2)}, u32[]{:S(2)}) collective-permute-start(f32[64,1024]{1,0:T(8,128)S(1)} %get-tuple-element.28), channel_id=1, source_target_pairs={{0,16},{4,20},{8,24},{12,28},{16,0},{20,4},{24,8},{28,12},{1,17},{... | collective-permute-start | bytes 786440 | tf_op jit(solution)/shard_map/ppermute | solution.py:686
  24.9 6.4 %collective-permute-start.10 = (f32[64,1024]{1,0:T(8,128)S(1)}, f32[64,1024]{1,0:T(8,128)S(1)}, u32[]{:S(2)}, u32[]{:S(2)}) collective-permute-start(f32[64,1024]{1,0:T(8,128)S(1)} %get-tuple-element.29), channel_id=1, source_target_pairs={{0,8},{4,12},{8,0},{12,4},{16,24},{20,28},{24,16},{28,20},{1,9},{5... | collective-permute-start | bytes 786440 | tf_op jit(solution)/shard_map/ppermute | solution.py:686
  32.3 1.8 %collective-permute-start.11 = (f32[776,128]{1,0:T(8,128)S(1)}, f32[776,128]{1,0:T(8,128)S(1)}, u32[]{:S(2)}, u32[]{:S(2)}) collective-permute-start(f32[776,128]{1,0:T(8,128)S(1)} %first_late.1.refs_1_.refs_3_), channel_id=1, source_target_pairs={{0,4},{4,0},{8,12},{12,8},{16,20},{20,16},{24,28},{28,24},{1,5},{5... | collective-permute-start | bytes 1191944 | tf_op jit(solution)/shard_map/ppermute | solution.py:686
  36.2 1.8 %collective-permute-start.12 = (f32[776,128]{1,0:T(8,128)S(1)}, f32[776,128]{1,0:T(8,128)S(1)}, u32[]{:S(2)}, u32[]{:S(2)}) collective-permute-start(f32[776,128]{1,0:T(8,128)S(1)} %next.2.refs_1_.refs_3_), channel_id=1, source_target_pairs={{0,4},{4,0},{8,12},{12,8},{16,20},{20,16},{24,28},{28,24},{1,5},{5... | collective-permute-start | bytes 1191944 | tf_op jit(solution)/shard_map/ppermute | solution.py:686
  40.1 1.8 %collective-permute-start.13 = (f32[776,128]{1,0:T(8,128)S(1)}, f32[776,128]{1,0:T(8,128)S(1)}, u32[]{:S(2)}, u32[]{:S(2)}) collective-permute-start(f32[776,128]{1,0:T(8,128)S(1)} %next.3.refs_1_), channel_id=1, source_target_pairs={{0,4},{4,0},{8,12},{12,8},{16,20},{20,16},{24,28},{28,24},{1,5},{5... | collective-permute-start | bytes 1191944 | tf_op jit(solution)/shard_map/ppermute | solution.py:686
